TPU v7x, 256 devices: a whole 4x4x8 slice. The times are simulated.
256 devices in a mesh: segment: 2 (over z_lo), tm: 16 (over x, z_hi), space: 8 (over y, core).
Axes of the slice: x: 4, y: 4, z: 8 (z_hi: 4, z_lo: 2; z = z_hi * 2 + z_lo), core: 2. Of those that a mesh axis runs over, the one named last changes fastest.
Arguments:
- clip_frames: bfloat16 [64, 64, 128, 128], P('tm', 'space'), may hold values from -6 to 6
- enc_weight: bfloat16 [3, 3, 3, 128, 256], replicated, may hold values from -0.109375 to 0.109375
- dec_weight: bfloat16 [3, 3, 3, 256, 128], replicated, may hold values from -0.078125 to 0.078125
- out_grad: bfloat16 [32, 32, 64, 128], P('tm', 'space'), may hold values from -6 to 6
Outputs:
- latent_pair: bfloat16 [2, 32, 32, 64, 256], P('segment', 'tm', 'space')
- weight_grads: float32 [2, 27, 32768], P('segment')
All inputs are finite; a program needn't handle non-finite values.
Results may differ from a plain program's by a relative error of at most 0.0056.
Values may be sent and summed in bfloat16 or wider, within the bound.
No kernel may reach another device: no remote copies, remote signals or barrier semaphores. Data moves between devices by JAX's collectives and lax.ppermute only.
A program may use at most 128 MiB of HBM per device.

v0:
```python
import math

import jax
import jax.numpy as jnp
from jax import lax
from jax.sharding import PartitionSpec as P


def from_behind(array, axis, by):
    size = lax.axis_size(axis)
    pairs = [(i, i + by) for i in range(size) if 0 <= i + by < size]
    return lax.ppermute(array, axis, pairs)


def with_halo(cells, sides, width):
    for axis, dim in sides:
        count = lax.axis_size(axis)
        ends = count - 1
        head = lax.slice_in_dim(cells, 0, width, axis=dim)
        tail = lax.slice_in_dim(cells, cells.shape[dim] - width, cells.shape[dim], axis=dim)
        cells = jnp.concatenate(
            [
                lax.ppermute(tail, axis, [(i, (i + 1) % count) for i in range(ends)]),
                cells,
                lax.ppermute(head, axis, [((i + 1) % count, i) for i in range(ends)]),
            ],
            axis=dim,
        )
    return cells


def widen(field):
    return jnp.pad(field, ((0, 0), (0, 0), (1, 1), (0, 0)))


def encode_taps(padded, enc_weight, frame_count, row_count, col_count):
    chans = padded.shape[-1]
    summed = jnp.zeros((frame_count * row_count * col_count, enc_weight.shape[-1]), jnp.float32)
    for tap_t in range(3):
        for tap_h in range(3):
            for tap_w in range(3):
                window = padded[
                    tap_t : tap_t + 2 * frame_count : 2,
                    tap_h : tap_h + 2 * row_count : 2,
                    tap_w : tap_w + 2 * col_count : 2,
                ]
                summed = summed + jnp.dot(
                    window.reshape(-1, chans),
                    enc_weight[tap_t, tap_h, tap_w],
                    preferred_element_type=jnp.float32,
                )
    return summed.reshape(frame_count, row_count, col_count, -1).astype(jnp.bfloat16)


def decode_taps(extended, dec_weight, out_grad):
    frame_count, row_count, col_count, out_chans = out_grad.shape
    chans = extended.shape[-1]
    pre_act = jnp.zeros((frame_count * row_count * col_count, out_chans), jnp.float32)
    for tap_t in range(3):
        for tap_h in range(3):
            for tap_w in range(3):
                window = extended[
                    tap_t : tap_t + frame_count,
                    tap_h : tap_h + row_count,
                    tap_w : tap_w + col_count,
                ]
                pre_act = pre_act + jnp.dot(
                    window.reshape(-1, chans),
                    dec_weight[tap_t, tap_h, tap_w],
                    preferred_element_type=jnp.float32,
                )
    sigm = jax.nn.sigmoid(pre_act)
    slope = (
        out_grad.reshape(-1, out_chans).astype(jnp.float32) * sigm * (1.0 + pre_act * (1.0 - sigm))
    )
    return slope.astype(jnp.bfloat16).reshape(out_grad.shape)


def transpose_taps(rimmed, dec_weight, frame_count, row_count, col_count):
    chans = rimmed.shape[-1]
    summed = jnp.zeros((frame_count * row_count * col_count, dec_weight.shape[3]), jnp.float32)
    for tap_t in range(3):
        for tap_h in range(3):
            for tap_w in range(3):
                window = rimmed[
                    2 - tap_t : 2 - tap_t + frame_count,
                    2 - tap_h : 2 - tap_h + row_count,
                    2 - tap_w : 2 - tap_w + col_count,
                ]
                summed = summed + lax.dot_general(
                    window.reshape(-1, chans),
                    dec_weight[tap_t, tap_h, tap_w],
                    (((1,), (1,)), ((), ())),
                    preferred_element_type=jnp.float32,
                )
    return summed.reshape(frame_count, row_count, col_count, -1).astype(jnp.bfloat16)


def enc_taps_grad(padded, lat_grad):
    frame_count, row_count, col_count, lat_chans = lat_grad.shape
    chans = padded.shape[-1]
    flat_grad = lat_grad.reshape(-1, lat_chans)
    pieces = []
    for tap_t in range(3):
        for tap_h in range(3):
            for tap_w in range(3):
                window = padded[
                    tap_t : tap_t + 2 * frame_count : 2,
                    tap_h : tap_h + 2 * row_count : 2,
                    tap_w : tap_w + 2 * col_count : 2,
                ]
                pieces.append(
                    lax.dot_general(
                        window.reshape(-1, chans),
                        flat_grad,
                        (((0,), (0,)), ((), ())),
                        preferred_element_type=jnp.float32,
                    ).reshape(-1)
                )
    return jnp.stack(pieces)


def dec_taps_grad(extended, slope):
    frame_count, row_count, col_count, out_chans = slope.shape
    chans = extended.shape[-1]
    flat_slope = slope.reshape(-1, out_chans)
    pieces = []
    for tap_t in range(3):
        for tap_h in range(3):
            for tap_w in range(3):
                window = extended[
                    tap_t : tap_t + frame_count,
                    tap_h : tap_h + row_count,
                    tap_w : tap_w + col_count,
                ]
                pieces.append(
                    lax.dot_general(
                        window.reshape(-1, chans),
                        flat_slope,
                        (((0,), (0,)), ((), ())),
                        preferred_element_type=jnp.float32,
                    ).reshape(-1)
                )
    return jnp.stack(pieces)


def latent_rim(received):
    before = from_behind(received, "tm", 1)
    joined = jnp.concatenate([before, received], 0)
    return widen(with_halo(joined, (("space", 1),), 1))


def slope_rim(slope):
    later = from_behind(slope, "tm", -1)
    joined = jnp.concatenate([slope, later], 0)
    return widen(with_halo(joined, (("space", 1),), 1))


def on_device(clip_frames, enc_weight, dec_weight, out_grad):
    is_encoder = lax.axis_index("segment") == 0
    is_decoder = jnp.logical_not(is_encoder)
    frame_count, row_count, whole_cols, out_chans = out_grad.shape
    lat_chans = enc_weight.shape[-1]
    wide_clip = widen(clip_frames)
    lat_shape = (frame_count, row_count, whole_cols, lat_chans)
    earlier = from_behind(wide_clip[-2:], "tm", 1)
    joined = jnp.concatenate([earlier, wide_clip], 0)
    above = from_behind(joined[:, -1:], "space", 1)
    padded = jnp.concatenate([above, joined], 1)
    latent = lax.cond(
        is_encoder,
        lambda: encode_taps(padded, enc_weight, frame_count, row_count, whole_cols),
        lambda: jnp.zeros(lat_shape, jnp.bfloat16),
    )
    received = from_behind(latent, "segment", 1)
    extended = latent_rim(received)
    slope = lax.cond(
        is_decoder,
        lambda: decode_taps(extended, dec_weight, out_grad),
        lambda: jnp.zeros(out_grad.shape, jnp.bfloat16),
    )
    rimmed = slope_rim(slope)
    lat_local = lax.cond(
        is_decoder,
        lambda: transpose_taps(rimmed, dec_weight, frame_count, row_count, whole_cols),
        lambda: jnp.zeros(lat_shape, jnp.bfloat16),
    )
    lat_grad = from_behind(lat_local, "segment", -1)
    own_grad = lax.cond(
        is_encoder, lambda: enc_taps_grad(padded, lat_grad), lambda: dec_taps_grad(extended, slope)
    )
    latent_pair = jnp.where(is_encoder, lat_grad, received)[None]
    summed_grads = lax.psum(own_grad, ("tm", "space"))
    whole_count = (
        frame_count * row_count * whole_cols * lax.axis_size("tm") * lax.axis_size("space")
    )
    grad_scale = 1.0 / math.sqrt(whole_count)
    weight_grads = (summed_grads * grad_scale)[None]
    return (latent_pair, weight_grads)


def solution(mesh):
    placed = (P("tm", "space", None, None), P(), P(), P("tm", "space", None, None))
    return jax.shard_map(
        on_device,
        mesh=mesh,
        in_specs=placed,
        out_specs=(P("segment", "tm", "space", None, None), P("segment", None, None)),
        check_vma=False,
    )
```

profile of v0, /device:TPU:1, one launch (start us, length us, event | category | flops | bytes accessed | tf_op | source)
XLA Modules:
  0.0 1732.6 jit_solution(4482286904958584437)
XLA Ops:
  9.2 5.7 collective-permute-start
  15.0 14.1 collective-permute-done
  30.5 5.1 collective-permute-start.1
  35.8 4.9 collective-permute-done.1
  40.7 3.9 maximum_maximum_fusion
  44.6 118.7 %conditional.4 = (bf16[2,4,64,256]{3,2,1,0:T(8,128)(2,1)}) conditional(s32[]{:T(128)} %convert_element_type.36, () %tuple.34, (bf16[6,9,130,128]{3,1,2,0:T(8,128)(2,1)}, bf16[3,3,3,128,256]{4,3,2,1,0:T(8,128)(2,1)}, bf16[6,8,130,128]{3,1,2,0:T(8,128)(2,1)S(1)}, bf16[4,8,130,128]{3,1,2,0:T(8,128)(2,1)S(1)}) %tuple.35), branch_computations={%region_0.1_spmd, %region_1.2_spmd} | conditional | flops 909508608 | bytes 66394708 | solution.py:170
  56.5 4.7 slice.497
  61.2 4.7 slice.495
  71.0 4.6 slice.485
  75.6 4.6 slice.483
  80.1 4.8 slice.481
  85.0 4.7 slice.479
  89.6 4.7 slice.477
  94.3 4.7 slice.469
  99.0 4.6 slice.467
  103.6 4.6 slice.465
  108.2 4.8 slice.463
  113.0 4.7 slice.461
  117.7 4.7 slice.459
  122.3 4.7 slice.487
  168.3 13.5 collective-permute-start.3
  181.8 5.2 collective-permute-done.3
  187.1 5.9 collective-permute-start.4
  194.9 4.3 collective-permute-done.5
  201.2 12.6 collective-permute-done.6
  225.1 21.6 %collective-permute-done.9 = bf16[2,4,64,256]{3,2,1,0:T(8,128)(2,1)S(1)} collective-permute-done((bf16[2,4,64,256]{3,2,1,0:T(8,128)(2,1)}, bf16[2,4,64,256]{3,2,1,0:T(8,128)(2,1)S(1)}, u32[]{:S(2)}, u32[]{:S(2)}) %collective-permute-start.9) | collective-permute-done | bytes 262176 | tf_op jit(solution)/shard_map/ppermute | solution.py:12
  246.7 114.8 %conditional.7 = (f32[27,32768]{1,0:T(8,128)}) conditional(s32[]{:T(128)} %convert_element_type.36, (bf16[4,6,66,256]{3,2,1,0:T(8,128)(2,1)S(1)}, bf16[2,4,64,128]{3,2,1,0:T(8,128)(2,1)S(1)}) %tuple.38, (bf16[6,9,130,128]{3,1,2,0:T(8,128)(2,1)}, bf16[2,4,64,256]{3,2,1,0:T(8,128)(2,1)S(1)}, bf16[6,8,130,128]{3,1,2,0:T(8,128)(2,1)}, ...), branch_computations={%region_6.7_spmd, %region_7.8_spmd} | conditional | flops 905969664 | bytes 44308488 | solution.py:189
  329.8 4.7 slice.643
  336.4 4.7 slice.642
  341.1 4.8 slice.662
  349.7 11.7 stack.5
  363.1 1356.4 %all-reduce.5.cloned.1.call-done = f32[27,32768]{1,0:T(8,128)} async-done(((f32[27,32768]{1,0:T(8,128)}), f32[27,32768]{1,0:T(8,128)}) %all-reduce.5.cloned.1.call-update) | async-done | bytes 3538960 | tf_op jit(solution)/shard_map/psum | solution.py:193
  (204 shorter events, 173.7 us)
Async XLA Ops:
  7.2 1712.3 %all-reduce.5.cloned.1.call-start = ((), (), s32[]{:S(2)}) async-start(), calls=%async_computation | async-start | bytes 8388608 | tf_op jit(solution)/shard_map/psum | solution.py:193
  9.2 20.0 %collective-permute-start = (bf16[2,8,130,128]{3,1,2,0:T(8,128)(2,1)S(1)}, bf16[2,8,130,128]{3,1,2,0:T(8,128)(2,1)S(1)}, u32[]{:S(2)}, u32[]{:S(2)}) collective-permute-start(bf16[2,8,130,128]{3,1,2,0:T(8,128)(2,1)S(1)} %pad_slice_fusion.20), channel_id=1, source_target_pairs={{0,8},{8,16},{16,24},{24,32},{32,40},{40,48},{48,56},{56,64},{64,7... | collective-permute-start | bytes 1597448 | tf_op jit(solution)/shard_map/ppermute | solution.py:12
  30.5 10.2 collective-permute-start.1
  35.7 8.8 copy-start
  152.0 2.4 copy-start.3
  152.0 3.6 copy-start.25
  153.3 2.6 copy-start.24
  154.5 1.6 copy-start.23
  156.1 0.9 copy-start.17
  156.6 0.9 copy-start.22
  156.8 0.9 copy-start.20
  157.1 0.9 copy-start.18
  157.5 0.9 copy-start.16
  157.7 0.9 copy-start.15
  158.0 0.9 copy-start.11
  158.4 0.9 copy-start.9
  158.7 0.9 copy-start.8
  158.9 0.9 copy-start.12
  159.4 0.9 copy-start.13
  159.6 0.9 copy-start.10
  160.6 0.9 copy-start.6
  163.3 36.4 %copy-start.26 = (bf16[2,4,64,128]{3,2,1,0:T(8,128)(2,1)S(1)}, bf16[2,4,64,128]{3,2,1,0:T(8,128)(2,1)}, u32[]{:S(2)}) copy-start(bf16[2,4,64,128]{3,2,1,0:T(8,128)(2,1)} %param.15) | copy-start | bytes 393220
  163.3 5.0 collective-permute-start.2
  168.3 18.8 %copy-start.4 = (bf16[2,4,64,256]{3,2,1,0:T(8,128)(2,1)}, bf16[2,4,64,256]{3,2,1,0:T(8,128)(2,1)S(1)}, u32[]{:S(2)}) copy-start(bf16[2,4,64,256]{3,2,1,0:T(8,128)(2,1)S(1)} %collective-permute-done.2) | copy-start | bytes 786436
  168.3 18.7 %collective-permute-start.3 = (bf16[2,4,64,256]{3,2,1,0:T(8,128)(2,1)S(1)}, bf16[2,4,64,256]{3,2,1,0:T(8,128)(2,1)S(1)}, u32[]{:S(2)}, u32[]{:S(2)}) collective-permute-start(bf16[2,4,64,256]{3,2,1,0:T(8,128)(2,1)S(1)} %collective-permute-done.2), channel_id=1, source_target_pairs={{0,8},{8,16},{16,24},{24,32},{32,40},{40,48},{48,56},{56,64},{64,7... | collective-permute-start | bytes 786440 | tf_op jit(solution)/shard_map/ppermute | solution.py:12
  187.1 7.8 collective-permute-start.4
  193.0 6.3 collective-permute-start.5
  199.9 13.9 collective-permute-start.6
  213.9 5.5 collective-permute-start.7
  217.4 5.6 collective-permute-start.8
  223.8 22.9 %collective-permute-start.9 = (bf16[2,4,64,256]{3,2,1,0:T(8,128)(2,1)}, bf16[2,4,64,256]{3,2,1,0:T(8,128)(2,1)S(1)}, u32[]{:S(2)}, u32[]{:S(2)}) collective-permute-start(bf16[2,4,64,256]{3,2,1,0:T(8,128)(2,1)} %get-tuple-element.133), channel_id=1, source_target_pairs={{128,0},{129,1},{130,2},{131,3},{132,4},{133,5},{134,6},{135,7},{1... | collective-permute-start | bytes 786440 | tf_op jit(solution)/shard_map/ppermute | solution.py:12
  361.4 0.9 copy-start.5
  (4 other events, 3.7 us)
Sparse Core Ops, SparseCore 0:
  361.6 1357.8 all-reduce.4
where the time goes:
time: 1750 us; the launch traced here: 1730 us
  waiting for transfers between devices  1430 us (82%)
  local copies, waits for them, and re-layouts  222 us (13%)
  starting transfers between devices  41.5 us (2%)
  matrix products  18 us (1%)
    psum x1, waiting for transfers between devices, on_device(): summed_grads = lax.psum(own_grad, ('tm', 'space'))  1360 us
    slice x27, local copies, waits for them, and re-layouts, encode_taps(): padded[tap_t:tap_t + 2 * frame_count:2, tap_h:tap_h + 2 * row_count:2, ta...  102 us
    slice x27, local copies, waits for them, and re-layouts, enc_taps_grad(): padded[tap_t:tap_t + 2 * frame_count:2, tap_h:tap_h + 2 * row_count:2, ta...  81.5 us
    ppermute x6, waiting for transfers between devices, from_behind(): return lax.ppermute(array, axis, pairs)  62.1 us
  transfers between devices with their start and end apart: 11, of which 9 were waited for; matrix products, arithmetic and copies ran while one was open for 0% of the time, Pallas kernels for 0%

commit v1 on v0

v1 whole, which is shorter than its diff:
```python
import math

import jax
import jax.numpy as jnp
from jax import lax
from jax.experimental import pallas as pl
from jax.experimental.pallas import tpu as pltpu
from jax.sharding import PartitionSpec as P

F32 = jnp.float32
BF16 = jnp.bfloat16
PART = BF16
VMEM_LIMIT = 56 * 1024 * 1024


def shape(dims, dtype):
    return jax.ShapeDtypeStruct(dims, dtype)


def on_chip(body, outs, name, smem=0, scratch=()):
    def call(*args):
        specs = [pl.BlockSpec(memory_space=pltpu.SMEM)] * smem
        specs += [pl.BlockSpec(memory_space=pltpu.VMEM)] * (len(args) - smem)
        return pl.pallas_call(
            body,
            out_shape=outs,
            in_specs=specs,
            out_specs=[pl.BlockSpec(memory_space=pltpu.VMEM)] * len(outs),
            scratch_shapes=list(scratch),
            name=name,
            compiler_params=pltpu.CompilerParams(vmem_limit_bytes=VMEM_LIMIT),
        )(*args)

    return call


def dot(left, right):
    return jnp.dot(left, right, preferred_element_type=F32)


def dot_tn(left, right):
    return lax.dot_general(left, right, (((0,), (0,)), ((), ())), preferred_element_type=F32)


def dot_nt(left, right):
    return lax.dot_general(left, right, (((1,), (1,)), ((), ())), preferred_element_type=F32)


def clip_windows(row, stage):
    stage[8:136, :] = row.astype(F32)
    before = stage[pl.ds(7, 64, stride=2), :]
    here = stage[pl.ds(8, 64, stride=2), :]
    after = stage[pl.ds(9, 64, stride=2), :]
    return jnp.concatenate([before, here, after], axis=1).astype(BF16)


def neighbour_cols(row):
    wide = row.astype(F32)
    place = lax.broadcasted_iota(jnp.int32, wide.shape, 0)
    last = wide.shape[0] - 1
    before = jnp.where(place == 0, 0.0, pltpu.roll(wide, 1, 0)).astype(BF16)
    after = jnp.where(place == last, 0.0, pltpu.roll(wide, last, 0)).astype(BF16)
    return before, row, after


def fill_clip(stage, src, top, dst, frames):
    stage[0:8, :] = jnp.zeros((8, stage.shape[1]), F32)
    for f in range(frames):
        dst[f, 0] = clip_windows(top[f, 0], stage)

        def one(r, carry, f=f):
            dst[f, r + 1] = clip_windows(src[f, r], stage)
            return carry

        lax.fori_loop(0, 8, one, 0)


def clip_im2col(taps, f, b):
    return jnp.concatenate([taps[f, 2 * h + b] for h in range(4)], axis=0)


def encode_body(clip, top, weight, lat1, part, own0, taps, stage):
    fill_clip(stage, clip, top, taps, 4)

    def conv(f, a):
        total = None
        for b in range(3):
            term = dot(clip_im2col(taps, f, b), weight[a, b].reshape(384, 256))
            total = term if total is None else total + term
        return total

    lat1[...] = (conv(0, 0) + conv(1, 1) + conv(2, 2)).astype(BF16).reshape(4, 64, 256)
    part[...] = (conv(2, 0) + conv(3, 1)).astype(part.dtype).reshape(4, 64, 256)
    own0[...] = conv(0, 2).reshape(4, 64, 256)


def decode_body(
    p0, p1, o0, o1, pt0, pt1, t0, t1, pb0, pb1, b0, b1, weight, cot, slope, wide
):
    frames = ((p0, pt0, pb0), (p1, pt1, pb1), (o0, t0, b0), (o1, t1, b1))
    for f, (mid, top, bottom) in enumerate(frames):
        wide[f, 0] = jnp.concatenate(neighbour_cols(top[0]), axis=1)
        wide[f, 5] = jnp.concatenate(neighbour_cols(bottom[0]), axis=1)

        def one(r, carry, f=f, mid=mid):
            wide[f, r + 1] = jnp.concatenate(neighbour_cols(mid[r]), axis=1)
            return carry

        lax.fori_loop(0, 4, one, 0)
    for t in range(2):
        pre = None
        for a in range(3):
            for b in range(3):
                window = wide[t + a, b : b + 4].reshape(256, 768)
                term = dot(window, weight[a, b].reshape(768, 128))
                pre = term if pre is None else pre + term
        sigm = jax.nn.sigmoid(pre)
        grad = cot[t].reshape(256, 128).astype(F32)
        slope[t] = (grad * sigm * (1.0 + pre * (1.0 - sigm))).astype(BF16).reshape(4, 64, 128)


def grads_body(
    where, slope, later, top, bottom, ltop, lbottom, weight, taps, before, btop, wide,
    lat_grad, own, send, gathered, rim, btaps, stage,
):
    seg = where[0]
    core = where[1]

    @pl.when(seg == 0)
    def _():
        for f in range(4):
            mid = slope if f < 2 else later
            up = top if f < 2 else ltop
            down = bottom if f < 2 else lbottom
            i = f % 2

            def lay(row):
                left, same, right = neighbour_cols(row)
                return jnp.concatenate([right, same, left], axis=1)

            rim[f, 0] = lay(up[i, 0])
            rim[f, 5] = lay(down[i, 0])
            for r in range(4):
                rim[f, r + 1] = lay(mid[i, r])
        fill_clip(stage, before, btop, btaps, 2)
        grads = []
        for t in range(2):
            total = None
            for a in range(3):
                for b in range(3):
                    window = rim[t + 2 - a, 2 - b : 6 - b].reshape(256, 384)
                    side = jnp.concatenate([weight[a, b, c] for c in range(3)], axis=1)
                    term = dot_nt(window, side)
                    total = term if total is None else total + term
            grad = total.astype(BF16)
            lat_grad[t] = grad.reshape(4, 64, 256)
            grads.append(grad)
        for a in range(3):
            for b in range(3):
                total = None
                for t in range(2):
                    f = 2 * t + a
                    rows = clip_im2col(btaps, f, b) if f < 2 else clip_im2col(taps, f - 2, b)
                    term = dot_tn(rows, grads[t])
                    total = term if total is None else total + term
                for c in range(3):
                    tap = (a * 3 + b) * 3 + c
                    for j in range(2):
                        gathered[pl.ds(tap * 256 + j, 128, stride=2), :] = total[
                            c * 128 : (c + 1) * 128, j * 128 : (j + 1) * 128
                        ]

    @pl.when(seg != 0)
    def _():
        lat_grad[...] = jnp.zeros(lat_grad.shape, BF16)
        for a in range(3):
            for b in range(3):
                total = None
                for t in range(2):
                    window = wide[t + a, b : b + 4].reshape(256, 768)
                    term = dot_tn(window, slope[t].reshape(256, 128))
                    total = term if total is None else total + term
                start = (a * 3 + b) * 768
                gathered[start : start + 768, :] = total

    half = own.shape[0]
    own[...] = gathered[pl.ds(pl.multiple_of(core * half, 8), half), :]
    send[...] = gathered[pl.ds(pl.multiple_of((1 - core) * half, 8), half), :].astype(BF16)


def part_of(ref, start, chunk, rows):
    return ref[pl.ds(pl.multiple_of(start + chunk * rows, 8), rows), :]


def halves_body(where, own, got, a_own, a1, a2, a3, b_own, b1, b2, b3, held):
    held[...] = own[...] + got[...].astype(F32)
    for start, at, mine, outs in ((0, where[0], a_own, (a1, a2, a3)), (1728, where[1], b_own, (b1, b2, b3))):
        mine[...] = part_of(held, start, at, 432)
        for k, out in enumerate(outs):
            out[...] = part_of(held, start, (at + k + 1) % 4, 432).astype(BF16)


def second_body(
    where, a_own, ra1, ra2, ra3, b_own, rb1, rb2, rb3, oa, a1, a2, a3, ob, b1, b2, b3, held
):
    held[...] = jnp.zeros(held.shape, F32)
    for start, at, own, got, mine, outs in (
        (0, where[1], a_own, (ra1, ra2, ra3), oa, (a1, a2, a3)),
        (448, where[0], b_own, (rb1, rb2, rb3), ob, (b1, b2, b3)),
    ):
        total = own[...]
        for one in got:
            total = total + one[...].astype(F32)
        held[start : start + 432, :] = total
        mine[...] = part_of(held, start, at, 112)
        for k, out in enumerate(outs):
            out[...] = part_of(held, start, (at + k + 1) % 4, 112)


def third_body(where, a_own, ra1, ra2, ra3, b_own, rb1, rb2, rb3, mine, s1, s2, s3, held):
    held[0:112, :] = a_own[...] + ra1[...] + ra2[...] + ra3[...]
    held[112:224, :] = b_own[...] + rb1[...] + rb2[...] + rb3[...]
    at = where[2]
    mine[...] = part_of(held, 0, at, 56)
    for k, out in enumerate((s1, s2, s3)):
        out[...] = part_of(held, 0, (at + k + 1) % 4, 56)


def fourth_body(own, r1, r2, r3, total):
    total[...] = own[...] + r1[...] + r2[...] + r3[...]


def put(ref, start, at, rows, pieces):
    for k, piece in enumerate(pieces):
        spot = pl.multiple_of(start + (at + 4 - k) % 4 * rows, 8)
        ref[pl.ds(spot, rows), :] = piece[...].astype(ref.dtype)


def fifth_body(where, own, r1, r2, r3, a, b, held):
    put(held, 0, where[2], 56, (own, r1, r2, r3))
    a[...] = held[0:112, :].astype(BF16)
    b[...] = held[112:224, :].astype(BF16)


def sixth_body(where, a, ra1, ra2, ra3, b, rb1, rb2, rb3, a_out, b_out, held):
    put(held, 0, where[1], 112, (a, ra1, ra2, ra3))
    put(held, 448, where[0], 112, (b, rb1, rb2, rb3))
    a_out[...] = held[0:432, :]
    b_out[...] = held[448 : 448 + 432, :]


def seventh_body(where, a, ra1, ra2, ra3, b, rb1, rb2, rb3, half):
    for start, at, pieces in ((0, where[0], (a, ra1, ra2, ra3)), (1728, where[1], (b, rb1, rb2, rb3))):
        put(half, start, at, 432, pieces)


def moved(array, axis, pairs):
    return lax.ppermute(array, axis, pairs)


def along_x(array, k):
    return moved(array, "tm", [(i, (i + 4 * k) % 16) for i in range(16)])


def along_z(array, k):
    return moved(array, "tm", [(i, i // 4 * 4 + (i + k) % 4) for i in range(16)])


def along_y(array, k):
    return moved(array, "space", [(i, (i + 2 * k) % 8) for i in range(8)])


def to_core(array):
    return moved(array, "space", [(i, i ^ 1) for i in range(8)])


def shifted(array, by_tm, by_space):
    frames = lax.axis_size("tm")
    rows = lax.axis_size("space")
    pairs = [
        (t * rows + s, (t + by_tm) * rows + s + by_space)
        for t in range(frames)
        for s in range(rows)
        if 0 <= t + by_tm < frames and 0 <= s + by_space < rows
    ]
    return moved(array, ("tm", "space"), pairs)


def summed(own, send, spots):
    rows = lambda n, dtype: shape((n, 128), dtype)
    got = to_core(send)
    outs = [rows(432, F32)] + [rows(432, BF16)] * 3
    a, a1, a2, a3, b, b1, b2, b3 = on_chip(
        halves_body, outs + outs, "halves", 1, [pltpu.VMEM((3456, 128), F32)]
    )(spots, own, got)
    ra = [along_x(v, k) for k, v in ((1, a1), (3, a3), (2, a2))]
    rb = [along_y(v, k) for k, v in ((1, b1), (3, b3), (2, b2))]
    outs = [rows(112, F32)] * 4
    a, a1, a2, a3, b, b1, b2, b3 = on_chip(
        second_body, outs + outs, "second", 1, [pltpu.VMEM((896, 128), F32)]
    )(spots, a, *ra, b, *rb)
    ra = [along_y(v, k) for k, v in ((1, a1), (3, a3), (2, a2))]
    rb = [along_x(v, k) for k, v in ((1, b1), (3, b3), (2, b2))]
    own, s1, s2, s3 = on_chip(
        third_body, [rows(56, F32)] * 4, "third", 1, [pltpu.VMEM((224, 128), F32)]
    )(spots, a, *ra, b, *rb)
    got = [along_z(v, k) for k, v in ((1, s1), (3, s3), (2, s2))]
    (total,) = on_chip(fourth_body, [rows(56, F32)], "fourth")(own, *got)
    got = [along_z(total, k) for k in (1, 2, 3)]
    a, b = on_chip(
        fifth_body, [rows(112, BF16)] * 2, "fifth", 1, [pltpu.VMEM((224, 128), F32)]
    )(spots, total, *got)
    ra = [along_y(a, k) for k in (1, 2, 3)]
    rb = [along_x(b, k) for k in (1, 2, 3)]
    a, b = on_chip(
        sixth_body, [rows(432, BF16)] * 2, "sixth", 1, [pltpu.VMEM((896, 128), BF16)]
    )(spots, a, *ra, b, *rb)
    ra = [along_x(a, k) for k in (1, 2, 3)]
    rb = [along_y(b, k) for k in (1, 2, 3)]
    (half,) = on_chip(seventh_body, [rows(3456, BF16)], "seventh", 1)(spots, a, *ra, b, *rb)
    return half, to_core(half)


def on_device(clip_frames, enc_weight, dec_weight, out_grad):
    seg = lax.axis_index("segment")
    tm = lax.axis_index("tm")
    space = lax.axis_index("space")
    core = space % 2
    spots = jnp.stack([tm // 4, space // 2, tm % 4])

    above = shifted(clip_frames[:, 7:8], 0, 1)
    lat1, part, own0, taps = on_chip(
        encode_body,
        [
            shape((4, 64, 256), BF16),
            shape((4, 64, 256), PART),
            shape((4, 64, 256), F32),
            shape((4, 9, 64, 384), BF16),
        ],
        "encode",
        scratch=[pltpu.VMEM((136, 128), F32)],
    )(clip_frames, above, enc_weight)

    def halo(lat):
        return (
            shifted(lat, 1, 0),
            shifted(lat[3:4], 0, 1),
            shifted(lat[0:1], 0, -1),
            shifted(lat[3:4], 1, 1),
            shifted(lat[0:1], 1, -1),
        )

    part = shifted(part, 1, 0)
    p1, t1, b1, pt1, pb1 = halo(lat1)
    lat0 = (own0 + part.astype(F32)).astype(BF16)
    p0, t0, b0, pt0, pb0 = halo(lat0)
    slope, wide = on_chip(
        decode_body, [shape((2, 4, 64, 128), BF16), shape((4, 6, 64, 768), BF16)], "decode"
    )(p0, p1, lat0, lat1, pt0, pt1, t0, t1, pb0, pb1, b0, b1, dec_weight, out_grad)

    clip_late, above_late, _ = lax.optimization_barrier((clip_frames[2:4], above[2:4], p0))
    before = shifted(clip_late, 1, 0)
    before_top = shifted(above_late, 1, 0)
    later = shifted(slope, -1, 0)
    top = shifted(slope[:, 3:4], 0, 1)
    bottom = shifted(slope[:, 0:1], 0, -1)
    later_top = shifted(slope[:, 3:4], -1, 1)
    later_bottom = shifted(slope[:, 0:1], -1, -1)
    lat_grad, own, send = on_chip(
        grads_body,
        [
            shape((2, 4, 64, 256), BF16),
            shape((3456, 128), F32),
            shape((3456, 128), BF16),
        ],
        "grads",
        1,
        [
            pltpu.VMEM((6912, 128), F32),
            pltpu.VMEM((4, 6, 64, 384), BF16),
            pltpu.VMEM((2, 9, 64, 384), BF16),
            pltpu.VMEM((136, 128), F32),
        ],
    )(
        jnp.stack([seg, core]),
        slope, later, top, bottom, later_top, later_bottom, dec_weight, taps, before, before_top, wide,
    )
    latent = jnp.stack([lat0, lat1])
    latent_pair = jnp.where(seg == 0, lat_grad, latent)[None]
    half, other = summed(own, send, spots)
    whole = jnp.where(core == 0, jnp.stack([half, other]), jnp.stack([other, half]))
    weight_grads = whole.reshape(27, 32768).astype(F32) * (1.0 / math.sqrt(32 * 32 * 64))
    return latent_pair, weight_grads[None]


def solution(mesh):
    placed = (P("tm", "space", None, None), P(), P(), P("tm", "space", None, None))
    return jax.shard_map(
        on_device,
        mesh=mesh,
        in_specs=placed,
        out_specs=(P("segment", "tm", "space", None, None), P("segment", None, None)),
        check_vma=False,
    )
```

time: 1750 us -> 229 us (0.13)
  waiting for transfers between devices: 1430 us -> 51.6 us
  local copies, waits for them, and re-layouts: 222 us -> 10.2 us
  starting transfers between devices: 41.5 us -> 126 us
  Pallas kernels: 0 us -> 31.4 us
  matrix products: 18 us -> 0 us
    psum x1 -> x0, waiting for transfers between devices: 1360 us -> none  [on_device(): summed_grads = lax.psum(own_grad, ('tm', 'space'))]
    slice x56 -> x6, local copies, waits for them, and re-layouts: 184 us -> 3.37 us  [the longest x1 0.92 us: on_device(): above = shifted(clip_frames[:, 7:8], 0, 1)]
    ppermute x10 -> x51, starting transfers between devices: 41.5 us -> 126 us  [moved(): return lax.ppermute(array, axis, pairs)]
    pallas_call x0 -> x10, Pallas kernels: none -> 31.4 us  [call(): pl.pallas_call(body, out_shape=outs, in_specs=specs, out_specs=[pl.BlockS...]
    another operation x9 -> x0, local copies, waits for them, and re-layouts: 24.1 us -> none
    ppermute x10 -> x51, waiting for transfers between devices: 70.1 us -> 51.6 us  [moved(): return lax.ppermute(array, axis, pairs)]
    dot_general x54 -> x0, matrix products: 18 us -> none  [the longest x27 9.23 us: encode_taps(): jnp.dot(window.reshape(-1, chans), enc_weight[tap_t, tap_h, tap_w], prefe...]
  transfers between devices with their start and end apart: 11 -> 51, of which waited for: 9 -> 26; matrix products, arithmetic and copies ran while one was open for 0% -> 2% of each run, Pallas kernels for 0% -> 2%
where the time goes in v1:
time: 229 us; the launch traced here: 227 us
  starting transfers between devices  126 us (55%)
  waiting for transfers between devices  51.6 us (23%)
  Pallas kernels  31.4 us (14%)
  local copies, waits for them, and re-layouts  10.2 us (4%)
  other arithmetic  6.62 us (3%)
    ppermute x51, starting transfers between devices, moved(): return lax.ppermute(array, axis, pairs)  126 us
    ppermute x51, waiting for transfers between devices, moved(): return lax.ppermute(array, axis, pairs)  51.6 us
    pallas_call x10, Pallas kernels, call(): pl.pallas_call(body, out_shape=outs, in_specs=specs, out_specs=[pl.BlockS...  31.4 us
    unnamed x110, local copies, waits for them, and re-layouts  6.82 us
  transfers between devices with their start and end apart: 51, of which 26 were waited for; matrix products, arithmetic and copies ran while one was open for 2% of the time, Pallas kernels for 2%

profile of v1, /device:TPU:1, one launch (start us, length us, event | category | flops | bytes accessed | tf_op | source)
XLA Modules:
  0.0 227.5 jit_solution(4152343864861261965)
XLA Ops:
  1.6 4.7 %collective-permute-start = (bf16[4,1,128,128]{3,2,1,0:T(8,128)(2,1)S(1)}, bf16[4,1,128,128]{3,2,1,0:T(8,128)(2,1)S(1)}, u32[]{:S(2)}, u32[]{:S(2)}) collective-permute-start(bf16[4,1,128,128]{3,2,1,0:T(8,128)(2,1)S(1)} %slice.33), channel_id=1, source_target_pairs={{0,1},{1,2},{2,3},{3,4},{4,5},{5,6},{6,7},{8,9},{9,10},{10,11},{11... | collective-permute-start | bytes 393224 | tf_op jit(solution)/shard_map/ppermute | solution.py:258
  8.9 4.8 %encode.1 = (bf16[4,64,256]{2,1,0:T(8,128)(2,1)}, bf16[4,64,256]{2,1,0:T(8,128)(2,1)}, f32[4,64,256]{2,1,0:T(8,128)}, bf16[4,9,64,384]{3,2,1,0:T(8,128)(2,1)}) custom-call(bf16[4,8,128,128]{3,2,1,0:T(8,128)(2,1)} %clip.1, bf16[4,1,128,128]{3,2,1,0:T(8,128)(2,1)} %copy-done.7, bf16[3,3,3,128,256]{4,3,2,1,0:T(8,128)(2,1)} %weight.3), custom_call_target="tpu_custom_call" | custom-call | tf_op jit(solution)/shard_map/encode/pallas_call | solution.py:24
  13.7 5.0 %collective-permute-start.1 = (bf16[4,64,256]{2,1,0:T(8,128)(2,1)}, bf16[4,64,256]{2,1,0:T(8,128)(2,1)S(1)}, u32[]{:S(2)}, u32[]{:S(2)}) collective-permute-start(bf16[4,64,256]{2,1,0:T(8,128)(2,1)} %get-tuple-element.38), channel_id=1, source_target_pairs={{0,8},{1,9},{2,10},{3,11},{4,12},{5,13},{6,14},{7,15},{8,16},{9,17... | collective-permute-start | bytes 393224 | tf_op jit(solution)/shard_map/ppermute | solution.py:258
  18.7 2.8 %collective-permute-done.1 = bf16[4,64,256]{2,1,0:T(8,128)(2,1)S(1)} collective-permute-done((bf16[4,64,256]{2,1,0:T(8,128)(2,1)}, bf16[4,64,256]{2,1,0:T(8,128)(2,1)S(1)}, u32[]{:S(2)}, u32[]{:S(2)}) %collective-permute-start.1) | collective-permute-done | bytes 131104 | tf_op jit(solution)/shard_map/ppermute | solution.py:258
  22.5 7.4 %collective-permute-start.2 = (bf16[4,64,256]{2,1,0:T(8,128)(2,1)S(1)}, bf16[4,64,256]{2,1,0:T(8,128)(2,1)S(1)}, u32[]{:S(2)}, u32[]{:S(2)}) collective-permute-start(bf16[4,64,256]{2,1,0:T(8,128)(2,1)S(1)} %add_convert_fusion.o0), channel_id=1, source_target_pairs={{0,8},{1,9},{2,10},{3,11},{4,12},{5,13},{6,14},{7,15},{8,16},{9,17... | collective-permute-start | bytes 393224 | tf_op jit(solution)/shard_map/ppermute | solution.py:258
  32.7 4.8 %collective-permute-start.9 = (bf16[1,64,256]{2,1,0:T(8,128)(2,1)S(1)}, bf16[1,64,256]{2,1,0:T(8,128)(2,1)S(1)}, u32[]{:S(2)}, u32[]{:S(2)}) collective-permute-start(bf16[1,64,256]{2,1,0:T(8,128)(2,1)S(1)} %get-tuple-element.78), channel_id=1, source_target_pairs={{1,8},{2,9},{3,10},{4,11},{5,12},{6,13},{7,14},{9,16},{10,17},{11,... | collective-permute-start | bytes 98312 | tf_op jit(solution)/shard_map/ppermute | solution.py:258
  37.5 4.4 %collective-permute-start.7 = (bf16[1,64,256]{2,1,0:T(8,128)(2,1)S(1)}, bf16[1,64,256]{2,1,0:T(8,128)(2,1)S(1)}, u32[]{:S(2)}, u32[]{:S(2)}) collective-permute-start(bf16[1,64,256]{2,1,0:T(8,128)(2,1)S(1)} %get-tuple-element.79), channel_id=1, source_target_pairs={{0,1},{1,2},{2,3},{3,4},{4,5},{5,6},{6,7},{8,9},{9,10},{10,11},{11... | collective-permute-start | bytes 98312 | tf_op jit(solution)/shard_map/ppermute | solution.py:258
  41.9 5.2 %collective-permute-start.5 = (bf16[1,64,256]{2,1,0:T(8,128)(2,1)S(1)}, bf16[1,64,256]{2,1,0:T(8,128)(2,1)S(1)}, u32[]{:S(2)}, u32[]{:S(2)}) collective-permute-start(bf16[1,64,256]{2,1,0:T(8,128)(2,1)S(1)} %get-tuple-element.79), channel_id=1, source_target_pairs={{0,9},{1,10},{2,11},{3,12},{4,13},{5,14},{6,15},{8,17},{9,18},{10,... | collective-permute-start | bytes 98312 | tf_op jit(solution)/shard_map/ppermute | solution.py:258
  50.1 3.9 %collective-permute-start.17 = (bf16[2,8,128,128]{3,2,1,0:T(8,128)(2,1)S(1)}, bf16[2,8,128,128]{3,2,1,0:T(8,128)(2,1)S(1)}, u32[]{:S(2)}, u32[]{:S(2)}) collective-permute-start(bf16[2,8,128,128]{3,2,1,0:T(8,128)(2,1)S(1)} %slice.40), channel_id=1, source_target_pairs={{0,8},{1,9},{2,10},{3,11},{4,12},{5,13},{6,14},{7,15},{8,16},{9,17... | collective-permute-start | bytes 1572872 | tf_op jit(solution)/shard_map/ppermute | solution.py:258
  56.0 3.5 %collective-permute-start.8 = (bf16[1,64,256]{2,1,0:T(8,128)(2,1)S(1)}, bf16[1,64,256]{2,1,0:T(8,128)(2,1)S(1)}, u32[]{:S(2)}, u32[]{:S(2)}) collective-permute-start(bf16[1,64,256]{2,1,0:T(8,128)(2,1)S(1)} %get-tuple-element.80), channel_id=1, source_target_pairs={{1,8},{2,9},{3,10},{4,11},{5,12},{6,13},{7,14},{9,16},{10,17},{11,... | collective-permute-start | bytes 98312 | tf_op jit(solution)/shard_map/ppermute | solution.py:258
  59.5 5.9 %collective-permute-start.6 = (bf16[1,64,256]{2,1,0:T(8,128)(2,1)S(1)}, bf16[1,64,256]{2,1,0:T(8,128)(2,1)S(1)}, u32[]{:S(2)}, u32[]{:S(2)}) collective-permute-start(bf16[1,64,256]{2,1,0:T(8,128)(2,1)S(1)} %get-tuple-element.81), channel_id=1, source_target_pairs={{0,1},{1,2},{2,3},{3,4},{4,5},{5,6},{6,7},{8,9},{9,10},{10,11},{11... | collective-permute-start | bytes 98312 | tf_op jit(solution)/shard_map/ppermute | solution.py:258
  65.5 3.4 %collective-permute-start.4 = (bf16[1,64,256]{2,1,0:T(8,128)(2,1)S(1)}, bf16[1,64,256]{2,1,0:T(8,128)(2,1)S(1)}, u32[]{:S(2)}, u32[]{:S(2)}) collective-permute-start(bf16[1,64,256]{2,1,0:T(8,128)(2,1)S(1)} %get-tuple-element.81), channel_id=1, source_target_pairs={{0,9},{1,10},{2,11},{3,12},{4,13},{5,14},{6,15},{8,17},{9,18},{10,... | collective-permute-start | bytes 98312 | tf_op jit(solution)/shard_map/ppermute | solution.py:258
  68.9 11.2 %collective-permute-done.8.pb0 = bf16[1,64,256]{2,1,0:T(8,128)(2,1)S(1)} collective-permute-done((bf16[1,64,256]{2,1,0:T(8,128)(2,1)S(1)}, bf16[1,64,256]{2,1,0:T(8,128)(2,1)S(1)}, u32[]{:S(2)}, u32[]{:S(2)}) %collective-permute-start.8) | collective-permute-done | bytes 32800 | tf_op jit(solution)/shard_map/ppermute | solution.py:258
  81.5 4.9 %decode.1 = (bf16[2,4,64,128]{3,2,1,0:T(8,128)(2,1)}, bf16[4,6,64,768]{3,2,1,0:T(8,128)(2,1)}) custom-call(bf16[4,64,256]{2,1,0:T(8,128)(2,1)} %copy-done.10, bf16[4,64,256]{2,1,0:T(8,128)(2,1)} %copy-done.11, bf16[4,64,256]{2,1,0:T(8,128)(2,1)} %copy-done.1, bf16[4,64,256]{2,1,0:T(8,128)(2,1)} %get-tuple-element.39.o1, bf16[1,64,256]{2,1,0:T(8,128)(2,1)} %copy-done.42, ...), custom_call_target="tpu_custom_call" | custom-call | tf_op jit(solution)/shard_map/decode/pallas_call | solution.py:24
  88.5 2.1 collective-permute-start.14
  93.3 3.1 %collective-permute-done.16.lbottom = bf16[2,1,64,128]{3,2,1,0:T(8,128)(2,1)S(1)} collective-permute-done((bf16[2,1,64,128]{3,2,1,0:T(8,128)(2,1)S(1)}, bf16[2,1,64,128]{3,2,1,0:T(8,128)(2,1)S(1)}, u32[]{:S(2)}, u32[]{:S(2)}) %collective-permute-start.16) | collective-permute-done | bytes 32800 | tf_op jit(solution)/shard_map/ppermute | solution.py:258
  96.4 2.4 %collective-permute-start.13 = (bf16[2,1,64,128]{3,2,1,0:T(8,128)(2,1)S(1)}, bf16[2,1,64,128]{3,2,1,0:T(8,128)(2,1)S(1)}, u32[]{:S(2)}, u32[]{:S(2)}) collective-permute-start(bf16[2,1,64,128]{3,2,1,0:T(8,128)(2,1)S(1)} %get-tuple-element.77), channel_id=1, source_target_pairs={{0,1},{1,2},{2,3},{3,4},{4,5},{5,6},{6,7},{8,9},{9,10},{10,11},{11... | collective-permute-start | bytes 98312 | tf_op jit(solution)/shard_map/ppermute | solution.py:258
  98.8 7.3 %collective-permute-start.18 = (bf16[2,1,128,128]{3,2,1,0:T(8,128)(2,1)S(1)}, bf16[2,1,128,128]{3,2,1,0:T(8,128)(2,1)S(1)}, u32[]{:S(2)}, u32[]{:S(2)}) collective-permute-start(bf16[2,1,128,128]{3,2,1,0:T(8,128)(2,1)S(1)} %slice.44), channel_id=1, source_target_pairs={{0,8},{1,9},{2,10},{3,11},{4,12},{5,13},{6,14},{7,15},{8,16},{9,17... | collective-permute-start | bytes 196616 | tf_op jit(solution)/shard_map/ppermute | solution.py:258
  108.3 8.1 %grads.1 = (bf16[2,4,64,256]{3,2,1,0:T(8,128)(2,1)}, f32[3456,128]{1,0:T(8,128)}, bf16[3456,128]{1,0:T(8,128)(2,1)}) custom-call(s32[2]{0:T(128)} %pad_add_fusion.where, bf16[2,4,64,128]{3,2,1,0:T(8,128)(2,1)} %get-tuple-element.40.slope, bf16[2,4,64,128]{3,2,1,0:T(8,128)(2,1)} %copy-done.9, bf16[2,1,64,128]{3,2,1,0:T(8,128)(2,1)} %copy-done.39, ...), custom_call_target="tpu_custom_call" | custom-call | tf_op jit(solution)/shard_map/grads/pallas_call | solution.py:24
  119.9 2.9 %halves.1 = (f32[432,128]{1,0:T(8,128)}, bf16[432,128]{1,0:T(8,128)(2,1)}, bf16[432,128]{1,0:T(8,128)(2,1)}, bf16[432,128]{1,0:T(8,128)(2,1)}, f32[432,128]{1,0:...) custom-call(s32[3]{0:T(128)} %pad_add_fusion.1.where, ...), custom_call_target="tpu_custom_call" | custom-call | tf_op jit(solution)/shard_map/halves/pallas_call | solution.py:24
  122.9 11.1 %collective-permute-start.20 = (bf16[432,128]{1,0:T(8,128)(2,1)}, bf16[432,128]{1,0:T(8,128)(2,1)S(1)}, u32[]{:S(2)}, u32[]{:S(2)}) collective-permute-start(bf16[432,128]{1,0:T(8,128)(2,1)} %get-tuple-element.49), channel_id=1, source_target_pairs={{0,32},{8,40},{16,48},{24,56},{32,64},{40,72},{48,80},{56,88},{64,... | collective-permute-start | bytes 331784 | tf_op jit(solution)/shard_map/ppermute | solution.py:258
  142.8 2.2 collective-permute-done.25.rb3
  145.6 2.2 second.1
  151.7 2.2 collective-permute-start.30
  156.0 3.4 %collective-permute-done.31.rb3 = f32[112,128]{1,0:T(8,128)S(1)} collective-permute-done((f32[112,128]{1,0:T(8,128)}, f32[112,128]{1,0:T(8,128)S(1)}, u32[]{:S(2)}, u32[]{:S(2)}) %collective-permute-start.31) | collective-permute-done | bytes 57376 | tf_op jit(solution)/shard_map/ppermute | solution.py:258
  162.9 2.4 %collective-permute-start.33 = (f32[56,128]{1,0:T(8,128)}, f32[56,128]{1,0:T(8,128)S(1)}, u32[]{:S(2)}, u32[]{:S(2)}) collective-permute-start(f32[56,128]{1,0:T(8,128)} %get-tuple-element.66), channel_id=1, source_target_pairs={{0,24},{8,0},{16,8},{24,16},{32,56},{40,32},{48,40},{56,48},{64,88... | collective-permute-start | bytes 86024 | tf_op jit(solution)/shard_map/ppermute | solution.py:258
  167.3 5.0 %collective-permute-done.34.r3 = f32[56,128]{1,0:T(8,128)S(1)} collective-permute-done((f32[56,128]{1,0:T(8,128)}, f32[56,128]{1,0:T(8,128)S(1)}, u32[]{:S(2)}, u32[]{:S(2)}) %collective-permute-start.34) | collective-permute-done | bytes 28704 | tf_op jit(solution)/shard_map/ppermute | solution.py:258
  174.3 3.1 %collective-permute-start.36 = (f32[56,128]{1,0:T(8,128)}, f32[56,128]{1,0:T(8,128)S(1)}, u32[]{:S(2)}, u32[]{:S(2)}) collective-permute-start(f32[56,128]{1,0:T(8,128)} %fourth.1.own), channel_id=1, source_target_pairs={{0,16},{8,24},{16,0},{24,8},{32,48},{40,56},{48,32},{56,40},{64,80... | collective-permute-start | bytes 86024 | tf_op jit(solution)/shard_map/ppermute | solution.py:258
  178.8 2.5 %collective-permute-done.36.r2 = f32[56,128]{1,0:T(8,128)S(1)} collective-permute-done((f32[56,128]{1,0:T(8,128)}, f32[56,128]{1,0:T(8,128)S(1)}, u32[]{:S(2)}, u32[]{:S(2)}) %collective-permute-start.36) | collective-permute-done | bytes 28704 | tf_op jit(solution)/shard_map/ppermute | solution.py:258
  207.2 2.2 seventh.1
  209.4 12.1 %collective-permute-start.50 = (bf16[3456,128]{1,0:T(8,128)(2,1)}, bf16[3456,128]{1,0:T(8,128)(2,1)S(1)}, u32[]{:S(2)}, u32[]{:S(2)}) collective-permute-start(bf16[3456,128]{1,0:T(8,128)(2,1)} %seventh.1), channel_id=1, source_target_pairs={{0,1},{1,0},{2,3},{3,2},{4,5},{5,4},{6,7},{7,6},{8,9},{9,8},{10,11... | collective-permute-start | bytes 2654216 | tf_op jit(solution)/shard_map/ppermute | solution.py:258
  223.8 3.7 %convert_multiply_fusion = f32[2,3456,128]{2,1,0:T(8,128)} fusion(bf16[1,3456,128]{2,1,0:T(8,128)(2,1)S(1)} %bitcast.15, bf16[1,3456,128]{2,1,0:T(8,128)(2,1)} %bitcast.13, pred[]{:T(512)S(6)} %eq.10), kind=kLoop, calls=%fused_computation | loop fusion | flops 4423680 | bytes 5308417 | tf_op jit(solution)/shard_map/mul | solution.py:392
  (201 shorter events, 76.0 us)
Async XLA Ops:
  1.6 6.6 %collective-permute-start = (bf16[4,1,128,128]{3,2,1,0:T(8,128)(2,1)S(1)}, bf16[4,1,128,128]{3,2,1,0:T(8,128)(2,1)S(1)}, u32[]{:S(2)}, u32[]{:S(2)}) collective-permute-start(bf16[4,1,128,128]{3,2,1,0:T(8,128)(2,1)S(1)} %slice.33), channel_id=1, source_target_pairs={{0,1},{1,2},{2,3},{3,4},{4,5},{5,6},{6,7},{8,9},{9,10},{10,11},{11... | collective-permute-start | bytes 393224 | tf_op jit(solution)/shard_map/ppermute | solution.py:258
  13.7 7.8 %collective-permute-start.1 = (bf16[4,64,256]{2,1,0:T(8,128)(2,1)}, bf16[4,64,256]{2,1,0:T(8,128)(2,1)S(1)}, u32[]{:S(2)}, u32[]{:S(2)}) collective-permute-start(bf16[4,64,256]{2,1,0:T(8,128)(2,1)} %get-tuple-element.38), channel_id=1, source_target_pairs={{0,8},{1,9},{2,10},{3,11},{4,12},{5,13},{6,14},{7,15},{8,16},{9,17... | collective-permute-start | bytes 393224 | tf_op jit(solution)/shard_map/ppermute | solution.py:258
  22.5 25.5 %collective-permute-start.2 = (bf16[4,64,256]{2,1,0:T(8,128)(2,1)S(1)}, bf16[4,64,256]{2,1,0:T(8,128)(2,1)S(1)}, u32[]{:S(2)}, u32[]{:S(2)}) collective-permute-start(bf16[4,64,256]{2,1,0:T(8,128)(2,1)S(1)} %add_convert_fusion.o0), channel_id=1, source_target_pairs={{0,8},{1,9},{2,10},{3,11},{4,12},{5,13},{6,14},{7,15},{8,16},{9,17... | collective-permute-start | bytes 393224 | tf_op jit(solution)/shard_map/ppermute | solution.py:258
  30.7 19.3 %collective-permute-start.11 = (bf16[1,64,256]{2,1,0:T(8,128)(2,1)S(1)}, bf16[1,64,256]{2,1,0:T(8,128)(2,1)S(1)}, u32[]{:S(2)}, u32[]{:S(2)}) collective-permute-start(bf16[1,64,256]{2,1,0:T(8,128)(2,1)S(1)} %get-tuple-element.78), channel_id=1, source_target_pairs={{1,0},{2,1},{3,2},{4,3},{5,4},{6,5},{7,6},{9,8},{10,9},{11,10},{12... | collective-permute-start | bytes 98312 | tf_op jit(solution)/shard_map/ppermute | solution.py:258
  32.7 21.3 %collective-permute-start.9 = (bf16[1,64,256]{2,1,0:T(8,128)(2,1)S(1)}, bf16[1,64,256]{2,1,0:T(8,128)(2,1)S(1)}, u32[]{:S(2)}, u32[]{:S(2)}) collective-permute-start(bf16[1,64,256]{2,1,0:T(8,128)(2,1)S(1)} %get-tuple-element.78), channel_id=1, source_target_pairs={{1,8},{2,9},{3,10},{4,11},{5,12},{6,13},{7,14},{9,16},{10,17},{11,... | collective-permute-start | bytes 98312 | tf_op jit(solution)/shard_map/ppermute | solution.py:258
  37.5 18.4 %collective-permute-start.7 = (bf16[1,64,256]{2,1,0:T(8,128)(2,1)S(1)}, bf16[1,64,256]{2,1,0:T(8,128)(2,1)S(1)}, u32[]{:S(2)}, u32[]{:S(2)}) collective-permute-start(bf16[1,64,256]{2,1,0:T(8,128)(2,1)S(1)} %get-tuple-element.79), channel_id=1, source_target_pairs={{0,1},{1,2},{2,3},{3,4},{4,5},{5,6},{6,7},{8,9},{9,10},{10,11},{11... | collective-permute-start | bytes 98312 | tf_op jit(solution)/shard_map/ppermute | solution.py:258
  41.9 17.6 %collective-permute-start.5 = (bf16[1,64,256]{2,1,0:T(8,128)(2,1)S(1)}, bf16[1,64,256]{2,1,0:T(8,128)(2,1)S(1)}, u32[]{:S(2)}, u32[]{:S(2)}) collective-permute-start(bf16[1,64,256]{2,1,0:T(8,128)(2,1)S(1)} %get-tuple-element.79), channel_id=1, source_target_pairs={{0,9},{1,10},{2,11},{3,12},{4,13},{5,14},{6,15},{8,17},{9,18},{10,... | collective-permute-start | bytes 98312 | tf_op jit(solution)/shard_map/ppermute | solution.py:258
  48.0 17.5 %collective-permute-start.3 = (bf16[4,64,256]{2,1,0:T(8,128)(2,1)S(1)}, bf16[4,64,256]{2,1,0:T(8,128)(2,1)S(1)}, u32[]{:S(2)}, u32[]{:S(2)}) collective-permute-start(bf16[4,64,256]{2,1,0:T(8,128)(2,1)S(1)} %copy-done.4), channel_id=1, source_target_pairs={{0,8},{1,9},{2,10},{3,11},{4,12},{5,13},{6,14},{7,15},{8,16},{9,17... | collective-permute-start | bytes 393224 | tf_op jit(solution)/shard_map/ppermute | solution.py:258
  50.1 57.4 %collective-permute-start.17 = (bf16[2,8,128,128]{3,2,1,0:T(8,128)(2,1)S(1)}, bf16[2,8,128,128]{3,2,1,0:T(8,128)(2,1)S(1)}, u32[]{:S(2)}, u32[]{:S(2)}) collective-permute-start(bf16[2,8,128,128]{3,2,1,0:T(8,128)(2,1)S(1)} %slice.40), channel_id=1, source_target_pairs={{0,8},{1,9},{2,10},{3,11},{4,12},{5,13},{6,14},{7,15},{8,16},{9,17... | collective-permute-start | bytes 1572872 | tf_op jit(solution)/shard_map/ppermute | solution.py:258
  54.0 14.9 %collective-permute-start.10 = (bf16[1,64,256]{2,1,0:T(8,128)(2,1)S(1)}, bf16[1,64,256]{2,1,0:T(8,128)(2,1)S(1)}, u32[]{:S(2)}, u32[]{:S(2)}) collective-permute-start(bf16[1,64,256]{2,1,0:T(8,128)(2,1)S(1)} %get-tuple-element.80), channel_id=1, source_target_pairs={{1,0},{2,1},{3,2},{4,3},{5,4},{6,5},{7,6},{9,8},{10,9},{11,10},{12... | collective-permute-start | bytes 98312 | tf_op jit(solution)/shard_map/ppermute | solution.py:258
  56.0 24.2 %collective-permute-start.8 = (bf16[1,64,256]{2,1,0:T(8,128)(2,1)S(1)}, bf16[1,64,256]{2,1,0:T(8,128)(2,1)S(1)}, u32[]{:S(2)}, u32[]{:S(2)}) collective-permute-start(bf16[1,64,256]{2,1,0:T(8,128)(2,1)S(1)} %get-tuple-element.80), channel_id=1, source_target_pairs={{1,8},{2,9},{3,10},{4,11},{5,12},{6,13},{7,14},{9,16},{10,17},{11,... | collective-permute-start | bytes 98312 | tf_op jit(solution)/shard_map/ppermute | solution.py:258
  59.5 20.6 %collective-permute-start.6 = (bf16[1,64,256]{2,1,0:T(8,128)(2,1)S(1)}, bf16[1,64,256]{2,1,0:T(8,128)(2,1)S(1)}, u32[]{:S(2)}, u32[]{:S(2)}) collective-permute-start(bf16[1,64,256]{2,1,0:T(8,128)(2,1)S(1)} %get-tuple-element.81), channel_id=1, source_target_pairs={{0,1},{1,2},{2,3},{3,4},{4,5},{5,6},{6,7},{8,9},{9,10},{10,11},{11... | collective-permute-start | bytes 98312 | tf_op jit(solution)/shard_map/ppermute | solution.py:258
  65.5 15.4 %collective-permute-start.4 = (bf16[1,64,256]{2,1,0:T(8,128)(2,1)S(1)}, bf16[1,64,256]{2,1,0:T(8,128)(2,1)S(1)}, u32[]{:S(2)}, u32[]{:S(2)}) collective-permute-start(bf16[1,64,256]{2,1,0:T(8,128)(2,1)S(1)} %get-tuple-element.81), channel_id=1, source_target_pairs={{0,9},{1,10},{2,11},{3,12},{4,13},{5,14},{6,15},{8,17},{9,18},{10,... | collective-permute-start | bytes 98312 | tf_op jit(solution)/shard_map/ppermute | solution.py:258
  87.2 9.2 %collective-permute-start.16 = (bf16[2,1,64,128]{3,2,1,0:T(8,128)(2,1)S(1)}, bf16[2,1,64,128]{3,2,1,0:T(8,128)(2,1)S(1)}, u32[]{:S(2)}, u32[]{:S(2)}) collective-permute-start(bf16[2,1,64,128]{3,2,1,0:T(8,128)(2,1)S(1)} %get-tuple-element.76), channel_id=1, source_target_pairs={{9,0},{10,1},{11,2},{12,3},{13,4},{14,5},{15,6},{17,8},{18,9},{19,... | collective-permute-start | bytes 98312 | tf_op jit(solution)/shard_map/ppermute | solution.py:258
  88.5 10.3 %collective-permute-start.14 = (bf16[2,1,64,128]{3,2,1,0:T(8,128)(2,1)S(1)}, bf16[2,1,64,128]{3,2,1,0:T(8,128)(2,1)S(1)}, u32[]{:S(2)}, u32[]{:S(2)}) collective-permute-start(bf16[2,1,64,128]{3,2,1,0:T(8,128)(2,1)S(1)} %get-tuple-element.76), channel_id=1, source_target_pairs={{1,0},{2,1},{3,2},{4,3},{5,4},{6,5},{7,6},{9,8},{10,9},{11,10},{12... | collective-permute-start | bytes 98312 | tf_op jit(solution)/shard_map/ppermute | solution.py:258
  90.7 16.8 %collective-permute-start.12 = (bf16[2,4,64,128]{3,2,1,0:T(8,128)(2,1)}, bf16[2,4,64,128]{3,2,1,0:T(8,128)(2,1)S(1)}, u32[]{:S(2)}, u32[]{:S(2)}) collective-permute-start(bf16[2,4,64,128]{3,2,1,0:T(8,128)(2,1)} %get-tuple-element.40.slope), channel_id=1, source_target_pairs={{8,0},{9,1},{10,2},{11,3},{12,4},{13,5},{14,6},{15,7},{16,8},{17,9... | collective-permute-start | bytes 393224 | tf_op jit(solution)/shard_map/ppermute | solution.py:258
  92.0 14.8 %collective-permute-start.15 = (bf16[2,1,64,128]{3,2,1,0:T(8,128)(2,1)S(1)}, bf16[2,1,64,128]{3,2,1,0:T(8,128)(2,1)S(1)}, u32[]{:S(2)}, u32[]{:S(2)}) collective-permute-start(bf16[2,1,64,128]{3,2,1,0:T(8,128)(2,1)S(1)} %get-tuple-element.77), channel_id=1, source_target_pairs={{8,1},{9,2},{10,3},{11,4},{12,5},{13,6},{14,7},{16,9},{17,10},{18,... | collective-permute-start | bytes 98312 | tf_op jit(solution)/shard_map/ppermute | solution.py:258
  96.4 10.4 %collective-permute-start.13 = (bf16[2,1,64,128]{3,2,1,0:T(8,128)(2,1)S(1)}, bf16[2,1,64,128]{3,2,1,0:T(8,128)(2,1)S(1)}, u32[]{:S(2)}, u32[]{:S(2)}) collective-permute-start(bf16[2,1,64,128]{3,2,1,0:T(8,128)(2,1)S(1)} %get-tuple-element.77), channel_id=1, source_target_pairs={{0,1},{1,2},{2,3},{3,4},{4,5},{5,6},{6,7},{8,9},{9,10},{10,11},{11... | collective-permute-start | bytes 98312 | tf_op jit(solution)/shard_map/ppermute | solution.py:258
  98.8 8.7 %collective-permute-start.18 = (bf16[2,1,128,128]{3,2,1,0:T(8,128)(2,1)S(1)}, bf16[2,1,128,128]{3,2,1,0:T(8,128)(2,1)S(1)}, u32[]{:S(2)}, u32[]{:S(2)}) collective-permute-start(bf16[2,1,128,128]{3,2,1,0:T(8,128)(2,1)S(1)} %slice.44), channel_id=1, source_target_pairs={{0,8},{1,9},{2,10},{3,11},{4,12},{5,13},{6,14},{7,15},{8,16},{9,17... | collective-permute-start | bytes 196616 | tf_op jit(solution)/shard_map/ppermute | solution.py:258
  122.9 16.8 %collective-permute-start.20 = (bf16[432,128]{1,0:T(8,128)(2,1)}, bf16[432,128]{1,0:T(8,128)(2,1)S(1)}, u32[]{:S(2)}, u32[]{:S(2)}) collective-permute-start(bf16[432,128]{1,0:T(8,128)(2,1)} %get-tuple-element.49), channel_id=1, source_target_pairs={{0,32},{8,40},{16,48},{24,56},{32,64},{40,72},{48,80},{56,88},{64,... | collective-permute-start | bytes 331784 | tf_op jit(solution)/shard_map/ppermute | solution.py:258
  134.0 6.8 %collective-permute-start.21 = (bf16[432,128]{1,0:T(8,128)(2,1)}, bf16[432,128]{1,0:T(8,128)(2,1)S(1)}, u32[]{:S(2)}, u32[]{:S(2)}) collective-permute-start(bf16[432,128]{1,0:T(8,128)(2,1)} %get-tuple-element.50), channel_id=1, source_target_pairs={{0,96},{8,104},{16,112},{24,120},{32,0},{40,8},{48,16},{56,24},{64... | collective-permute-start | bytes 331784 | tf_op jit(solution)/shard_map/ppermute | solution.py:258
  135.5 6.7 %collective-permute-start.22 = (bf16[432,128]{1,0:T(8,128)(2,1)}, bf16[432,128]{1,0:T(8,128)(2,1)S(1)}, u32[]{:S(2)}, u32[]{:S(2)}) collective-permute-start(bf16[432,128]{1,0:T(8,128)(2,1)} %get-tuple-element.51), channel_id=1, source_target_pairs={{0,64},{8,72},{16,80},{24,88},{32,96},{40,104},{48,112},{56,120},{... | collective-permute-start | bytes 331784 | tf_op jit(solution)/shard_map/ppermute | solution.py:258
  147.9 6.0 %collective-permute-start.26 = (f32[112,128]{1,0:T(8,128)}, f32[112,128]{1,0:T(8,128)S(1)}, u32[]{:S(2)}, u32[]{:S(2)}) collective-permute-start(f32[112,128]{1,0:T(8,128)} %get-tuple-element.57), channel_id=1, source_target_pairs={{0,2},{1,3},{2,4},{3,5},{4,6},{5,7},{6,0},{7,1},{8,10},{9,11},{10,... | collective-permute-start | bytes 172040 | tf_op jit(solution)/shard_map/ppermute | solution.py:258
  153.9 5.5 %collective-permute-start.31 = (f32[112,128]{1,0:T(8,128)}, f32[112,128]{1,0:T(8,128)S(1)}, u32[]{:S(2)}, u32[]{:S(2)}) collective-permute-start(f32[112,128]{1,0:T(8,128)} %get-tuple-element.63), channel_id=1, source_target_pairs={{0,64},{8,72},{16,80},{24,88},{32,96},{40,104},{48,112},{56,120},{... | collective-permute-start | bytes 172040 | tf_op jit(solution)/shard_map/ppermute | solution.py:258
  161.7 5.5 %collective-permute-start.32 = (f32[56,128]{1,0:T(8,128)}, f32[56,128]{1,0:T(8,128)S(1)}, u32[]{:S(2)}, u32[]{:S(2)}) collective-permute-start(f32[56,128]{1,0:T(8,128)} %get-tuple-element.65), channel_id=1, source_target_pairs={{0,8},{8,16},{16,24},{24,0},{32,40},{40,48},{48,56},{56,32},{64,72... | collective-permute-start | bytes 86024 | tf_op jit(solution)/shard_map/ppermute | solution.py:258
  165.3 7.0 %collective-permute-start.34 = (f32[56,128]{1,0:T(8,128)}, f32[56,128]{1,0:T(8,128)S(1)}, u32[]{:S(2)}, u32[]{:S(2)}) collective-permute-start(f32[56,128]{1,0:T(8,128)} %get-tuple-element.67), channel_id=1, source_target_pairs={{0,16},{8,24},{16,0},{24,8},{32,48},{40,56},{48,32},{56,40},{64,80... | collective-permute-start | bytes 86024 | tf_op jit(solution)/shard_map/ppermute | solution.py:258
  174.3 7.0 %collective-permute-start.36 = (f32[56,128]{1,0:T(8,128)}, f32[56,128]{1,0:T(8,128)S(1)}, u32[]{:S(2)}, u32[]{:S(2)}) collective-permute-start(f32[56,128]{1,0:T(8,128)} %fourth.1.own), channel_id=1, source_target_pairs={{0,16},{8,24},{16,0},{24,8},{32,48},{40,56},{48,32},{56,40},{64,80... | collective-permute-start | bytes 86024 | tf_op jit(solution)/shard_map/ppermute | solution.py:258
  196.5 5.7 %collective-permute-start.45 = (bf16[432,128]{1,0:T(8,128)(2,1)}, bf16[432,128]{1,0:T(8,128)(2,1)S(1)}, u32[]{:S(2)}, u32[]{:S(2)}) collective-permute-start(bf16[432,128]{1,0:T(8,128)(2,1)} %get-tuple-element.70.a), channel_id=1, source_target_pairs={{0,64},{8,72},{16,80},{24,88},{32,96},{40,104},{48,112},{56,120},{... | collective-permute-start | bytes 331784 | tf_op jit(solution)/shard_map/ppermute | solution.py:258
  198.0 5.6 %collective-permute-start.44 = (bf16[432,128]{1,0:T(8,128)(2,1)}, bf16[432,128]{1,0:T(8,128)(2,1)S(1)}, u32[]{:S(2)}, u32[]{:S(2)}) collective-permute-start(bf16[432,128]{1,0:T(8,128)(2,1)} %get-tuple-element.70.a), channel_id=1, source_target_pairs={{0,32},{8,40},{16,48},{24,56},{32,64},{40,72},{48,80},{56,88},{64,... | collective-permute-start | bytes 331784 | tf_op jit(solution)/shard_map/ppermute | solution.py:258
  198.0 5.6 %collective-permute-start.49 = (bf16[432,128]{1,0:T(8,128)(2,1)}, bf16[432,128]{1,0:T(8,128)(2,1)S(1)}, u32[]{:S(2)}, u32[]{:S(2)}) collective-permute-start(bf16[432,128]{1,0:T(8,128)(2,1)} %get-tuple-element.71.b), channel_id=1, source_target_pairs={{0,6},{1,7},{2,0},{3,1},{4,2},{5,3},{6,4},{7,5},{8,14},{9,15},{10,... | collective-permute-start | bytes 331784 | tf_op jit(solution)/shard_map/ppermute | solution.py:258
  200.4 6.1 %collective-permute-start.47 = (bf16[432,128]{1,0:T(8,128)(2,1)}, bf16[432,128]{1,0:T(8,128)(2,1)S(1)}, u32[]{:S(2)}, u32[]{:S(2)}) collective-permute-start(bf16[432,128]{1,0:T(8,128)(2,1)} %get-tuple-element.71.b), channel_id=1, source_target_pairs={{0,2},{1,3},{2,4},{3,5},{4,6},{5,7},{6,0},{7,1},{8,10},{9,11},{10,... | collective-permute-start | bytes 331784 | tf_op jit(solution)/shard_map/ppermute | solution.py:258
  209.4 14.4 %collective-permute-start.50 = (bf16[3456,128]{1,0:T(8,128)(2,1)}, bf16[3456,128]{1,0:T(8,128)(2,1)S(1)}, u32[]{:S(2)}, u32[]{:S(2)}) collective-permute-start(bf16[3456,128]{1,0:T(8,128)(2,1)} %seventh.1), channel_id=1, source_target_pairs={{0,1},{1,0},{2,3},{3,2},{4,5},{5,4},{6,7},{7,6},{8,9},{9,8},{10,11... | collective-permute-start | bytes 2654216 | tf_op jit(solution)/shard_map/ppermute | solution.py:258
  (74 other events, 715.6 us)

commit v2 on v1

v2 whole, which is shorter than its diff:
```python
import math

import jax
import jax.numpy as jnp
from jax import lax
from jax.experimental import pallas as pl
from jax.experimental.pallas import tpu as pltpu
from jax.sharding import Mesh, PartitionSpec as P

F32 = jnp.float32
BF16 = jnp.bfloat16
PART = BF16
MIB = 1024 * 1024


def shape(dims, dtype):
    return jax.ShapeDtypeStruct(dims, dtype)


def on_chip(body, outs, name, smem=0, scratch=(), grant=10):
    def call(*args):
        specs = [pl.BlockSpec(memory_space=pltpu.SMEM)] * smem
        specs += [pl.BlockSpec(memory_space=pltpu.VMEM)] * (len(args) - smem)
        return pl.pallas_call(
            body,
            out_shape=outs,
            in_specs=specs,
            out_specs=[pl.BlockSpec(memory_space=pltpu.VMEM)] * len(outs),
            scratch_shapes=list(scratch),
            name=name,
            compiler_params=pltpu.CompilerParams(vmem_limit_bytes=grant * MIB),
        )(*args)

    return call


def dot(left, right):
    return jnp.dot(left, right, preferred_element_type=F32)


def dot_tn(left, right):
    return lax.dot_general(left, right, (((0,), (0,)), ((), ())), preferred_element_type=F32)


def dot_nt(left, right):
    return lax.dot_general(left, right, (((1,), (1,)), ((), ())), preferred_element_type=F32)


def clip_windows(row, stage):
    stage[8:136, :] = row.astype(F32)
    before = stage[pl.ds(7, 64, stride=2), :]
    here = stage[pl.ds(8, 64, stride=2), :]
    after = stage[pl.ds(9, 64, stride=2), :]
    return jnp.concatenate([before, here, after], axis=1).astype(BF16)


def neighbour_cols(row):
    wide = row.astype(F32)
    place = lax.broadcasted_iota(jnp.int32, wide.shape, 0)
    last = wide.shape[0] - 1
    before = jnp.where(place == 0, 0.0, pltpu.roll(wide, 1, 0)).astype(BF16)
    after = jnp.where(place == last, 0.0, pltpu.roll(wide, last, 0)).astype(BF16)
    return before, row, after


def fill_clip(stage, src, top, dst, frames):
    stage[0:8, :] = jnp.zeros((8, stage.shape[1]), F32)
    for f in range(frames):
        dst[f, 0] = clip_windows(top[f, 0], stage)

        def one(r, carry, f=f):
            dst[f, r + 1] = clip_windows(src[f, r], stage)
            return carry

        lax.fori_loop(0, 8, one, 0)


def clip_im2col(taps, f, b):
    return jnp.concatenate([taps[f, 2 * h + b] for h in range(4)], axis=0)


def encode_body(clip, top, weight, lat1, part, own0, tail, taps, stage):
    fill_clip(stage, clip, top, taps, 4)

    def conv(f, a):
        total = None
        for b in range(3):
            term = dot(clip_im2col(taps, f, b), weight[a, b].reshape(384, 256))
            total = term if total is None else total + term
        return total

    part[...] = (conv(2, 0) + conv(3, 1)).astype(part.dtype).reshape(4, 64, 256)
    lat1[...] = (conv(0, 0) + conv(1, 1) + conv(2, 2)).astype(BF16).reshape(4, 64, 256)
    own0[...] = conv(0, 2).reshape(4, 64, 256)
    tail[:, 0:1] = top[2:4]
    tail[:, 1:9] = clip[2:4]


def decode_body(lat, top, bottom, weight, own, part, wide):
    for f in range(2):
        wide[f, 0] = jnp.concatenate(neighbour_cols(top[f, 0]), axis=1)
        wide[f, 5] = jnp.concatenate(neighbour_cols(bottom[f, 0]), axis=1)

        def one(r, carry, f=f):
            wide[f, r + 1] = jnp.concatenate(neighbour_cols(lat[f, r]), axis=1)
            return carry

        lax.fori_loop(0, 4, one, 0)

    def conv(f, a):
        total = None
        for b in range(3):
            window = wide[f, b : b + 4].reshape(256, 768)
            term = dot(window, weight[a, b].reshape(768, 128))
            total = term if total is None else total + term
        return total

    part[0] = (conv(0, 0) + conv(1, 1)).astype(part.dtype).reshape(4, 64, 128)
    part[1] = conv(1, 0).astype(part.dtype).reshape(4, 64, 128)
    own[0] = conv(0, 2).reshape(4, 64, 128)
    own[1] = (conv(0, 1) + conv(1, 2)).reshape(4, 64, 128)


def slope_body(own, part, cot, slope):
    pre = own[...] + part[...].astype(F32)
    sigm = jax.nn.sigmoid(pre)
    slope[...] = (cot[...].astype(F32) * sigm * (1.0 + pre * (1.0 - sigm))).astype(BF16)


def grads_body(
    where, slope, later, weight, taps, tail, wide, lat_grad, own, send, gathered, rim, btaps, stage
):
    seg = where[0]
    core = where[1]

    @pl.when(seg == 0)
    def _():
        for f in range(4):
            src = slope if f < 2 else later
            for r in range(6):
                left, same, right = neighbour_cols(src[f % 2, r])
                rim[f, r] = jnp.concatenate([right, same, left], axis=1)
        fill_clip(stage, tail.at[:, 1:9], tail, btaps, 2)
        grads = []
        for t in range(2):
            total = None
            for a in range(3):
                for b in range(3):
                    window = rim[t + 2 - a, 2 - b : 6 - b].reshape(256, 384)
                    side = jnp.concatenate([weight[a, b, c] for c in range(3)], axis=1)
                    term = dot_nt(window, side)
                    total = term if total is None else total + term
            grad = total.astype(BF16)
            lat_grad[t] = grad.reshape(4, 64, 256)
            grads.append(grad)
        for a in range(3):
            for b in range(3):
                total = None
                for t in range(2):
                    f = 2 * t + a
                    rows = clip_im2col(btaps, f, b) if f < 2 else clip_im2col(taps, f - 2, b)
                    term = dot_tn(rows, grads[t])
                    total = term if total is None else total + term
                for c in range(3):
                    tap = (a * 3 + b) * 3 + c
                    for j in range(2):
                        gathered[pl.ds(tap * 256 + j, 128, stride=2), :] = total[
                            c * 128 : (c + 1) * 128, j * 128 : (j + 1) * 128
                        ]

    @pl.when(seg != 0)
    def _():
        lat_grad[...] = jnp.zeros(lat_grad.shape, BF16)
        for a in range(3):
            for b in range(3):
                total = None
                for f in range(2):
                    t = f + 2 - a
                    cells = (slope if t < 2 else later)[t % 2, 1:5].reshape(256, 128)
                    term = dot_tn(wide[f, b : b + 4].reshape(256, 768), cells)
                    total = term if total is None else total + term
                start = (a * 3 + b) * 768
                gathered[start : start + 768, :] = total

    half = own.shape[0]
    own[...] = gathered[pl.ds(pl.multiple_of(core * half, 8), half), :]
    send[...] = gathered[pl.ds(pl.multiple_of((1 - core) * half, 8), half), :].astype(BF16)


def halves_body(own, got, spread):
    for j in range(16):
        rows = slice(216 * j, 216 * (j + 1))
        spread[j] = (own[rows, :] + got[rows, :].astype(F32)).astype(BF16)


def second_body(got, spread, held):
    total = got[0].astype(F32)
    for j in range(1, 16):
        total = total + got[j].astype(F32)
    held[0:216, :] = total
    held[216:224, :] = jnp.zeros((8, 128), F32)
    for j in range(4):
        spread[j] = held[56 * j : 56 * (j + 1), :]


def third_body(got, spread):
    total = got[0] + got[1] + got[2] + got[3]
    for j in range(4):
        spread[j] = total


def fourth_body(got, spread, held):
    for j in range(4):
        held[56 * j : 56 * (j + 1), :] = got[j]
    total = held[0:216, :].astype(BF16)
    for j in range(16):
        spread[j] = total


def exchanged(array, axes):
    return lax.all_to_all(array, axes, 0, 0, tiled=True)


def to_core(array):
    return lax.ppermute(array, "c", [(0, 1), (1, 0)])


def by_frames(array, by):
    pairs = [(i, i + by) for i in range(16) if 0 <= i + by < 16]
    return lax.ppermute(array, ("x", "z"), pairs)


def by_rows(array, by):
    pairs = [(i, i + by) for i in range(8) if 0 <= i + by < 8]
    return lax.ppermute(array, ("y", "c"), pairs)


def summed(own, send):
    got = to_core(send)
    (wide,) = on_chip(halves_body, [shape((16, 216, 128), BF16)], "halves")(own, got)
    (thin,) = on_chip(
        second_body, [shape((4, 56, 128), F32)], "second", scratch=[pltpu.VMEM((224, 128), F32)]
    )(exchanged(wide, ("x", "y")))
    (thin,) = on_chip(third_body, [shape((4, 56, 128), F32)], "third")(exchanged(thin, "z"))
    (wide,) = on_chip(
        fourth_body, [shape((16, 216, 128), BF16)], "fourth", scratch=[pltpu.VMEM((224, 128), F32)]
    )(exchanged(thin, "z"))
    half = exchanged(wide, ("x", "y")).reshape(3456, 128)
    return half, to_core(half)


def on_device(clip_frames, enc_weight, dec_weight, out_grad):
    seg = lax.axis_index("segment")
    core = lax.axis_index("c")

    above = by_rows(clip_frames[:, 7:8], 1)
    lat1, part, own0, tail, taps = on_chip(
        encode_body,
        [
            shape((4, 64, 256), BF16),
            shape((4, 64, 256), PART),
            shape((4, 64, 256), F32),
            shape((2, 9, 128, 128), BF16),
            shape((4, 9, 64, 384), BF16),
        ],
        "encode",
        scratch=[pltpu.VMEM((136, 128), F32)],
        grant=16,
    )(clip_frames, above, enc_weight)
    part = by_frames(part, 1)
    latent = jnp.stack([(own0 + part.astype(F32)).astype(BF16), lat1])
    top = by_rows(latent[:, 3:4], 1)
    bottom = by_rows(latent[:, 0:1], -1)
    own, part, wide = on_chip(
        decode_body,
        [
            shape((2, 4, 64, 128), F32),
            shape((2, 4, 64, 128), PART),
            shape((2, 6, 64, 768), BF16),
        ],
        "decode",
        grant=12,
    )(latent, top, bottom, dec_weight)
    part = by_frames(part, 1)
    tail, _ = lax.optimization_barrier((tail, part))
    tail = lax.ppermute(tail, ("segment", "x", "z"), [(16 + t - 1, t) for t in range(1, 16)])
    (slope,) = on_chip(slope_body, [shape((2, 4, 64, 128), BF16)], "slope")(own, part, out_grad)
    top = by_rows(slope[:, 3:4], 1)
    bottom = by_rows(slope[:, 0:1], -1)
    slope = jnp.concatenate([top, slope, bottom], axis=1)
    later = by_frames(slope, -1)
    lat_grad, own, send = on_chip(
        grads_body,
        [
            shape((2, 4, 64, 256), BF16),
            shape((3456, 128), F32),
            shape((3456, 128), BF16),
        ],
        "grads",
        1,
        [
            pltpu.VMEM((6912, 128), F32),
            pltpu.VMEM((4, 6, 64, 384), BF16),
            pltpu.VMEM((2, 9, 64, 384), BF16),
            pltpu.VMEM((136, 128), F32),
        ],
        24,
    )(jnp.stack([seg, core]), slope, later, dec_weight, taps, tail, wide)
    latent_pair = jnp.where(seg == 0, lat_grad, latent)[None]
    half, other = summed(own, send)
    whole = jnp.where(core == 0, jnp.stack([half, other]), jnp.stack([other, half]))
    weight_grads = whole.reshape(27, 32768).astype(F32) * (1.0 / math.sqrt(32 * 32 * 64))
    return latent_pair, weight_grads[None]


def solution(mesh):
    fine = Mesh(mesh.devices.reshape(2, 4, 4, 4, 2), ("segment", "x", "z", "y", "c"))
    cells = P(("x", "z"), ("y", "c"), None, None)
    return jax.shard_map(
        on_device,
        mesh=fine,
        in_specs=(cells, P(), P(), cells),
        out_specs=(P("segment", ("x", "z"), ("y", "c"), None, None), P("segment", None, None)),
        check_vma=False,
    )
```

time: 229 us -> 149 us (0.65)
  starting transfers between devices: 126 us -> 38.5 us
  blocking collectives: 0 us -> 63.3 us
  waiting for transfers between devices: 51.6 us -> 25.4 us
  Pallas kernels: 31.4 us -> 10 us
  local copies, waits for them, and re-layouts: 10.2 us -> 5.95 us
  other arithmetic: 6.62 us -> 3.81 us
    ppermute x51 -> x11, starting transfers between devices: 126 us -> 38.5 us  [the longest x5 17.6 us: by_rows(): return lax.ppermute(array, ('y', 'c'), pairs)]
    all_to_all x0 -> x4, blocking collectives: none -> 63.3 us  [exchanged(): return lax.all_to_all(array, axes, 0, 0, tiled=True)]
    ppermute x51 -> x11, waiting for transfers between devices: 51.6 us -> 25.4 us  [the longest x3 15.2 us: by_frames(): return lax.ppermute(array, ('x', 'z'), pairs)]
    pallas_call x10 -> x8, Pallas kernels: 31.4 us -> 10 us  [call(): pl.pallas_call(body, out_shape=outs, in_specs=specs, out_specs=[pl.BlockS...]
    slice x6 -> x2, local copies, waits for them, and re-layouts: 3.37 us -> 0.93 us  [the longest x1 0.92 us: on_device(): above = by_rows(clip_frames[:, 7:8], 1)]
    unnamed x110 -> x24, local copies, waits for them, and re-layouts: 6.82 us -> 5.02 us
  transfers between devices with their start and end apart: 51 -> 11, of which waited for: 26 -> 8; matrix products, arithmetic and copies ran while one was open for 2% -> 1% of each run, Pallas kernels for 2% -> 0%
where the time goes in v2:
time: 149 us; the launch traced here: 148 us
  blocking collectives  63.3 us (42%)
  starting transfers between devices  38.5 us (26%)
  waiting for transfers between devices  25.4 us (17%)
  Pallas kernels  10 us (7%)
  local copies, waits for them, and re-layouts  5.95 us (4%)
  other arithmetic  3.81 us (3%)
    all_to_all x4, blocking collectives, exchanged(): return lax.all_to_all(array, axes, 0, 0, tiled=True)  63.3 us
    ppermute x5, starting transfers between devices, by_rows(): return lax.ppermute(array, ('y', 'c'), pairs)  17.6 us
    ppermute x3, waiting for transfers between devices, by_frames(): return lax.ppermute(array, ('x', 'z'), pairs)  15.2 us
    ppermute x3, starting transfers between devices, by_frames(): return lax.ppermute(array, ('x', 'z'), pairs)  13.9 us
    pallas_call x8, Pallas kernels, call(): pl.pallas_call(body, out_shape=outs, in_specs=specs, out_specs=[pl.BlockS...  10 us
    ppermute x5, waiting for transfers between devices, by_rows(): return lax.ppermute(array, ('y', 'c'), pairs)  6.48 us
    ppermute x2, starting transfers between devices, to_core(): return lax.ppermute(array, 'c', [(0, 1), (1, 0)])  5.49 us
    unnamed x24, local copies, waits for them, and re-layouts  5.02 us
  transfers between devices with their start and end apart: 11, of which 8 were waited for; matrix products, arithmetic and copies ran while one was open for 1% of the time, Pallas kernels for 0%

profile of v2, /device:TPU:1, one launch (start us, length us, event | category | flops | bytes accessed | tf_op | source)
XLA Modules:
  0.0 147.9 jit_solution(3678296426161877507)
XLA Ops:
  0.6 0.9 slice.15
  1.6 4.7 %collective-permute-start = (bf16[4,1,128,128]{3,2,1,0:T(8,128)(2,1)S(1)}, bf16[4,1,128,128]{3,2,1,0:T(8,128)(2,1)S(1)}, u32[]{:S(2)}, u32[]{:S(2)}) collective-permute-start(bf16[4,1,128,128]{3,2,1,0:T(8,128)(2,1)S(1)} %slice.15), channel_id=1, source_target_pairs={{0,1},{1,2},{2,3},{3,4},{4,5},{5,6},{6,7},{8,9},{9,10},{10,11},{11... | collective-permute-start | bytes 393224 | tf_op jit(solution)/shard_map/ppermute | solution.py:235
  6.3 1.9 %collective-permute-done.top = bf16[4,1,128,128]{3,2,1,0:T(8,128)(2,1)S(1)} collective-permute-done((bf16[4,1,128,128]{3,2,1,0:T(8,128)(2,1)S(1)}, bf16[4,1,128,128]{3,2,1,0:T(8,128)(2,1)S(1)}, u32[]{:S(2)}, u32[]{:S(2)}) %collective-permute-start) | collective-permute-done | bytes 131104 | tf_op jit(solution)/shard_map/ppermute | solution.py:235
  8.2 1.5 copy-done.1
  9.7 1.2 copy-done.2
  10.9 2.8 %encode.1 = (bf16[4,64,256]{2,1,0:T(8,128)(2,1)S(1)}, bf16[4,64,256]{2,1,0:T(8,128)(2,1)S(1)}, f32[4,64,256]{2,1,0:T(8,128)S(1)}, bf16[2,9,128,128]{3,2,1,0:T(8,128)(2,1)}, bf16[4,9,64,384]{3,2,1,0:T(8,128)(2,1)S(1)}) custom-call(bf16[4,8,128,128]{3,2,1,0:T(8,128)(2,1)S(1)} %copy-done.2, bf16[4,1,128,128]{3,2,1,0:T(8,128)(2,1)S(1)} %collective-permute-done.top, ...), custom_call_target="tpu_custom_call" | custom-call | tf_op jit(solution)/shard_map/encode/pallas_call | solution.py:24
  13.7 4.9 %collective-permute-start.1 = (bf16[4,64,256]{2,1,0:T(8,128)(2,1)S(1)}, bf16[4,64,256]{2,1,0:T(8,128)(2,1)S(1)}, u32[]{:S(2)}, u32[]{:S(2)}) collective-permute-start(bf16[4,64,256]{2,1,0:T(8,128)(2,1)S(1)} %get-tuple-element.15), channel_id=1, source_target_pairs={{0,8},{8,16},{16,24},{24,32},{32,40},{40,48},{48,56},{56,64},{64,7... | collective-permute-start | bytes 393224 | tf_op jit(solution)/shard_map/ppermute | solution.py:230
  18.6 2.4 %collective-permute-done.1 = bf16[4,64,256]{2,1,0:T(8,128)(2,1)S(1)} collective-permute-done((bf16[4,64,256]{2,1,0:T(8,128)(2,1)S(1)}, bf16[4,64,256]{2,1,0:T(8,128)(2,1)S(1)}, u32[]{:S(2)}, u32[]{:S(2)}) %collective-permute-start.1) | collective-permute-done | bytes 131104 | tf_op jit(solution)/shard_map/ppermute | solution.py:230
  21.1 2.1 %collective-permute-start.3 = (bf16[2,1,64,256]{3,2,1,0:T(8,128)(2,1)S(1)}, bf16[2,1,64,256]{3,2,1,0:T(8,128)(2,1)S(1)}, u32[]{:S(2)}, u32[]{:S(2)}) collective-permute-start(bf16[2,1,64,256]{3,2,1,0:T(8,128)(2,1)S(1)} %get-tuple-element.26), channel_id=1, source_target_pairs={{1,0},{2,1},{3,2},{4,3},{5,4},{6,5},{7,6},{9,8},{10,9},{11,10},{12... | collective-permute-start | bytes 196616 | tf_op jit(solution)/shard_map/ppermute | solution.py:235
  23.1 5.2 %collective-permute-start.2 = (bf16[2,1,64,256]{3,2,1,0:T(8,128)(2,1)S(1)}, bf16[2,1,64,256]{3,2,1,0:T(8,128)(2,1)S(1)}, u32[]{:S(2)}, u32[]{:S(2)}) collective-permute-start(bf16[2,1,64,256]{3,2,1,0:T(8,128)(2,1)S(1)} %get-tuple-element.27), channel_id=1, source_target_pairs={{0,1},{1,2},{2,3},{3,4},{4,5},{5,6},{6,7},{8,9},{9,10},{10,11},{11... | collective-permute-start | bytes 196616 | tf_op jit(solution)/shard_map/ppermute | solution.py:235
  28.4 1.3 collective-permute-done.2.top
  29.7 2.2 %decode.1 = (f32[2,4,64,128]{3,2,1,0:T(8,128)S(1)}, bf16[2,4,64,128]{3,2,1,0:T(8,128)(2,1)S(1)}, bf16[2,6,64,768]{3,2,1,0:T(8,128)(2,1)S(1)}) custom-call(bf16[2,4,64,256]{3,2,1,0:T(8,128)(2,1)S(1)} %pad_maximum_fusion.lat, bf16[2,1,64,256]{3,2,1,0:T(8,128)(2,1)S(1)} %collective-permute-done.2.top, ...), custom_call_target="tpu_custom_call" | custom-call | tf_op jit(solution)/shard_map/decode/pallas_call | solution.py:24
  31.9 1.0 copy-done.5
  32.9 7.7 %collective-permute-start.4 = (bf16[2,4,64,128]{3,2,1,0:T(8,128)(2,1)S(1)}, bf16[2,4,64,128]{3,2,1,0:T(8,128)(2,1)S(1)}, u32[]{:S(2)}, u32[]{:S(2)}) collective-permute-start(bf16[2,4,64,128]{3,2,1,0:T(8,128)(2,1)S(1)} %get-tuple-element.18), channel_id=1, source_target_pairs={{0,8},{8,16},{16,24},{24,32},{32,40},{40,48},{48,56},{56,64},{64,7... | collective-permute-start | bytes 393224 | tf_op jit(solution)/shard_map/ppermute | solution.py:230
  40.6 3.3 %collective-permute-done.4.part = bf16[2,4,64,128]{3,2,1,0:T(8,128)(2,1)S(1)} collective-permute-done((bf16[2,4,64,128]{3,2,1,0:T(8,128)(2,1)S(1)}, bf16[2,4,64,128]{3,2,1,0:T(8,128)(2,1)S(1)}, u32[]{:S(2)}, u32[]{:S(2)}) %collective-permute-start.4) | collective-permute-done | bytes 131104 | tf_op jit(solution)/shard_map/ppermute | solution.py:230
  43.9 1.5 %collective-permute-start.8 = (bf16[2,9,128,128]{3,2,1,0:T(8,128)(2,1)}, bf16[2,9,128,128]{3,2,1,0:T(8,128)(2,1)}, u32[]{:S(2)}, u32[]{:S(2)}) collective-permute-start(bf16[2,9,128,128]{3,2,1,0:T(8,128)(2,1)} %get-tuple-element.21), channel_id=1, source_target_pairs={{128,8},{136,16},{144,24},{152,32},{160,40},{168,48},{176,56},{184... | collective-permute-start | bytes 1769480 | tf_op jit(solution)/shard_map/ppermute | solution.py:286
  45.5 3.8 %collective-permute-start.5 = (bf16[2,1,64,128]{3,2,1,0:T(8,128)(2,1)S(1)}, bf16[2,1,64,128]{3,2,1,0:T(8,128)(2,1)S(1)}, u32[]{:S(2)}, u32[]{:S(2)}) collective-permute-start(bf16[2,1,64,128]{3,2,1,0:T(8,128)(2,1)S(1)} %get-tuple-element.28), channel_id=1, source_target_pairs={{0,1},{1,2},{2,3},{3,4},{4,5},{5,6},{6,7},{8,9},{9,10},{10,11},{11... | collective-permute-start | bytes 98312 | tf_op jit(solution)/shard_map/ppermute | solution.py:235
  49.3 1.9 %collective-permute-start.6 = (bf16[2,1,64,128]{3,2,1,0:T(8,128)(2,1)S(1)}, bf16[2,1,64,128]{3,2,1,0:T(8,128)(2,1)S(1)}, u32[]{:S(2)}, u32[]{:S(2)}) collective-permute-start(bf16[2,1,64,128]{3,2,1,0:T(8,128)(2,1)S(1)} %get-tuple-element.29), channel_id=1, source_target_pairs={{1,0},{2,1},{3,2},{4,3},{5,4},{6,5},{7,6},{9,8},{10,9},{11,10},{12... | collective-permute-start | bytes 98312 | tf_op jit(solution)/shard_map/ppermute | solution.py:235
  51.2 3.3 %collective-permute-done.6 = bf16[2,1,64,128]{3,2,1,0:T(8,128)(2,1)S(1)} collective-permute-done((bf16[2,1,64,128]{3,2,1,0:T(8,128)(2,1)S(1)}, bf16[2,1,64,128]{3,2,1,0:T(8,128)(2,1)S(1)}, u32[]{:S(2)}, u32[]{:S(2)}) %collective-permute-start.6) | collective-permute-done | bytes 32800 | tf_op jit(solution)/shard_map/ppermute | solution.py:235
  55.2 1.3 collective-permute-start.7
  56.6 9.5 %collective-permute-done.7.later = bf16[2,6,64,128]{3,2,1,0:T(8,128)(2,1)} collective-permute-done((bf16[2,6,64,128]{3,2,1,0:T(8,128)(2,1)}, bf16[2,6,64,128]{3,2,1,0:T(8,128)(2,1)}, u32[]{:S(2)}, u32[]{:S(2)}) %collective-permute-start.7) | collective-permute-done | bytes 196640 | tf_op jit(solution)/shard_map/ppermute | solution.py:230
  66.0 1.3 copy-done.6
  67.3 4.6 %grads.1 = (bf16[2,4,64,256]{3,2,1,0:T(8,128)(2,1)S(1)}, f32[3456,128]{1,0:T(8,128)S(1)}, bf16[3456,128]{1,0:T(8,128)(2,1)S(1)}) custom-call(s32[2]{0:T(128)S(1)} %pad_add_fusion.where, bf16[2,6,64,128]{3,2,1,0:T(8,128)(2,1)} %pad_maximum_fusion.1.slope, bf16[2,6,64,128]{3,2,1,0:T(8,128)(2,1)} %collective-permute-done.7.later, ...), custom_call_target="tpu_custom_call" | custom-call | tf_op jit(solution)/shard_map/grads/pallas_call | solution.py:24
  72.0 2.4 %collective-permute-done.9.got = bf16[3456,128]{1,0:T(8,128)(2,1)S(1)} collective-permute-done((bf16[3456,128]{1,0:T(8,128)(2,1)S(1)}, bf16[3456,128]{1,0:T(8,128)(2,1)S(1)}, u32[]{:S(2)}, u32[]{:S(2)}) %collective-permute-start.9) | collective-permute-done | bytes 884768 | tf_op jit(solution)/shard_map/ppermute | solution.py:225
  74.7 28.8 %all_to_all.20.got = bf16[16,216,128]{2,1,0:T(8,128)(2,1)S(1)} all-to-all(bf16[16,216,128]{2,1,0:T(8,128)(2,1)S(1)} %halves.1), channel_id=1, replica_groups=mesh['segment'=2,'x'=4,'z'=4,'y'=4,'c'=2] {'x','y'}, dimensions={0} | all-to-all | bytes 1769472 | tf_op jit(solution)/shard_map/all_to_all | solution.py:221
  103.6 10.0 %all_to_all.21.got = f32[4,56,128]{2,1,0:T(8,128)S(1)} all-to-all(f32[4,56,128]{2,1,0:T(8,128)S(1)} %second.1), channel_id=1, replica_groups=mesh['segment'=2,'x'=4,'z'=4,'y'=4,'c'=2] {'z'}, dimensions={0} | all-to-all | bytes 229376 | tf_op jit(solution)/shard_map/all_to_all | solution.py:221
  113.6 9.8 %all_to_all.22.got = f32[4,56,128]{2,1,0:T(8,128)S(1)} all-to-all(f32[4,56,128]{2,1,0:T(8,128)S(1)} %third.1), channel_id=1, replica_groups=mesh['segment'=2,'x'=4,'z'=4,'y'=4,'c'=2] {'z'}, dimensions={0} | all-to-all | bytes 229376 | tf_op jit(solution)/shard_map/all_to_all | solution.py:221
  123.5 14.7 %all_to_all.23 = bf16[16,216,128]{2,1,0:T(8,128)(2,1)S(1)} all-to-all(bf16[16,216,128]{2,1,0:T(8,128)(2,1)S(1)} %fourth.1), channel_id=1, replica_groups=mesh['segment'=2,'x'=4,'z'=4,'y'=4,'c'=2] {'x','y'}, dimensions={0} | all-to-all | bytes 1769472 | tf_op jit(solution)/shard_map/all_to_all | solution.py:221
  138.2 5.4 %collective-permute-start.10 = (bf16[3456,128]{1,0:T(8,128)(2,1)S(1)}, bf16[3456,128]{1,0:T(8,128)(2,1)S(1)}, u32[]{:S(2)}, u32[]{:S(2)}) collective-permute-start(bf16[3456,128]{1,0:T(8,128)(2,1)S(1)} %bitcast.15), channel_id=1, source_target_pairs={{0,1},{1,0},{2,3},{3,2},{4,5},{5,4},{6,7},{7,6},{8,9},{9,8},{10,11... | collective-permute-start | bytes 2654216 | tf_op jit(solution)/shard_map/ppermute | solution.py:225
  143.6 0.7 select_bitcast_fusion
  144.4 1.3 collective-permute-done.10
  145.7 2.2 %convert_multiply_fusion = f32[2,3456,128]{2,1,0:T(8,128)} fusion(bf16[1,3456,128]{2,1,0:T(8,128)(2,1)S(1)} %bitcast.17, bf16[1,3456,128]{2,1,0:T(8,128)(2,1)S(1)} %bitcast.16, pred[]{:T(512)S(6)} %eq.7), kind=kLoop, calls=%fused_computation | loop fusion | flops 4423680 | bytes 5308417 | tf_op jit(solution)/shard_map/mul | solution.py:312
  (35 shorter events, 1.5 us)
Async XLA Ops:
  1.6 28.1 %copy-start = (bf16[3,3,3,256,128]{4,3,2,1,0:T(8,128)(2,1)S(1)}, bf16[3,3,3,256,128]{4,3,2,1,0:T(8,128)(2,1)}, u32[]{:S(2)}) copy-start(bf16[3,3,3,256,128]{4,3,2,1,0:T(8,128)(2,1)} %weight.5) | copy-start | bytes 5308420
  1.6 6.6 %collective-permute-start = (bf16[4,1,128,128]{3,2,1,0:T(8,128)(2,1)S(1)}, bf16[4,1,128,128]{3,2,1,0:T(8,128)(2,1)S(1)}, u32[]{:S(2)}, u32[]{:S(2)}) collective-permute-start(bf16[4,1,128,128]{3,2,1,0:T(8,128)(2,1)S(1)} %slice.15), channel_id=1, source_target_pairs={{0,1},{1,2},{2,3},{3,4},{4,5},{5,6},{6,7},{8,9},{9,10},{10,11},{11... | collective-permute-start | bytes 393224 | tf_op jit(solution)/shard_map/ppermute | solution.py:235
  8.2 1.5 copy-start.1
  9.7 1.2 copy-start.2
  13.7 18.2 %copy-start.3 = (bf16[4,64,256]{2,1,0:T(8,128)(2,1)}, bf16[4,64,256]{2,1,0:T(8,128)(2,1)S(1)}, u32[]{:S(2)}) copy-start(bf16[4,64,256]{2,1,0:T(8,128)(2,1)S(1)} %get-tuple-element.16) | copy-start | bytes 393220
  13.7 7.3 %collective-permute-start.1 = (bf16[4,64,256]{2,1,0:T(8,128)(2,1)S(1)}, bf16[4,64,256]{2,1,0:T(8,128)(2,1)S(1)}, u32[]{:S(2)}, u32[]{:S(2)}) collective-permute-start(bf16[4,64,256]{2,1,0:T(8,128)(2,1)S(1)} %get-tuple-element.15), channel_id=1, source_target_pairs={{0,8},{8,16},{16,24},{24,32},{32,40},{40,48},{48,56},{56,64},{64,7... | collective-permute-start | bytes 393224 | tf_op jit(solution)/shard_map/ppermute | solution.py:230
  21.0 24.4 %copy-start.9 = (bf16[2,4,64,128]{3,2,1,0:T(8,128)(2,1)S(1)}, bf16[2,4,64,128]{3,2,1,0:T(8,128)(2,1)}, u32[]{:S(2)}) copy-start(bf16[2,4,64,128]{3,2,1,0:T(8,128)(2,1)} %cot.1) | copy-start | bytes 393220
  21.0 7.4 %copy-start.10 = (bf16[1,4,64,256]{3,2,1,0:T(8,128)(2,1)}, bf16[1,4,64,256]{3,2,1,0:T(8,128)(2,1)S(1)}, u32[]{:S(2)}) copy-start(bf16[1,4,64,256]{3,2,1,0:T(8,128)(2,1)S(1)} %fusion) | copy-start | bytes 393220
  21.1 7.3 %collective-permute-start.3 = (bf16[2,1,64,256]{3,2,1,0:T(8,128)(2,1)S(1)}, bf16[2,1,64,256]{3,2,1,0:T(8,128)(2,1)S(1)}, u32[]{:S(2)}, u32[]{:S(2)}) collective-permute-start(bf16[2,1,64,256]{3,2,1,0:T(8,128)(2,1)S(1)} %get-tuple-element.26), channel_id=1, source_target_pairs={{1,0},{2,1},{3,2},{4,3},{5,4},{6,5},{7,6},{9,8},{10,9},{11,10},{12... | collective-permute-start | bytes 196616 | tf_op jit(solution)/shard_map/ppermute | solution.py:235
  23.1 6.5 %collective-permute-start.2 = (bf16[2,1,64,256]{3,2,1,0:T(8,128)(2,1)S(1)}, bf16[2,1,64,256]{3,2,1,0:T(8,128)(2,1)S(1)}, u32[]{:S(2)}, u32[]{:S(2)}) collective-permute-start(bf16[2,1,64,256]{3,2,1,0:T(8,128)(2,1)S(1)} %get-tuple-element.27), channel_id=1, source_target_pairs={{0,1},{1,2},{2,3},{3,4},{4,5},{5,6},{6,7},{8,9},{9,10},{10,11},{11... | collective-permute-start | bytes 196616 | tf_op jit(solution)/shard_map/ppermute | solution.py:235
  31.9 1.0 copy-start.5
  32.9 11.0 %collective-permute-start.4 = (bf16[2,4,64,128]{3,2,1,0:T(8,128)(2,1)S(1)}, bf16[2,4,64,128]{3,2,1,0:T(8,128)(2,1)S(1)}, u32[]{:S(2)}, u32[]{:S(2)}) collective-permute-start(bf16[2,4,64,128]{3,2,1,0:T(8,128)(2,1)S(1)} %get-tuple-element.18), channel_id=1, source_target_pairs={{0,8},{8,16},{16,24},{24,32},{32,40},{40,48},{48,56},{56,64},{64,7... | collective-permute-start | bytes 393224 | tf_op jit(solution)/shard_map/ppermute | solution.py:230
  43.9 22.1 %collective-permute-start.8 = (bf16[2,9,128,128]{3,2,1,0:T(8,128)(2,1)}, bf16[2,9,128,128]{3,2,1,0:T(8,128)(2,1)}, u32[]{:S(2)}, u32[]{:S(2)}) collective-permute-start(bf16[2,9,128,128]{3,2,1,0:T(8,128)(2,1)} %get-tuple-element.21), channel_id=1, source_target_pairs={{128,8},{136,16},{144,24},{152,32},{160,40},{168,48},{176,56},{184... | collective-permute-start | bytes 1769480 | tf_op jit(solution)/shard_map/ppermute | solution.py:286
  45.5 5.7 %collective-permute-start.5 = (bf16[2,1,64,128]{3,2,1,0:T(8,128)(2,1)S(1)}, bf16[2,1,64,128]{3,2,1,0:T(8,128)(2,1)S(1)}, u32[]{:S(2)}, u32[]{:S(2)}) collective-permute-start(bf16[2,1,64,128]{3,2,1,0:T(8,128)(2,1)S(1)} %get-tuple-element.28), channel_id=1, source_target_pairs={{0,1},{1,2},{2,3},{3,4},{4,5},{5,6},{6,7},{8,9},{9,10},{10,11},{11... | collective-permute-start | bytes 98312 | tf_op jit(solution)/shard_map/ppermute | solution.py:235
  49.3 5.2 %collective-permute-start.6 = (bf16[2,1,64,128]{3,2,1,0:T(8,128)(2,1)S(1)}, bf16[2,1,64,128]{3,2,1,0:T(8,128)(2,1)S(1)}, u32[]{:S(2)}, u32[]{:S(2)}) collective-permute-start(bf16[2,1,64,128]{3,2,1,0:T(8,128)(2,1)S(1)} %get-tuple-element.29), channel_id=1, source_target_pairs={{1,0},{2,1},{3,2},{4,3},{5,4},{6,5},{7,6},{9,8},{10,9},{11,10},{12... | collective-permute-start | bytes 98312 | tf_op jit(solution)/shard_map/ppermute | solution.py:235
  55.2 10.8 %collective-permute-start.7 = (bf16[2,6,64,128]{3,2,1,0:T(8,128)(2,1)}, bf16[2,6,64,128]{3,2,1,0:T(8,128)(2,1)}, u32[]{:S(2)}, u32[]{:S(2)}) collective-permute-start(bf16[2,6,64,128]{3,2,1,0:T(8,128)(2,1)} %pad_maximum_fusion.1.slope), channel_id=1, source_target_pairs={{8,0},{16,8},{24,16},{32,24},{40,32},{48,40},{56,48},{64,56},{72,6... | collective-permute-start | bytes 589832 | tf_op jit(solution)/shard_map/ppermute | solution.py:230
  66.0 1.3 copy-start.6
  71.9 2.7 %copy-start.7 = (bf16[2,4,64,256]{3,2,1,0:T(8,128)(2,1)}, bf16[2,4,64,256]{3,2,1,0:T(8,128)(2,1)S(1)}, u32[]{:S(2)}) copy-start(bf16[2,4,64,256]{3,2,1,0:T(8,128)(2,1)S(1)} %get-tuple-element.23) | copy-start | bytes 786436
  71.9 2.5 %collective-permute-start.9 = (bf16[3456,128]{1,0:T(8,128)(2,1)S(1)}, bf16[3456,128]{1,0:T(8,128)(2,1)S(1)}, u32[]{:S(2)}, u32[]{:S(2)}) collective-permute-start(bf16[3456,128]{1,0:T(8,128)(2,1)S(1)} %get-tuple-element.25), channel_id=1, source_target_pairs={{0,1},{1,0},{2,3},{3,2},{4,5},{5,4},{6,7},{7,6},{8,9},{9,8},{10,11... | collective-permute-start | bytes 2654216 | tf_op jit(solution)/shard_map/ppermute | solution.py:225
  103.6 40.1 %copy-start.4 = (bf16[4,64,256]{2,1,0:T(8,128)(2,1)S(1)}, bf16[4,64,256]{2,1,0:T(8,128)(2,1)}, u32[]{:S(2)}) copy-start(bf16[4,64,256]{2,1,0:T(8,128)(2,1)} %copy-done.3) | copy-start | bytes 393220
  103.6 40.1 %copy-start.8 = (bf16[2,4,64,256]{3,2,1,0:T(8,128)(2,1)S(1)}, bf16[2,4,64,256]{3,2,1,0:T(8,128)(2,1)}, u32[]{:S(2)}) copy-start(bf16[2,4,64,256]{3,2,1,0:T(8,128)(2,1)} %copy-done.7) | copy-start | bytes 786436
  103.6 40.0 %copy-start.11 = (bf16[1,4,64,256]{3,2,1,0:T(8,128)(2,1)S(1)}, bf16[1,4,64,256]{3,2,1,0:T(8,128)(2,1)}, u32[]{:S(2)}) copy-start(bf16[1,4,64,256]{3,2,1,0:T(8,128)(2,1)} %copy-done.10) | copy-start | bytes 393220
  138.2 7.5 %collective-permute-start.10 = (bf16[3456,128]{1,0:T(8,128)(2,1)S(1)}, bf16[3456,128]{1,0:T(8,128)(2,1)S(1)}, u32[]{:S(2)}, u32[]{:S(2)}) collective-permute-start(bf16[3456,128]{1,0:T(8,128)(2,1)S(1)} %bitcast.15), channel_id=1, source_target_pairs={{0,1},{1,0},{2,3},{3,2},{4,5},{5,4},{6,7},{7,6},{8,9},{9,8},{10,11... | collective-permute-start | bytes 2654216 | tf_op jit(solution)/shard_map/ppermute | solution.py:225

commit v3 on v2

--- a/solution.py
+++ b/solution.py
@@ -79,7 +79,7 @@
     return jnp.concatenate([taps[f, 2 * h + b] for h in range(4)], axis=0)
 
 
-def encode_body(clip, top, weight, lat1, part, own0, tail, taps, stage):
+def encode_body(clip, top, weight, cot, lat1, part, own0, tail, cot_down, cot_up, taps, stage):
     fill_clip(stage, clip, top, taps, 4)
 
     def conv(f, a):
@@ -94,44 +94,64 @@
     own0[...] = conv(0, 2).reshape(4, 64, 256)
     tail[:, 0:1] = top[2:4]
     tail[:, 1:9] = clip[2:4]
+    cot_down[...] = cot[:, 3:4]
+    cot_up[...] = cot[:, 0:1]
+
+
+def join_body(own0, part, lat1, lat, down, up):
+    lat[0] = (own0[...] + part[...].astype(F32)).astype(BF16)
+    lat[1] = lat1[...]
+    down[...] = lat[:, 2:4]
+    up[...] = lat[:, 0:2]
+
+
+def fill_latent(lat, top, bottom, wide):
+    for f in range(2):
+        for r in range(2):
+            wide[f, r] = jnp.concatenate(neighbour_cols(top[f, r]), axis=1)
+            wide[f, 6 + r] = jnp.concatenate(neighbour_cols(bottom[f, r]), axis=1)
+
+        def one(r, carry, f=f):
+            wide[f, r + 2] = jnp.concatenate(neighbour_cols(lat[f, r]), axis=1)
+            return carry
+
+        lax.fori_loop(0, 4, one, 0)
 
 
 def decode_body(lat, top, bottom, weight, own, part, wide):
-    for f in range(2):
-        wide[f, 0] = jnp.concatenate(neighbour_cols(top[f, 0]), axis=1)
-        wide[f, 5] = jnp.concatenate(neighbour_cols(bottom[f, 0]), axis=1)
-
-        def one(r, carry, f=f):
-            wide[f, r + 1] = jnp.concatenate(neighbour_cols(lat[f, r]), axis=1)
-            return carry
-
-        lax.fori_loop(0, 4, one, 0)
+    fill_latent(lat, top, bottom, wide)
 
     def conv(f, a):
         total = None
         for b in range(3):
-            window = wide[f, b : b + 4].reshape(256, 768)
+            window = wide[f, b : b + 6].reshape(384, 768)
             term = dot(window, weight[a, b].reshape(768, 128))
             total = term if total is None else total + term
         return total
 
-    part[0] = (conv(0, 0) + conv(1, 1)).astype(part.dtype).reshape(4, 64, 128)
-    part[1] = conv(1, 0).astype(part.dtype).reshape(4, 64, 128)
-    own[0] = conv(0, 2).reshape(4, 64, 128)
-    own[1] = (conv(0, 1) + conv(1, 2)).reshape(4, 64, 128)
-
-
-def slope_body(own, part, cot, slope):
-    pre = own[...] + part[...].astype(F32)
-    sigm = jax.nn.sigmoid(pre)
-    slope[...] = (cot[...].astype(F32) * sigm * (1.0 + pre * (1.0 - sigm))).astype(BF16)
+    part[0] = (conv(0, 0) + conv(1, 1)).astype(part.dtype).reshape(6, 64, 128)
+    part[1] = conv(1, 0).astype(part.dtype).reshape(6, 64, 128)
+    own[0] = conv(0, 2).reshape(6, 64, 128)
+    own[1] = (conv(0, 1) + conv(1, 2)).reshape(6, 64, 128)
+
+
+def slope_body(own, part, cot, top, bottom, slope):
+    def rows(at, grad):
+        pre = own[:, at] + part[:, at].astype(F32)
+        sigm = jax.nn.sigmoid(pre)
+        slope[:, at] = (grad.astype(F32) * sigm * (1.0 + pre * (1.0 - sigm))).astype(BF16)
+
+    rows(slice(0, 1), top[...])
+    rows(slice(1, 5), cot[...])
+    rows(slice(5, 6), bottom[...])
 
 
 def grads_body(
-    where, slope, later, weight, taps, tail, wide, lat_grad, own, send, gathered, rim, btaps, stage
+    seg_at, core_at, slope, later, weight, taps, tail, lat, top, bottom,
+    lat_grad, own, send, gathered, rim, btaps, wide, stage,
 ):
-    seg = where[0]
-    core = where[1]
+    seg = seg_at[0]
+    core = core_at[0]
 
     @pl.when(seg == 0)
     def _():
@@ -171,13 +191,14 @@
     @pl.when(seg != 0)
     def _():
         lat_grad[...] = jnp.zeros(lat_grad.shape, BF16)
+        fill_latent(lat, top, bottom, wide)
         for a in range(3):
             for b in range(3):
                 total = None
                 for f in range(2):
                     t = f + 2 - a
                     cells = (slope if t < 2 else later)[t % 2, 1:5].reshape(256, 128)
-                    term = dot_tn(wide[f, b : b + 4].reshape(256, 768), cells)
+                    term = dot_tn(wide[f, b + 1 : b + 5].reshape(256, 768), cells)
                     total = term if total is None else total + term
                 start = (a * 3 + b) * 768
                 gathered[start : start + 768, :] = total
@@ -193,28 +214,20 @@
         spread[j] = (own[rows, :] + got[rows, :].astype(F32)).astype(BF16)
 
 
-def second_body(got, spread, held):
+def second_body(got, spread):
     total = got[0].astype(F32)
     for j in range(1, 16):
         total = total + got[j].astype(F32)
-    held[0:216, :] = total
-    held[216:224, :] = jnp.zeros((8, 128), F32)
     for j in range(4):
-        spread[j] = held[56 * j : 56 * (j + 1), :]
+        spread[j] = total.astype(BF16)
 
 
 def third_body(got, spread):
-    total = got[0] + got[1] + got[2] + got[3]
-    for j in range(4):
-        spread[j] = total
-
-
-def fourth_body(got, spread, held):
-    for j in range(4):
-        held[56 * j : 56 * (j + 1), :] = got[j]
-    total = held[0:216, :].astype(BF16)
+    total = got[0].astype(F32)
+    for j in range(1, 4):
+        total = total + got[j].astype(F32)
     for j in range(16):
-        spread[j] = total
+        spread[j] = total.astype(BF16)
 
 
 def exchanged(array, axes):
@@ -238,13 +251,10 @@
 def summed(own, send):
     got = to_core(send)
     (wide,) = on_chip(halves_body, [shape((16, 216, 128), BF16)], "halves")(own, got)
-    (thin,) = on_chip(
-        second_body, [shape((4, 56, 128), F32)], "second", scratch=[pltpu.VMEM((224, 128), F32)]
-    )(exchanged(wide, ("x", "y")))
-    (thin,) = on_chip(third_body, [shape((4, 56, 128), F32)], "third")(exchanged(thin, "z"))
-    (wide,) = on_chip(
-        fourth_body, [shape((16, 216, 128), BF16)], "fourth", scratch=[pltpu.VMEM((224, 128), F32)]
-    )(exchanged(thin, "z"))
+    (thin,) = on_chip(second_body, [shape((4, 216, 128), BF16)], "second")(
+        exchanged(wide, ("x", "y"))
+    )
+    (wide,) = on_chip(third_body, [shape((16, 216, 128), BF16)], "third")(exchanged(thin, "z"))
     half = exchanged(wide, ("x", "y")).reshape(3456, 128)
     return half, to_core(half)
 
@@ -254,40 +264,49 @@
     core = lax.axis_index("c")
 
     above = by_rows(clip_frames[:, 7:8], 1)
-    lat1, part, own0, tail, taps = on_chip(
+    lat1, part, own0, tail, cot_down, cot_up, taps = on_chip(
         encode_body,
         [
             shape((4, 64, 256), BF16),
             shape((4, 64, 256), PART),
             shape((4, 64, 256), F32),
             shape((2, 9, 128, 128), BF16),
+            shape((2, 1, 64, 128), BF16),
+            shape((2, 1, 64, 128), BF16),
             shape((4, 9, 64, 384), BF16),
         ],
         "encode",
         scratch=[pltpu.VMEM((136, 128), F32)],
         grant=16,
-    )(clip_frames, above, enc_weight)
+    )(clip_frames, above, enc_weight, out_grad)
     part = by_frames(part, 1)
-    latent = jnp.stack([(own0 + part.astype(F32)).astype(BF16), lat1])
-    top = by_rows(latent[:, 3:4], 1)
-    bottom = by_rows(latent[:, 0:1], -1)
-    own, part, wide = on_chip(
+    cot_top = by_rows(cot_down, 1)
+    cot_bottom = by_rows(cot_up, -1)
+    part, cot_top, cot_bottom = lax.optimization_barrier((part, cot_top, cot_bottom))
+    latent, down, up = on_chip(
+        join_body,
+        [
+            shape((2, 4, 64, 256), BF16),
+            shape((2, 2, 64, 256), BF16),
+            shape((2, 2, 64, 256), BF16),
+        ],
+        "join",
+    )(own0, part, lat1)
+    top = by_rows(down, 1)
+    bottom = by_rows(up, -1)
+    own, part = on_chip(
         decode_body,
-        [
-            shape((2, 4, 64, 128), F32),
-            shape((2, 4, 64, 128), PART),
-            shape((2, 6, 64, 768), BF16),
-        ],
+        [shape((2, 6, 64, 128), F32), shape((2, 6, 64, 128), PART)],
         "decode",
-        grant=12,
+        scratch=[pltpu.VMEM((2, 8, 64, 768), BF16)],
+        grant=14,
     )(latent, top, bottom, dec_weight)
     part = by_frames(part, 1)
     tail, _ = lax.optimization_barrier((tail, part))
     tail = lax.ppermute(tail, ("segment", "x", "z"), [(16 + t - 1, t) for t in range(1, 16)])
-    (slope,) = on_chip(slope_body, [shape((2, 4, 64, 128), BF16)], "slope")(own, part, out_grad)
-    top = by_rows(slope[:, 3:4], 1)
-    bottom = by_rows(slope[:, 0:1], -1)
-    slope = jnp.concatenate([top, slope, bottom], axis=1)
+    (slope,) = on_chip(slope_body, [shape((2, 6, 64, 128), BF16)], "slope")(
+        own, part, out_grad, cot_top, cot_bottom
+    )
     later = by_frames(slope, -1)
     lat_grad, own, send = on_chip(
         grads_body,
@@ -297,15 +316,16 @@
             shape((3456, 128), BF16),
         ],
         "grads",
-        1,
+        2,
         [
             pltpu.VMEM((6912, 128), F32),
             pltpu.VMEM((4, 6, 64, 384), BF16),
             pltpu.VMEM((2, 9, 64, 384), BF16),
+            pltpu.VMEM((2, 8, 64, 768), BF16),
             pltpu.VMEM((136, 128), F32),
         ],
-        24,
-    )(jnp.stack([seg, core]), slope, later, dec_weight, taps, tail, wide)
+        26,
+    )(seg.reshape(1), core.reshape(1), slope, later, dec_weight, taps, tail, latent, top, bottom)
     latent_pair = jnp.where(seg == 0, lat_grad, latent)[None]
     half, other = summed(own, send)
     whole = jnp.where(core == 0, jnp.stack([half, other]), jnp.stack([other, half]))

time: 149 us -> 139 us (0.933)
  starting transfers between devices: 38.5 us -> 33.6 us
  blocking collectives: 63.3 us -> 58.6 us
    all_to_all x4 -> x3, blocking collectives: 63.3 us -> 58.6 us  [exchanged(): return lax.all_to_all(array, axes, 0, 0, tiled=True)]
    ppermute x5, waiting for transfers between devices: 6.48 us -> 9.08 us  [by_rows(): return lax.ppermute(array, ('y', 'c'), pairs)]
    ppermute x5, starting transfers between devices: 17.6 us -> 15.6 us  [by_rows(): return lax.ppermute(array, ('y', 'c'), pairs)]
    ppermute x3, waiting for transfers between devices: 15.2 us -> 13.6 us  [by_frames(): return lax.ppermute(array, ('x', 'z'), pairs)]
    ppermute x3, starting transfers between devices: 13.9 us -> 12.3 us  [by_frames(): return lax.ppermute(array, ('x', 'z'), pairs)]
    unnamed x24 -> x12, local copies, waits for them, and re-layouts: 5.02 us -> 5.09 us
  transfers between devices with their start and end apart: 11 -> 11, of which waited for: 8 -> 7; matrix products, arithmetic and copies ran while one was open for 1% -> 1% of each run, Pallas kernels for 0% -> 0%
where the time goes in v3:
time: 139 us; the launch traced here: 138 us
  blocking collectives  58.6 us (42%)
  starting transfers between devices  33.6 us (24%)
  waiting for transfers between devices  26.4 us (19%)
  Pallas kernels  9.77 us (7%)
  local copies, waits for them, and re-layouts  6.01 us (4%)
  other arithmetic  2.96 us (2%)
    all_to_all x3, blocking collectives, exchanged(): return lax.all_to_all(array, axes, 0, 0, tiled=True)  58.6 us
    ppermute x5, starting transfers between devices, by_rows(): return lax.ppermute(array, ('y', 'c'), pairs)  15.6 us
    ppermute x3, waiting for transfers between devices, by_frames(): return lax.ppermute(array, ('x', 'z'), pairs)  13.6 us
    ppermute x3, starting transfers between devices, by_frames(): return lax.ppermute(array, ('x', 'z'), pairs)  12.3 us
    pallas_call x8, Pallas kernels, call(): pl.pallas_call(body, out_shape=outs, in_specs=specs, out_specs=[pl.BlockS...  9.77 us
    ppermute x5, waiting for transfers between devices, by_rows(): return lax.ppermute(array, ('y', 'c'), pairs)  9.08 us
    unnamed x12, local copies, waits for them, and re-layouts  5.09 us
    ppermute x2, starting transfers between devices, to_core(): return lax.ppermute(array, 'c', [(0, 1), (1, 0)])  4.99 us
  transfers between devices with their start and end apart: 11, of which 7 were waited for; matrix products, arithmetic and copies ran while one was open for 1% of the time, Pallas kernels for 0%

profile of v3, /device:TPU:1, one launch (start us, length us, event | category | flops | bytes accessed | tf_op | source)
XLA Modules:
  0.0 138.1 jit_solution(103233122517318000)
XLA Ops:
  0.6 0.9 slice.3
  1.6 4.7 %collective-permute-start = (bf16[4,1,128,128]{3,2,1,0:T(8,128)(2,1)S(1)}, bf16[4,1,128,128]{3,2,1,0:T(8,128)(2,1)S(1)}, u32[]{:S(2)}, u32[]{:S(2)}) collective-permute-start(bf16[4,1,128,128]{3,2,1,0:T(8,128)(2,1)S(1)} %slice.3), channel_id=1, source_target_pairs={{0,1},{1,2},{2,3},{3,4},{4,5},{5,6},{6,7},{8,9},{9,10},{10,11},{11... | collective-permute-start | bytes 393224 | tf_op jit(solution)/shard_map/ppermute | solution.py:248
  6.3 1.9 %collective-permute-done.top = bf16[4,1,128,128]{3,2,1,0:T(8,128)(2,1)S(1)} collective-permute-done((bf16[4,1,128,128]{3,2,1,0:T(8,128)(2,1)S(1)}, bf16[4,1,128,128]{3,2,1,0:T(8,128)(2,1)S(1)}, u32[]{:S(2)}, u32[]{:S(2)}) %collective-permute-start) | collective-permute-done | bytes 131104 | tf_op jit(solution)/shard_map/ppermute | solution.py:248
  8.2 1.5 %copy-done.1 = bf16[3,3,3,128,256]{4,3,2,1,0:T(8,128)(2,1)S(1)} copy-done((bf16[3,3,3,128,256]{4,3,2,1,0:T(8,128)(2,1)S(1)}, bf16[3,3,3,128,256]{4,3,2,1,0:T(8,128)(2,1)}, u32[]{:S(2)}) %copy-start.1) | copy-done | bytes 1769496
  9.7 1.2 copy-done.4
  10.9 0.9 copy-done.5
  11.8 2.8 %encode.1 = (bf16[4,64,256]{2,1,0:T(8,128)(2,1)S(1)}, bf16[4,64,256]{2,1,0:T(8,128)(2,1)S(1)}, f32[4,64,256]{2,1,0:T(8,128)S(1)}, bf16[2,9,128,128]{3,2,1,0:T(8,...) custom-call(bf16[4,8,128,128]{3,2,1,0:T(8,128)(2,1)S(1)} %copy-done., ...), custom_call_target="tpu_custom_call" | custom-call | tf_op jit(solution)/shard_map/encode/pallas_call | solution.py:24
  14.6 4.9 %collective-permute-start.1 = (bf16[4,64,256]{2,1,0:T(8,128)(2,1)S(1)}, bf16[4,64,256]{2,1,0:T(8,128)(2,1)S(1)}, u32[]{:S(2)}, u32[]{:S(2)}) collective-permute-start(bf16[4,64,256]{2,1,0:T(8,128)(2,1)S(1)} %get-tuple-element.22), channel_id=1, source_target_pairs={{0,8},{8,16},{16,24},{24,32},{32,40},{40,48},{48,56},{56,64},{64,7... | collective-permute-start | bytes 393224 | tf_op jit(solution)/shard_map/ppermute | solution.py:243
  19.5 4.6 %collective-permute-start.2 = (bf16[2,1,64,128]{3,2,1,0:T(8,128)(2,1)S(1)}, bf16[2,1,64,128]{3,2,1,0:T(8,128)(2,1)S(1)}, u32[]{:S(2)}, u32[]{:S(2)}) collective-permute-start(bf16[2,1,64,128]{3,2,1,0:T(8,128)(2,1)S(1)} %get-tuple-element.23), channel_id=1, source_target_pairs={{0,1},{1,2},{2,3},{3,4},{4,5},{5,6},{6,7},{8,9},{9,10},{10,11},{11... | collective-permute-start | bytes 98312 | tf_op jit(solution)/shard_map/ppermute | solution.py:248
  24.1 1.9 %collective-permute-start.3 = (bf16[2,1,64,128]{3,2,1,0:T(8,128)(2,1)S(1)}, bf16[2,1,64,128]{3,2,1,0:T(8,128)(2,1)S(1)}, u32[]{:S(2)}, u32[]{:S(2)}) collective-permute-start(bf16[2,1,64,128]{3,2,1,0:T(8,128)(2,1)S(1)} %get-tuple-element.24), channel_id=1, source_target_pairs={{1,0},{2,1},{3,2},{4,3},{5,4},{6,5},{7,6},{9,8},{10,9},{11,10},{12... | collective-permute-start | bytes 98312 | tf_op jit(solution)/shard_map/ppermute | solution.py:248
  26.1 3.3 %collective-permute-done.3.bottom = bf16[2,1,64,128]{3,2,1,0:T(8,128)(2,1)S(1)} collective-permute-done((bf16[2,1,64,128]{3,2,1,0:T(8,128)(2,1)S(1)}, bf16[2,1,64,128]{3,2,1,0:T(8,128)(2,1)S(1)}, u32[]{:S(2)}, u32[]{:S(2)}) %collective-permute-start.3) | collective-permute-done | bytes 32800 | tf_op jit(solution)/shard_map/ppermute | solution.py:248
  29.4 1.9 %collective-permute-start.4 = (bf16[2,2,64,256]{3,2,1,0:T(8,128)(2,1)S(1)}, bf16[2,2,64,256]{3,2,1,0:T(8,128)(2,1)S(1)}, u32[]{:S(2)}, u32[]{:S(2)}) collective-permute-start(bf16[2,2,64,256]{3,2,1,0:T(8,128)(2,1)S(1)} %get-tuple-element.28), channel_id=1, source_target_pairs={{0,1},{1,2},{2,3},{3,4},{4,5},{5,6},{6,7},{8,9},{9,10},{10,11},{11... | collective-permute-start | bytes 393224 | tf_op jit(solution)/shard_map/ppermute | solution.py:248
  31.3 2.4 %collective-permute-start.5 = (bf16[2,2,64,256]{3,2,1,0:T(8,128)(2,1)S(1)}, bf16[2,2,64,256]{3,2,1,0:T(8,128)(2,1)S(1)}, u32[]{:S(2)}, u32[]{:S(2)}) collective-permute-start(bf16[2,2,64,256]{3,2,1,0:T(8,128)(2,1)S(1)} %get-tuple-element.29), channel_id=1, source_target_pairs={{1,0},{2,1},{3,2},{4,3},{5,4},{6,5},{7,6},{9,8},{10,9},{11,10},{12... | collective-permute-start | bytes 393224 | tf_op jit(solution)/shard_map/ppermute | solution.py:248
  33.8 3.9 %collective-permute-done.5.bottom = bf16[2,2,64,256]{3,2,1,0:T(8,128)(2,1)S(1)} collective-permute-done((bf16[2,2,64,256]{3,2,1,0:T(8,128)(2,1)S(1)}, bf16[2,2,64,256]{3,2,1,0:T(8,128)(2,1)S(1)}, u32[]{:S(2)}, u32[]{:S(2)}) %collective-permute-start.5) | collective-permute-done | bytes 131104 | tf_op jit(solution)/shard_map/ppermute | solution.py:248
  37.6 3.1 %decode.1 = (f32[2,6,64,128]{3,2,1,0:T(8,128)S(1)}, bf16[2,6,64,128]{3,2,1,0:T(8,128)(2,1)S(1)}) custom-call(bf16[2,4,64,256]{3,2,1,0:T(8,128)(2,1)S(1)} %get-tuple-element.27.lat, bf16[2,2,64,256]{3,2,1,0:T(8,128)(2,1)S(1)} %collective-permute-done.4.top, bf16[2,2,64,256]{3,2,1,0:T(8,128)(2,1)S(1)} %collective-permute-done.5.bottom, ...), custom_call_target="tpu_custom_call" | custom-call | tf_op jit(solution)/shard_map/decode/pallas_call | solution.py:24
  40.8 6.1 %collective-permute-start.6 = (bf16[2,6,64,128]{3,2,1,0:T(8,128)(2,1)S(1)}, bf16[2,6,64,128]{3,2,1,0:T(8,128)(2,1)S(1)}, u32[]{:S(2)}, u32[]{:S(2)}) collective-permute-start(bf16[2,6,64,128]{3,2,1,0:T(8,128)(2,1)S(1)} %get-tuple-element.31), channel_id=1, source_target_pairs={{0,8},{8,16},{16,24},{24,32},{32,40},{40,48},{48,56},{56,64},{64,7... | collective-permute-start | bytes 589832 | tf_op jit(solution)/shard_map/ppermute | solution.py:243
  46.9 5.6 %collective-permute-done.6.part = bf16[2,6,64,128]{3,2,1,0:T(8,128)(2,1)S(1)} collective-permute-done((bf16[2,6,64,128]{3,2,1,0:T(8,128)(2,1)S(1)}, bf16[2,6,64,128]{3,2,1,0:T(8,128)(2,1)S(1)}, u32[]{:S(2)}, u32[]{:S(2)}) %collective-permute-start.6) | collective-permute-done | bytes 196640 | tf_op jit(solution)/shard_map/ppermute | solution.py:243
  52.5 0.7 collective-permute-start.8
  53.2 0.1 slope.1
  53.4 1.3 collective-permute-start.7
  54.7 7.9 %collective-permute-done.7.later = bf16[2,6,64,128]{3,2,1,0:T(8,128)(2,1)S(1)} collective-permute-done((bf16[2,6,64,128]{3,2,1,0:T(8,128)(2,1)S(1)}, bf16[2,6,64,128]{3,2,1,0:T(8,128)(2,1)S(1)}, u32[]{:S(2)}, u32[]{:S(2)}) %collective-permute-start.7) | collective-permute-done | bytes 196640 | tf_op jit(solution)/shard_map/ppermute | solution.py:243
  62.6 1.5 %copy-done.3 = bf16[4,9,64,384]{3,2,1,0:T(8,128)(2,1)S(1)} copy-done((bf16[4,9,64,384]{3,2,1,0:T(8,128)(2,1)S(1)}, bf16[4,9,64,384]{3,2,1,0:T(8,128)(2,1)}, u32[]{:S(2)}) %copy-start.3) | copy-done | bytes 1769496
  64.1 3.4 %grads.1 = (bf16[2,4,64,256]{3,2,1,0:T(8,128)(2,1)S(1)}, f32[3456,128]{1,0:T(8,128)S(1)}, bf16[3456,128]{1,0:T(8,128)(2,1)S(1)}) custom-call(s32[1]{0:T(128)} %bitcast.seg_at, s32[1]{0:T(128)} %bitcast.1.core_at, bf16[2,6,64,128]{3,2,1,0:T(8,128)(2,1)S(1)} %slope.1, bf16[2,6,64,128]{3,2,1,0:T(8,128)(2,1)S(1)} %collective-permute-done.7.later, ...), custom_call_target="tpu_custom_call" | custom-call | tf_op jit(solution)/shard_map/grads/pallas_call | solution.py:24
  67.5 2.4 %collective-permute-done.9.got = bf16[3456,128]{1,0:T(8,128)(2,1)S(1)} collective-permute-done((bf16[3456,128]{1,0:T(8,128)(2,1)S(1)}, bf16[3456,128]{1,0:T(8,128)(2,1)S(1)}, u32[]{:S(2)}, u32[]{:S(2)}) %collective-permute-start.9) | collective-permute-done | bytes 884768 | tf_op jit(solution)/shard_map/ppermute | solution.py:238
  70.0 0.1 halves.1
  70.1 29.7 %all_to_all.15.got = bf16[16,216,128]{2,1,0:T(8,128)(2,1)S(1)} all-to-all(bf16[16,216,128]{2,1,0:T(8,128)(2,1)S(1)} %halves.1), channel_id=1, replica_groups=mesh['segment'=2,'x'=4,'z'=4,'y'=4,'c'=2] {'x','y'}, dimensions={0} | all-to-all | bytes 1769472 | tf_op jit(solution)/shard_map/all_to_all | solution.py:234
  99.9 14.1 %all_to_all.16.got = bf16[4,216,128]{2,1,0:T(8,128)(2,1)S(1)} all-to-all(bf16[4,216,128]{2,1,0:T(8,128)(2,1)S(1)} %second.1), channel_id=1, replica_groups=mesh['segment'=2,'x'=4,'z'=4,'y'=4,'c'=2] {'z'}, dimensions={0} | all-to-all | bytes 442368 | tf_op jit(solution)/shard_map/all_to_all | solution.py:234
  114.1 14.8 %all_to_all.17 = bf16[16,216,128]{2,1,0:T(8,128)(2,1)S(1)} all-to-all(bf16[16,216,128]{2,1,0:T(8,128)(2,1)S(1)} %third.1), channel_id=1, replica_groups=mesh['segment'=2,'x'=4,'z'=4,'y'=4,'c'=2] {'x','y'}, dimensions={0} | all-to-all | bytes 1769472 | tf_op jit(solution)/shard_map/all_to_all | solution.py:234
  128.9 4.9 %collective-permute-start.10 = (bf16[3456,128]{1,0:T(8,128)(2,1)S(1)}, bf16[3456,128]{1,0:T(8,128)(2,1)S(1)}, u32[]{:S(2)}, u32[]{:S(2)}) collective-permute-start(bf16[3456,128]{1,0:T(8,128)(2,1)S(1)} %bitcast.9), channel_id=1, source_target_pairs={{0,1},{1,0},{2,3},{3,2},{4,5},{5,4},{6,7},{7,6},{8,9},{9,8},{10,11... | collective-permute-start | bytes 2654216 | tf_op jit(solution)/shard_map/ppermute | solution.py:238
  133.8 0.7 select_bitcast_fusion
  134.6 1.3 collective-permute-done.10
  135.9 2.2 %convert_multiply_fusion = f32[2,3456,128]{2,1,0:T(8,128)} fusion(bf16[1,3456,128]{2,1,0:T(8,128)(2,1)S(1)} %bitcast.11, bf16[1,3456,128]{2,1,0:T(8,128)(2,1)S(1)} %bitcast.10, pred[]{:T(512)S(6)} %eq.7), kind=kLoop, calls=%fused_computation | loop fusion | flops 4423680 | bytes 5308417 | tf_op jit(solution)/shard_map/mul | solution.py:332
  (16 shorter events, 0.4 us)
Async XLA Ops:
  1.6 36.1 %copy-start = (bf16[3,3,3,256,128]{4,3,2,1,0:T(8,128)(2,1)S(1)}, bf16[3,3,3,256,128]{4,3,2,1,0:T(8,128)(2,1)}, u32[]{:S(2)}) copy-start(bf16[3,3,3,256,128]{4,3,2,1,0:T(8,128)(2,1)} %weight.5) | copy-start | bytes 5308420
  1.6 6.6 %collective-permute-start = (bf16[4,1,128,128]{3,2,1,0:T(8,128)(2,1)S(1)}, bf16[4,1,128,128]{3,2,1,0:T(8,128)(2,1)S(1)}, u32[]{:S(2)}, u32[]{:S(2)}) collective-permute-start(bf16[4,1,128,128]{3,2,1,0:T(8,128)(2,1)S(1)} %slice.3), channel_id=1, source_target_pairs={{0,1},{1,2},{2,3},{3,4},{4,5},{5,6},{6,7},{8,9},{9,10},{10,11},{11... | collective-permute-start | bytes 393224 | tf_op jit(solution)/shard_map/ppermute | solution.py:248
  8.2 1.5 %copy-start.1 = (bf16[3,3,3,128,256]{4,3,2,1,0:T(8,128)(2,1)S(1)}, bf16[3,3,3,128,256]{4,3,2,1,0:T(8,128)(2,1)}, u32[]{:S(2)}) copy-start(bf16[3,3,3,128,256]{4,3,2,1,0:T(8,128)(2,1)} %weight.3) | copy-start | bytes 5308420
  9.7 1.2 copy-start.4
  10.9 0.9 copy-start.5
  14.6 38.8 %copy-start.2 = (bf16[4,9,64,384]{3,2,1,0:T(8,128)(2,1)}, bf16[4,9,64,384]{3,2,1,0:T(8,128)(2,1)S(1)}, u32[]{:S(2)}) copy-start(bf16[4,9,64,384]{3,2,1,0:T(8,128)(2,1)S(1)} %get-tuple-element.34.taps) | copy-start | bytes 5308420
  14.6 14.8 %collective-permute-start.1 = (bf16[4,64,256]{2,1,0:T(8,128)(2,1)S(1)}, bf16[4,64,256]{2,1,0:T(8,128)(2,1)S(1)}, u32[]{:S(2)}, u32[]{:S(2)}) collective-permute-start(bf16[4,64,256]{2,1,0:T(8,128)(2,1)S(1)} %get-tuple-element.22), channel_id=1, source_target_pairs={{0,8},{8,16},{16,24},{24,32},{32,40},{40,48},{48,56},{56,64},{64,7... | collective-permute-start | bytes 393224 | tf_op jit(solution)/shard_map/ppermute | solution.py:243
  19.5 6.6 %collective-permute-start.2 = (bf16[2,1,64,128]{3,2,1,0:T(8,128)(2,1)S(1)}, bf16[2,1,64,128]{3,2,1,0:T(8,128)(2,1)S(1)}, u32[]{:S(2)}, u32[]{:S(2)}) collective-permute-start(bf16[2,1,64,128]{3,2,1,0:T(8,128)(2,1)S(1)} %get-tuple-element.23), channel_id=1, source_target_pairs={{0,1},{1,2},{2,3},{3,4},{4,5},{5,6},{6,7},{8,9},{9,10},{10,11},{11... | collective-permute-start | bytes 98312 | tf_op jit(solution)/shard_map/ppermute | solution.py:248
  24.1 5.2 %collective-permute-start.3 = (bf16[2,1,64,128]{3,2,1,0:T(8,128)(2,1)S(1)}, bf16[2,1,64,128]{3,2,1,0:T(8,128)(2,1)S(1)}, u32[]{:S(2)}, u32[]{:S(2)}) collective-permute-start(bf16[2,1,64,128]{3,2,1,0:T(8,128)(2,1)S(1)} %get-tuple-element.24), channel_id=1, source_target_pairs={{1,0},{2,1},{3,2},{4,3},{5,4},{6,5},{7,6},{9,8},{10,9},{11,10},{12... | collective-permute-start | bytes 98312 | tf_op jit(solution)/shard_map/ppermute | solution.py:248
  29.4 4.3 %collective-permute-start.4 = (bf16[2,2,64,256]{3,2,1,0:T(8,128)(2,1)S(1)}, bf16[2,2,64,256]{3,2,1,0:T(8,128)(2,1)S(1)}, u32[]{:S(2)}, u32[]{:S(2)}) collective-permute-start(bf16[2,2,64,256]{3,2,1,0:T(8,128)(2,1)S(1)} %get-tuple-element.28), channel_id=1, source_target_pairs={{0,1},{1,2},{2,3},{3,4},{4,5},{5,6},{6,7},{8,9},{9,10},{10,11},{11... | collective-permute-start | bytes 393224 | tf_op jit(solution)/shard_map/ppermute | solution.py:248
  31.3 6.3 %collective-permute-start.5 = (bf16[2,2,64,256]{3,2,1,0:T(8,128)(2,1)S(1)}, bf16[2,2,64,256]{3,2,1,0:T(8,128)(2,1)S(1)}, u32[]{:S(2)}, u32[]{:S(2)}) collective-permute-start(bf16[2,2,64,256]{3,2,1,0:T(8,128)(2,1)S(1)} %get-tuple-element.29), channel_id=1, source_target_pairs={{1,0},{2,1},{3,2},{4,3},{5,4},{6,5},{7,6},{9,8},{10,9},{11,10},{12... | collective-permute-start | bytes 393224 | tf_op jit(solution)/shard_map/ppermute | solution.py:248
  40.8 11.8 %collective-permute-start.6 = (bf16[2,6,64,128]{3,2,1,0:T(8,128)(2,1)S(1)}, bf16[2,6,64,128]{3,2,1,0:T(8,128)(2,1)S(1)}, u32[]{:S(2)}, u32[]{:S(2)}) collective-permute-start(bf16[2,6,64,128]{3,2,1,0:T(8,128)(2,1)S(1)} %get-tuple-element.31), channel_id=1, source_target_pairs={{0,8},{8,16},{16,24},{24,32},{32,40},{40,48},{48,56},{56,64},{64,7... | collective-permute-start | bytes 589832 | tf_op jit(solution)/shard_map/ppermute | solution.py:243
  52.5 10.1 %collective-permute-start.8 = (bf16[2,9,128,128]{3,2,1,0:T(8,128)(2,1)}, bf16[2,9,128,128]{3,2,1,0:T(8,128)(2,1)S(1)}, u32[]{:S(2)}, u32[]{:S(2)}) collective-permute-start(bf16[2,9,128,128]{3,2,1,0:T(8,128)(2,1)} %get-tuple-element.36), channel_id=1, source_target_pairs={{128,8},{136,16},{144,24},{152,32},{160,40},{168,48},{176,56},{184... | collective-permute-start | bytes 1769480 | tf_op jit(solution)/shard_map/ppermute | solution.py:306
  53.4 9.2 %collective-permute-start.7 = (bf16[2,6,64,128]{3,2,1,0:T(8,128)(2,1)S(1)}, bf16[2,6,64,128]{3,2,1,0:T(8,128)(2,1)S(1)}, u32[]{:S(2)}, u32[]{:S(2)}) collective-permute-start(bf16[2,6,64,128]{3,2,1,0:T(8,128)(2,1)S(1)} %slope.1), channel_id=1, source_target_pairs={{8,0},{16,8},{24,16},{32,24},{40,32},{48,40},{56,48},{64,56},{72,6... | collective-permute-start | bytes 589832 | tf_op jit(solution)/shard_map/ppermute | solution.py:243
  62.6 1.5 %copy-start.3 = (bf16[4,9,64,384]{3,2,1,0:T(8,128)(2,1)S(1)}, bf16[4,9,64,384]{3,2,1,0:T(8,128)(2,1)}, u32[]{:S(2)}) copy-start(bf16[4,9,64,384]{3,2,1,0:T(8,128)(2,1)} %copy-done.2) | copy-start | bytes 5308420
  67.4 2.5 %collective-permute-start.9 = (bf16[3456,128]{1,0:T(8,128)(2,1)S(1)}, bf16[3456,128]{1,0:T(8,128)(2,1)S(1)}, u32[]{:S(2)}, u32[]{:S(2)}) collective-permute-start(bf16[3456,128]{1,0:T(8,128)(2,1)S(1)} %get-tuple-element.39), channel_id=1, source_target_pairs={{0,1},{1,0},{2,3},{3,2},{4,5},{5,4},{6,7},{7,6},{8,9},{9,8},{10,11... | collective-permute-start | bytes 2654216 | tf_op jit(solution)/shard_map/ppermute | solution.py:238
  128.9 7.0 %collective-permute-start.10 = (bf16[3456,128]{1,0:T(8,128)(2,1)S(1)}, bf16[3456,128]{1,0:T(8,128)(2,1)S(1)}, u32[]{:S(2)}, u32[]{:S(2)}) collective-permute-start(bf16[3456,128]{1,0:T(8,128)(2,1)S(1)} %bitcast.9), channel_id=1, source_target_pairs={{0,1},{1,0},{2,3},{3,2},{4,5},{5,4},{6,7},{7,6},{8,9},{9,8},{10,11... | collective-permute-start | bytes 2654216 | tf_op jit(solution)/shard_map/ppermute | solution.py:238

commit v4 on v3

--- a/solution.py
+++ b/solution.py
@@ -63,39 +63,55 @@
     return before, row, after
 
 
-def fill_clip(stage, src, top, dst, frames):
+def start_stage(stage):
     stage[0:8, :] = jnp.zeros((8, stage.shape[1]), F32)
-    for f in range(frames):
-        dst[f, 0] = clip_windows(top[f, 0], stage)
+
+
+def edge_body(clip, cot, down):
+    down[0:4] = clip[:, 7]
+    down[4, 0:64] = cot[0, 3]
+    down[4, 64:128] = cot[1, 3]
+
+
+def windows_body(clip, taps, stage):
+    start_stage(stage)
+    for f in range(4):
 
         def one(r, carry, f=f):
-            dst[f, r + 1] = clip_windows(src[f, r], stage)
+            taps[f, r] = clip_windows(clip[f, r], stage)
             return carry
 
         lax.fori_loop(0, 8, one, 0)
 
 
-def clip_im2col(taps, f, b):
-    return jnp.concatenate([taps[f, 2 * h + b] for h in range(4)], axis=0)
-
-
-def encode_body(clip, top, weight, cot, lat1, part, own0, tail, cot_down, cot_up, taps, stage):
-    fill_clip(stage, clip, top, taps, 4)
+def clip_im2col(tops, taps, f, b):
+    rows = [2 * h + b for h in range(4)]
+    return jnp.concatenate([tops[f] if p == 0 else taps[f, p - 1] for p in rows], axis=0)
+
+
+def encode_body(
+    clip, taps, above, weight, cot, below, lat1, part, own0, tail, tops, rows6, stage
+):
+    start_stage(stage)
+    for f in range(4):
+        tops[f] = clip_windows(above[f], stage)
 
     def conv(f, a):
         total = None
         for b in range(3):
-            term = dot(clip_im2col(taps, f, b), weight[a, b].reshape(384, 256))
+            term = dot(clip_im2col(tops, taps, f, b), weight[a, b].reshape(384, 256))
             total = term if total is None else total + term
         return total
 
     part[...] = (conv(2, 0) + conv(3, 1)).astype(part.dtype).reshape(4, 64, 256)
     lat1[...] = (conv(0, 0) + conv(1, 1) + conv(2, 2)).astype(BF16).reshape(4, 64, 256)
     own0[...] = conv(0, 2).reshape(4, 64, 256)
-    tail[:, 0:1] = top[2:4]
+    tail[:, 0] = above[2:4]
     tail[:, 1:9] = clip[2:4]
-    cot_down[...] = cot[:, 3:4]
-    cot_up[...] = cot[:, 0:1]
+    rows6[0, 0] = above[4, 0:64]
+    rows6[1, 0] = above[4, 64:128]
+    rows6[:, 1:5] = cot[...]
+    rows6[:, 5:6] = below[...]
 
 
 def join_body(own0, part, lat1, lat, down, up):
@@ -118,7 +134,7 @@
         lax.fori_loop(0, 4, one, 0)
 
 
-def decode_body(lat, top, bottom, weight, own, part, wide):
+def decode_body(lat, top, bottom, weight, own, behind, part, wide):
     fill_latent(lat, top, bottom, wide)
 
     def conv(f, a):
@@ -133,34 +149,58 @@
     part[1] = conv(1, 0).astype(part.dtype).reshape(6, 64, 128)
     own[0] = conv(0, 2).reshape(6, 64, 128)
     own[1] = (conv(0, 1) + conv(1, 2)).reshape(6, 64, 128)
-
-
-def slope_body(own, part, cot, top, bottom, slope):
-    def rows(at, grad):
-        pre = own[:, at] + part[:, at].astype(F32)
-        sigm = jax.nn.sigmoid(pre)
-        slope[:, at] = (grad.astype(F32) * sigm * (1.0 + pre * (1.0 - sigm))).astype(BF16)
-
-    rows(slice(0, 1), top[...])
-    rows(slice(1, 5), cot[...])
-    rows(slice(5, 6), bottom[...])
+    behind[...] = own[...].astype(behind.dtype)
+
+
+def turned_body(seg_at, tail, tops, taps, lat, top, bottom, turned, btops, btaps, wide, stage):
+    seg = seg_at[0]
+
+    @pl.when(seg == 0)
+    def _():
+        start_stage(stage)
+        for f in range(2):
+            btops[f] = clip_windows(tail[f, 0], stage)
+
+            def one(r, carry, f=f):
+                btaps[f, r] = clip_windows(tail[f, r + 1], stage)
+                return carry
+
+            lax.fori_loop(0, 8, one, 0)
+        for f in range(5):
+            for b in range(3):
+                rows = clip_im2col(btops, btaps, f, b) if f < 2 else clip_im2col(tops, taps, f - 2, b)
+                turned[f * 3 + b] = rows.T
+
+    @pl.when(seg != 0)
+    def _():
+        fill_latent(lat, top, bottom, wide)
+        for f in range(2):
+            for b in range(3):
+                flat = wide[f, b + 1 : b + 5].reshape(256, 768).T
+                turned[(f * 3 + b) * 2] = flat[0:384]
+                turned[(f * 3 + b) * 2 + 1] = flat[384:768]
 
 
 def grads_body(
-    seg_at, core_at, slope, later, weight, taps, tail, lat, top, bottom,
-    lat_grad, own, send, gathered, rim, btaps, wide, stage,
+    seg_at, core_at, own_part, from_behind, gone, from_later, cot, later_cot, weight, turned,
+    lat_grad, own, send, gathered, slopes, rim,
 ):
     seg = seg_at[0]
     core = core_at[0]
 
+    def slope_of(pre, grad):
+        sigm = jax.nn.sigmoid(pre)
+        return (grad.astype(F32) * sigm * (1.0 + pre * (1.0 - sigm))).astype(BF16)
+
+    slopes[0:2] = slope_of(own_part[...] + from_behind[...].astype(F32), cot[...])
+    slopes[2:4] = slope_of(from_later[...].astype(F32) + gone[...].astype(F32), later_cot[...])
+
     @pl.when(seg == 0)
     def _():
         for f in range(4):
-            src = slope if f < 2 else later
             for r in range(6):
-                left, same, right = neighbour_cols(src[f % 2, r])
+                left, same, right = neighbour_cols(slopes[f, r])
                 rim[f, r] = jnp.concatenate([right, same, left], axis=1)
-        fill_clip(stage, tail.at[:, 1:9], tail, btaps, 2)
         grads = []
         for t in range(2):
             total = None
@@ -175,12 +215,7 @@
             grads.append(grad)
         for a in range(3):
             for b in range(3):
-                total = None
-                for t in range(2):
-                    f = 2 * t + a
-                    rows = clip_im2col(btaps, f, b) if f < 2 else clip_im2col(taps, f - 2, b)
-                    term = dot_tn(rows, grads[t])
-                    total = term if total is None else total + term
+                total = dot(turned[a * 3 + b], grads[0]) + dot(turned[(a + 2) * 3 + b], grads[1])
                 for c in range(3):
                     tap = (a * 3 + b) * 3 + c
                     for j in range(2):
@@ -191,17 +226,16 @@
     @pl.when(seg != 0)
     def _():
         lat_grad[...] = jnp.zeros(lat_grad.shape, BF16)
-        fill_latent(lat, top, bottom, wide)
         for a in range(3):
             for b in range(3):
-                total = None
-                for f in range(2):
-                    t = f + 2 - a
-                    cells = (slope if t < 2 else later)[t % 2, 1:5].reshape(256, 128)
-                    term = dot_tn(wide[f, b + 1 : b + 5].reshape(256, 768), cells)
-                    total = term if total is None else total + term
-                start = (a * 3 + b) * 768
-                gathered[start : start + 768, :] = total
+                for i in range(2):
+                    total = None
+                    for f in range(2):
+                        cells = slopes[f + 2 - a, 1:5].reshape(256, 128)
+                        term = dot(turned[(f * 3 + b) * 2 + i], cells)
+                        total = term if total is None else total + term
+                    start = (a * 3 + b) * 768 + i * 384
+                    gathered[start : start + 384, :] = total
 
     half = own.shape[0]
     own[...] = gathered[pl.ds(pl.multiple_of(core * half, 8), half), :]
@@ -263,26 +297,29 @@
     seg = lax.axis_index("segment")
     core = lax.axis_index("c")
 
-    above = by_rows(clip_frames[:, 7:8], 1)
-    lat1, part, own0, tail, cot_down, cot_up, taps = on_chip(
+    stage = pltpu.VMEM((136, 128), F32)
+    (down,) = on_chip(edge_body, [shape((5, 128, 128), BF16)], "edge")(clip_frames, out_grad)
+    above = by_rows(down, 1)
+    below = by_rows(out_grad[:, 0:1], -1)
+    (taps,) = on_chip(windows_body, [shape((4, 8, 64, 384), BF16)], "windows", scratch=[stage])(
+        clip_frames
+    )
+    lat1, part, own0, tail, tops, cot = on_chip(
         encode_body,
         [
             shape((4, 64, 256), BF16),
             shape((4, 64, 256), PART),
             shape((4, 64, 256), F32),
             shape((2, 9, 128, 128), BF16),
-            shape((2, 1, 64, 128), BF16),
-            shape((2, 1, 64, 128), BF16),
-            shape((4, 9, 64, 384), BF16),
+            shape((4, 64, 384), BF16),
+            shape((2, 6, 64, 128), BF16),
         ],
         "encode",
-        scratch=[pltpu.VMEM((136, 128), F32)],
+        scratch=[stage],
         grant=16,
-    )(clip_frames, above, enc_weight, out_grad)
+    )(clip_frames, taps, above, enc_weight, out_grad, below)
     part = by_frames(part, 1)
-    cot_top = by_rows(cot_down, 1)
-    cot_bottom = by_rows(cot_up, -1)
-    part, cot_top, cot_bottom = lax.optimization_barrier((part, cot_top, cot_bottom))
+    later_cot = by_frames(cot, -1)
     latent, down, up = on_chip(
         join_body,
         [
@@ -294,20 +331,33 @@
     )(own0, part, lat1)
     top = by_rows(down, 1)
     bottom = by_rows(up, -1)
-    own, part = on_chip(
+    tail, _ = lax.optimization_barrier((tail, down))
+    tail = lax.ppermute(tail, ("segment", "x", "z"), [(16 + t - 1, t) for t in range(1, 16)])
+    rows6 = (2, 6, 64, 128)
+    own_part, behind, gone = on_chip(
         decode_body,
-        [shape((2, 6, 64, 128), F32), shape((2, 6, 64, 128), PART)],
+        [shape(rows6, F32), shape(rows6, PART), shape(rows6, PART)],
         "decode",
         scratch=[pltpu.VMEM((2, 8, 64, 768), BF16)],
         grant=14,
     )(latent, top, bottom, dec_weight)
-    part = by_frames(part, 1)
-    tail, _ = lax.optimization_barrier((tail, part))
-    tail = lax.ppermute(tail, ("segment", "x", "z"), [(16 + t - 1, t) for t in range(1, 16)])
-    (slope,) = on_chip(slope_body, [shape((2, 6, 64, 128), BF16)], "slope")(
-        own, part, out_grad, cot_top, cot_bottom
-    )
-    later = by_frames(slope, -1)
+    from_behind = by_frames(gone, 1)
+    from_later = by_frames(behind, -1)
+    seg = seg.reshape(1)
+    tail, lat, _ = lax.optimization_barrier((tail, latent, gone))
+    (turned,) = on_chip(
+        turned_body,
+        [shape((15, 384, 256), BF16)],
+        "turned",
+        1,
+        [
+            pltpu.VMEM((2, 64, 384), BF16),
+            pltpu.VMEM((2, 8, 64, 384), BF16),
+            pltpu.VMEM((2, 8, 64, 768), BF16),
+            stage,
+        ],
+        16,
+    )(seg, tail, tops, taps, lat, top, bottom)
     lat_grad, own, send = on_chip(
         grads_body,
         [
@@ -319,14 +369,12 @@
         2,
         [
             pltpu.VMEM((6912, 128), F32),
+            pltpu.VMEM((4, 6, 64, 128), BF16),
             pltpu.VMEM((4, 6, 64, 384), BF16),
-            pltpu.VMEM((2, 9, 64, 384), BF16),
-            pltpu.VMEM((2, 8, 64, 768), BF16),
-            pltpu.VMEM((136, 128), F32),
-        ],
-        26,
-    )(seg.reshape(1), core.reshape(1), slope, later, dec_weight, taps, tail, latent, top, bottom)
-    latent_pair = jnp.where(seg == 0, lat_grad, latent)[None]
+        ],
+        24,
+    )(seg, core.reshape(1), own_part, from_behind, gone, from_later, cot, later_cot, dec_weight, turned)
+    latent_pair = jnp.where(seg[0] == 0, lat_grad, latent)[None]
     half, other = summed(own, send)
     whole = jnp.where(core == 0, jnp.stack([half, other]), jnp.stack([other, half]))
     weight_grads = whole.reshape(27, 32768).astype(F32) * (1.0 / math.sqrt(32 * 32 * 64))

time: 139 us -> 128 us (0.921)
  waiting for transfers between devices: 26.4 us -> 14.5 us
  blocking collectives: 58.6 us -> 53.3 us
  Pallas kernels: 9.77 us -> 13.6 us
  starting transfers between devices: 33.6 us -> 36.2 us
    ppermute x3 -> x4, waiting for transfers between devices: 13.6 us -> 5.01 us  [by_frames(): return lax.ppermute(array, ('x', 'z'), pairs)]
    ppermute x3 -> x4, starting transfers between devices: 12.3 us -> 17.7 us  [by_frames(): return lax.ppermute(array, ('x', 'z'), pairs)]
    all_to_all x3, blocking collectives: 58.6 us -> 53.3 us  [exchanged(): return lax.all_to_all(array, axes, 0, 0, tiled=True)]
    ppermute x5 -> x4, starting transfers between devices: 15.6 us -> 11.6 us  [by_rows(): return lax.ppermute(array, ('y', 'c'), pairs)]
    pallas_call x8 -> x10, Pallas kernels: 9.77 us -> 13.6 us  [call(): pl.pallas_call(body, out_shape=outs, in_specs=specs, out_specs=[pl.BlockS...]
    ppermute x5 -> x4, waiting for transfers between devices: 9.08 us -> 5.79 us  [by_rows(): return lax.ppermute(array, ('y', 'c'), pairs)]
    unnamed x12 -> x30, local copies, waits for them, and re-layouts: 5.09 us -> 6.39 us
  transfers between devices with their start and end apart: 11 -> 11, of which waited for: 7 -> 6; matrix products, arithmetic and copies ran while one was open for 1% -> 1% of each run, Pallas kernels for 0% -> 5%
where the time goes in v4:
time: 128 us
  blocking collectives  53.3 us (42%)
  starting transfers between devices  36.2 us (28%)
  waiting for transfers between devices  14.5 us (11%)
  Pallas kernels  13.6 us (11%)
  local copies, waits for them, and re-layouts  6.39 us (5%)
  other arithmetic  2.96 us (2%)
    all_to_all x3, blocking collectives, exchanged(): return lax.all_to_all(array, axes, 0, 0, tiled=True)  53.3 us
    ppermute x4, starting transfers between devices, by_frames(): return lax.ppermute(array, ('x', 'z'), pairs)  17.7 us
    pallas_call x10, Pallas kernels, call(): pl.pallas_call(body, out_shape=outs, in_specs=specs, out_specs=[pl.BlockS...  13.6 us
    ppermute x4, starting transfers between devices, by_rows(): return lax.ppermute(array, ('y', 'c'), pairs)  11.6 us
    unnamed x30, local copies, waits for them, and re-layouts  6.39 us
    ppermute x4, waiting for transfers between devices, by_rows(): return lax.ppermute(array, ('y', 'c'), pairs)  5.79 us
    ppermute x2, starting transfers between devices, to_core(): return lax.ppermute(array, 'c', [(0, 1), (1, 0)])  5.48 us
    ppermute x4, waiting for transfers between devices, by_frames(): return lax.ppermute(array, ('x', 'z'), pairs)  5.01 us
  transfers between devices with their start and end apart: 11, of which 6 were waited for; matrix products, arithmetic and copies ran while one was open for 1% of the time, Pallas kernels for 5%

profile of v4, /device:TPU:1, one launch (start us, length us, event | category | flops | bytes accessed | tf_op | source)
XLA Modules:
  0.0 127.8 jit_solution(16317671062599756223)
XLA Ops:
  0.6 1.2 copy-done
  1.9 0.9 copy-done.7
  2.8 4.8 %collective-permute-start = (bf16[5,128,128]{2,1,0:T(8,128)(2,1)S(1)}, bf16[5,128,128]{2,1,0:T(8,128)(2,1)S(1)}, u32[]{:S(2)}, u32[]{:S(2)}) collective-permute-start(bf16[5,128,128]{2,1,0:T(8,128)(2,1)S(1)} %edge.1), channel_id=1, source_target_pairs={{0,1},{1,2},{2,3},{3,4},{4,5},{5,6},{6,7},{8,9},{9,10},{10,11},{11... | collective-permute-start | bytes 491528 | tf_op jit(solution)/shard_map/ppermute | solution.py:282
  7.6 1.9 %collective-permute-start.1 = (bf16[2,1,64,128]{3,2,1,0:T(8,128)(2,1)S(1)}, bf16[2,1,64,128]{3,2,1,0:T(8,128)(2,1)S(1)}, u32[]{:S(2)}, u32[]{:S(2)}) collective-permute-start(bf16[2,1,64,128]{3,2,1,0:T(8,128)(2,1)S(1)} %slice.3), channel_id=1, source_target_pairs={{1,0},{2,1},{3,2},{4,3},{5,4},{6,5},{7,6},{9,8},{10,9},{11,10},{12... | collective-permute-start | bytes 98312 | tf_op jit(solution)/shard_map/ppermute | solution.py:282
  10.1 2.7 %collective-permute-done.1.below = bf16[2,1,64,128]{3,2,1,0:T(8,128)(2,1)S(1)} collective-permute-done((bf16[2,1,64,128]{3,2,1,0:T(8,128)(2,1)S(1)}, bf16[2,1,64,128]{3,2,1,0:T(8,128)(2,1)S(1)}, u32[]{:S(2)}, u32[]{:S(2)}) %collective-permute-start.1) | collective-permute-done | bytes 32800 | tf_op jit(solution)/shard_map/ppermute | solution.py:282
  12.9 2.2 %encode.1 = (bf16[4,64,256]{2,1,0:T(8,128)(2,1)S(1)}, bf16[4,64,256]{2,1,0:T(8,128)(2,1)S(1)}, f32[4,64,256]{2,1,0:T(8,128)S(1)}, bf16[2,9,128,128]{3,2,1,0:T(8,...) custom-call(bf16[4,8,128,128]{3,2,1,0:T(8,128)(2,1)S(1)} %copy-done.1, ...), custom_call_target="tpu_custom_call" | custom-call | tf_op jit(solution)/shard_map/encode/pallas_call | solution.py:24
  15.1 4.9 %collective-permute-start.2 = (bf16[4,64,256]{2,1,0:T(8,128)(2,1)S(1)}, bf16[4,64,256]{2,1,0:T(8,128)(2,1)S(1)}, u32[]{:S(2)}, u32[]{:S(2)}) collective-permute-start(bf16[4,64,256]{2,1,0:T(8,128)(2,1)S(1)} %get-tuple-element.21), channel_id=1, source_target_pairs={{0,8},{8,16},{16,24},{24,32},{32,40},{40,48},{48,56},{56,64},{64,7... | collective-permute-start | bytes 393224 | tf_op jit(solution)/shard_map/ppermute | solution.py:277
  20.0 2.4 %collective-permute-done.2.part = bf16[4,64,256]{2,1,0:T(8,128)(2,1)S(1)} collective-permute-done((bf16[4,64,256]{2,1,0:T(8,128)(2,1)S(1)}, bf16[4,64,256]{2,1,0:T(8,128)(2,1)S(1)}, u32[]{:S(2)}, u32[]{:S(2)}) %collective-permute-start.2) | collective-permute-done | bytes 131104 | tf_op jit(solution)/shard_map/ppermute | solution.py:277
  22.5 1.5 %collective-permute-start.8 = (bf16[2,9,128,128]{3,2,1,0:T(8,128)(2,1)}, bf16[2,9,128,128]{3,2,1,0:T(8,128)(2,1)}, u32[]{:S(2)}, u32[]{:S(2)}) collective-permute-start(bf16[2,9,128,128]{3,2,1,0:T(8,128)(2,1)} %get-tuple-element.31), channel_id=1, source_target_pairs={{128,8},{136,16},{144,24},{152,32},{160,40},{168,48},{176,56},{184... | collective-permute-start | bytes 1769480 | tf_op jit(solution)/shard_map/ppermute | solution.py:335
  24.0 2.9 %collective-permute-start.3 = (bf16[2,2,64,256]{3,2,1,0:T(8,128)(2,1)S(1)}, bf16[2,2,64,256]{3,2,1,0:T(8,128)(2,1)S(1)}, u32[]{:S(2)}, u32[]{:S(2)}) collective-permute-start(bf16[2,2,64,256]{3,2,1,0:T(8,128)(2,1)S(1)} %get-tuple-element.24), channel_id=1, source_target_pairs={{0,1},{1,2},{2,3},{3,4},{4,5},{5,6},{6,7},{8,9},{9,10},{10,11},{11... | collective-permute-start | bytes 393224 | tf_op jit(solution)/shard_map/ppermute | solution.py:282
  26.9 1.9 %collective-permute-start.4 = (bf16[2,2,64,256]{3,2,1,0:T(8,128)(2,1)S(1)}, bf16[2,2,64,256]{3,2,1,0:T(8,128)(2,1)S(1)}, u32[]{:S(2)}, u32[]{:S(2)}) collective-permute-start(bf16[2,2,64,256]{3,2,1,0:T(8,128)(2,1)S(1)} %get-tuple-element.25), channel_id=1, source_target_pairs={{1,0},{2,1},{3,2},{4,3},{5,4},{6,5},{7,6},{9,8},{10,9},{11,10},{12... | collective-permute-start | bytes 393224 | tf_op jit(solution)/shard_map/ppermute | solution.py:282
  28.8 1.3 %collective-permute-start.7 = (bf16[2,6,64,128]{3,2,1,0:T(8,128)(2,1)}, bf16[2,6,64,128]{3,2,1,0:T(8,128)(2,1)}, u32[]{:S(2)}, u32[]{:S(2)}) collective-permute-start(bf16[2,6,64,128]{3,2,1,0:T(8,128)(2,1)} %get-tuple-element.29.cot), channel_id=1, source_target_pairs={{8,0},{16,8},{24,16},{32,24},{40,32},{48,40},{56,48},{64,56},{72,6... | collective-permute-start | bytes 589832 | tf_op jit(solution)/shard_map/ppermute | solution.py:277
  30.1 3.0 %collective-permute-done.4.bottom = bf16[2,2,64,256]{3,2,1,0:T(8,128)(2,1)S(1)} collective-permute-done((bf16[2,2,64,256]{3,2,1,0:T(8,128)(2,1)S(1)}, bf16[2,2,64,256]{3,2,1,0:T(8,128)(2,1)S(1)}, u32[]{:S(2)}, u32[]{:S(2)}) %collective-permute-start.4) | collective-permute-done | bytes 131104 | tf_op jit(solution)/shard_map/ppermute | solution.py:282
  33.2 3.8 %decode.1 = (f32[2,6,64,128]{3,2,1,0:T(8,128)S(1)}, bf16[2,6,64,128]{3,2,1,0:T(8,128)(2,1)}, bf16[2,6,64,128]{3,2,1,0:T(8,128)(2,1)}) custom-call(bf16[2,4,64,256]{3,2,1,0:T(8,128)(2,1)S(1)} %get-tuple-element.34.lat, bf16[2,2,64,256]{3,2,1,0:T(8,128)(2,1)S(1)} %collective-permute-done.3.top, bf16[2,2,64,256]{3,2,1,0:T(8,128)(2,1)S(1)} %collective-permute-done.4.bottom, ...), custom_call_target="tpu_custom_call" | custom-call | tf_op jit(solution)/shard_map/decode/pallas_call | solution.py:24
  37.0 0.7 copy-done.3
  37.7 0.8 copy-done.11
  38.5 10.2 %collective-permute-start.5 = (bf16[2,6,64,128]{3,2,1,0:T(8,128)(2,1)}, bf16[2,6,64,128]{3,2,1,0:T(8,128)(2,1)}, u32[]{:S(2)}, u32[]{:S(2)}) collective-permute-start(bf16[2,6,64,128]{3,2,1,0:T(8,128)(2,1)} %get-tuple-element.27.gone), channel_id=1, source_target_pairs={{0,8},{8,16},{16,24},{24,32},{32,40},{40,48},{48,56},{56,64},{64,7... | collective-permute-start | bytes 589832 | tf_op jit(solution)/shard_map/ppermute | solution.py:277
  48.7 1.3 %collective-permute-start.6 = (bf16[2,6,64,128]{3,2,1,0:T(8,128)(2,1)}, bf16[2,6,64,128]{3,2,1,0:T(8,128)(2,1)}, u32[]{:S(2)}, u32[]{:S(2)}) collective-permute-start(bf16[2,6,64,128]{3,2,1,0:T(8,128)(2,1)} %get-tuple-element.28), channel_id=1, source_target_pairs={{8,0},{16,8},{24,16},{32,24},{40,32},{48,40},{56,48},{64,56},{72,6... | collective-permute-start | bytes 589832 | tf_op jit(solution)/shard_map/ppermute | solution.py:277
  50.0 0.9 copy-done.4
  50.9 0.9 copy-done.10
  51.9 0.9 copy-done.14
  52.8 2.2 %turned.1 = bf16[15,384,256]{2,1,0:T(8,128)(2,1)S(1)} custom-call(s32[1]{0:T(128)} %bitcast.seg_at, bf16[2,9,128,128]{3,2,1,0:T(8,128)(2,1)} %collective-permute-done.8.tail, bf16[4,64,384]{2,1,0:T(8,128)(2,1)S(1)} %copy-done.14, bf16[4,8,64,384]{3,2,1,0:T(8,128)(2,1)S(1)} %windows.1.taps, bf16[2,4,64,256]{3,2,1,0:T(8,128)(2,1)S(1)} %copy-done.4, ...), custom_call_target="tpu_custom_call" | custom-call | tf_op jit(solution)/shard_map/turned/pallas_call | solution.py:24
  55.0 2.6 %collective-permute-done.6.from_later = bf16[2,6,64,128]{3,2,1,0:T(8,128)(2,1)} collective-permute-done((bf16[2,6,64,128]{3,2,1,0:T(8,128)(2,1)}, bf16[2,6,64,128]{3,2,1,0:T(8,128)(2,1)}, u32[]{:S(2)}, u32[]{:S(2)}) %collective-permute-start.6) | collective-permute-done | bytes 196640 | tf_op jit(solution)/shard_map/ppermute | solution.py:277
  57.6 4.4 %grads.1 = (bf16[2,4,64,256]{3,2,1,0:T(8,128)(2,1)S(1)}, f32[3456,128]{1,0:T(8,128)S(1)}, bf16[3456,128]{1,0:T(8,128)(2,1)S(1)}) custom-call(s32[1]{0:T(128)} %bitcast.seg_at, s32[1]{0:T(128)} %bitcast.1.core_at, f32[2,6,64,128]{3,2,1,0:T(8,128)S(1)} %copy-done.12, bf16[2,6,64,128]{3,2,1,0:T(8,128)(2,1)} %collective-permute-done.5.from_behind, ...), custom_call_target="tpu_custom_call" | custom-call | tf_op jit(solution)/shard_map/grads/pallas_call | solution.py:24
  62.1 2.4 %collective-permute-done.9.got = bf16[3456,128]{1,0:T(8,128)(2,1)S(1)} collective-permute-done((bf16[3456,128]{1,0:T(8,128)(2,1)S(1)}, bf16[3456,128]{1,0:T(8,128)(2,1)S(1)}, u32[]{:S(2)}, u32[]{:S(2)}) %collective-permute-start.9) | collective-permute-done | bytes 884768 | tf_op jit(solution)/shard_map/ppermute | solution.py:272
  64.7 24.5 %all_to_all.15.got = bf16[16,216,128]{2,1,0:T(8,128)(2,1)S(1)} all-to-all(bf16[16,216,128]{2,1,0:T(8,128)(2,1)S(1)} %halves.1), channel_id=1, replica_groups=mesh['segment'=2,'x'=4,'z'=4,'y'=4,'c'=2] {'x','y'}, dimensions={0} | all-to-all | bytes 1769472 | tf_op jit(solution)/shard_map/all_to_all | solution.py:268
  89.3 14.5 %all_to_all.16.got = bf16[4,216,128]{2,1,0:T(8,128)(2,1)S(1)} all-to-all(bf16[4,216,128]{2,1,0:T(8,128)(2,1)S(1)} %second.1), channel_id=1, replica_groups=mesh['segment'=2,'x'=4,'z'=4,'y'=4,'c'=2] {'z'}, dimensions={0} | all-to-all | bytes 442368 | tf_op jit(solution)/shard_map/all_to_all | solution.py:268
  103.9 14.3 %all_to_all.17 = bf16[16,216,128]{2,1,0:T(8,128)(2,1)S(1)} all-to-all(bf16[16,216,128]{2,1,0:T(8,128)(2,1)S(1)} %third.1), channel_id=1, replica_groups=mesh['segment'=2,'x'=4,'z'=4,'y'=4,'c'=2] {'x','y'}, dimensions={0} | all-to-all | bytes 1769472 | tf_op jit(solution)/shard_map/all_to_all | solution.py:268
  118.2 5.4 %collective-permute-start.10 = (bf16[3456,128]{1,0:T(8,128)(2,1)S(1)}, bf16[3456,128]{1,0:T(8,128)(2,1)S(1)}, u32[]{:S(2)}, u32[]{:S(2)}) collective-permute-start(bf16[3456,128]{1,0:T(8,128)(2,1)S(1)} %bitcast.9), channel_id=1, source_target_pairs={{0,1},{1,0},{2,3},{3,2},{4,5},{5,4},{6,7},{7,6},{8,9},{9,8},{10,11... | collective-permute-start | bytes 2654216 | tf_op jit(solution)/shard_map/ppermute | solution.py:272
  123.6 0.7 select_bitcast_fusion
  124.3 1.3 %collective-permute-done.10 = bf16[3456,128]{1,0:T(8,128)(2,1)S(1)} collective-permute-done((bf16[3456,128]{1,0:T(8,128)(2,1)S(1)}, bf16[3456,128]{1,0:T(8,128)(2,1)S(1)}, u32[]{:S(2)}, u32[]{:S(2)}) %collective-permute-start.10) | collective-permute-done | bytes 884768 | tf_op jit(solution)/shard_map/ppermute | solution.py:272
  125.6 2.2 %convert_multiply_fusion = f32[2,3456,128]{2,1,0:T(8,128)} fusion(bf16[1,3456,128]{2,1,0:T(8,128)(2,1)S(1)} %bitcast.11, bf16[1,3456,128]{2,1,0:T(8,128)(2,1)S(1)} %bitcast.10, pred[]{:T(512)S(6)} %eq.7), kind=kLoop, calls=%fused_computation | loop fusion | flops 4423680 | bytes 5308417 | tf_op jit(solution)/shard_map/mul | solution.py:380
  (36 shorter events, 1.1 us)
Async XLA Ops:
  0.6 1.2 copy-start
  1.9 0.9 copy-start.7
  2.8 6.8 %copy-start.1 = (bf16[4,8,128,128]{3,2,1,0:T(8,128)(2,1)S(1)}, bf16[4,8,128,128]{3,2,1,0:T(8,128)(2,1)}, u32[]{:S(2)}) copy-start(bf16[4,8,128,128]{3,2,1,0:T(8,128)(2,1)} %clip.5) | copy-start | bytes 3145732
  2.8 10.1 %copy-start.6 = (bf16[3,3,3,128,256]{4,3,2,1,0:T(8,128)(2,1)S(1)}, bf16[3,3,3,128,256]{4,3,2,1,0:T(8,128)(2,1)}, u32[]{:S(2)}) copy-start(bf16[3,3,3,128,256]{4,3,2,1,0:T(8,128)(2,1)} %weight.3) | copy-start | bytes 5308420
  2.8 10.1 %copy-start.8 = (bf16[2,4,64,128]{3,2,1,0:T(8,128)(2,1)S(1)}, bf16[2,4,64,128]{3,2,1,0:T(8,128)(2,1)}, u32[]{:S(2)}) copy-start(bf16[2,4,64,128]{3,2,1,0:T(8,128)(2,1)} %cot.3) | copy-start | bytes 393220
  2.8 10.1 %collective-permute-start = (bf16[5,128,128]{2,1,0:T(8,128)(2,1)S(1)}, bf16[5,128,128]{2,1,0:T(8,128)(2,1)S(1)}, u32[]{:S(2)}, u32[]{:S(2)}) collective-permute-start(bf16[5,128,128]{2,1,0:T(8,128)(2,1)S(1)} %edge.1), channel_id=1, source_target_pairs={{0,1},{1,2},{2,3},{3,4},{4,5},{5,6},{6,7},{8,9},{9,10},{10,11},{11... | collective-permute-start | bytes 491528 | tf_op jit(solution)/shard_map/ppermute | solution.py:282
  7.6 5.2 %collective-permute-start.1 = (bf16[2,1,64,128]{3,2,1,0:T(8,128)(2,1)S(1)}, bf16[2,1,64,128]{3,2,1,0:T(8,128)(2,1)S(1)}, u32[]{:S(2)}, u32[]{:S(2)}) collective-permute-start(bf16[2,1,64,128]{3,2,1,0:T(8,128)(2,1)S(1)} %slice.3), channel_id=1, source_target_pairs={{1,0},{2,1},{3,2},{4,3},{5,4},{6,5},{7,6},{9,8},{10,9},{11,10},{12... | collective-permute-start | bytes 98312 | tf_op jit(solution)/shard_map/ppermute | solution.py:282
  10.1 23.1 %copy-start.2 = (bf16[3,3,3,256,128]{4,3,2,1,0:T(8,128)(2,1)S(1)}, bf16[3,3,3,256,128]{4,3,2,1,0:T(8,128)(2,1)}, u32[]{:S(2)}) copy-start(bf16[3,3,3,256,128]{4,3,2,1,0:T(8,128)(2,1)} %weight.5) | copy-start | bytes 5308420
  15.1 23.4 %copy-start.13 = (bf16[4,64,384]{2,1,0:T(8,128)(2,1)}, bf16[4,64,384]{2,1,0:T(8,128)(2,1)S(1)}, u32[]{:S(2)}) copy-start(bf16[4,64,384]{2,1,0:T(8,128)(2,1)S(1)} %get-tuple-element.33.tops) | copy-start | bytes 589828
  15.1 7.3 %collective-permute-start.2 = (bf16[4,64,256]{2,1,0:T(8,128)(2,1)S(1)}, bf16[4,64,256]{2,1,0:T(8,128)(2,1)S(1)}, u32[]{:S(2)}, u32[]{:S(2)}) collective-permute-start(bf16[4,64,256]{2,1,0:T(8,128)(2,1)S(1)} %get-tuple-element.21), channel_id=1, source_target_pairs={{0,8},{8,16},{16,24},{24,32},{32,40},{40,48},{48,56},{56,64},{64,7... | collective-permute-start | bytes 393224 | tf_op jit(solution)/shard_map/ppermute | solution.py:277
  22.5 27.5 %collective-permute-start.8 = (bf16[2,9,128,128]{3,2,1,0:T(8,128)(2,1)}, bf16[2,9,128,128]{3,2,1,0:T(8,128)(2,1)}, u32[]{:S(2)}, u32[]{:S(2)}) collective-permute-start(bf16[2,9,128,128]{3,2,1,0:T(8,128)(2,1)} %get-tuple-element.31), channel_id=1, source_target_pairs={{128,8},{136,16},{144,24},{152,32},{160,40},{168,48},{176,56},{184... | collective-permute-start | bytes 1769480 | tf_op jit(solution)/shard_map/ppermute | solution.py:335
  24.0 6.1 %collective-permute-start.3 = (bf16[2,2,64,256]{3,2,1,0:T(8,128)(2,1)S(1)}, bf16[2,2,64,256]{3,2,1,0:T(8,128)(2,1)S(1)}, u32[]{:S(2)}, u32[]{:S(2)}) collective-permute-start(bf16[2,2,64,256]{3,2,1,0:T(8,128)(2,1)S(1)} %get-tuple-element.24), channel_id=1, source_target_pairs={{0,1},{1,2},{2,3},{3,4},{4,5},{5,6},{6,7},{8,9},{9,10},{10,11},{11... | collective-permute-start | bytes 393224 | tf_op jit(solution)/shard_map/ppermute | solution.py:282
  26.9 6.3 %collective-permute-start.4 = (bf16[2,2,64,256]{3,2,1,0:T(8,128)(2,1)S(1)}, bf16[2,2,64,256]{3,2,1,0:T(8,128)(2,1)S(1)}, u32[]{:S(2)}, u32[]{:S(2)}) collective-permute-start(bf16[2,2,64,256]{3,2,1,0:T(8,128)(2,1)S(1)} %get-tuple-element.25), channel_id=1, source_target_pairs={{1,0},{2,1},{3,2},{4,3},{5,4},{6,5},{7,6},{9,8},{10,9},{11,10},{12... | collective-permute-start | bytes 393224 | tf_op jit(solution)/shard_map/ppermute | solution.py:282
  28.8 26.2 %collective-permute-start.7 = (bf16[2,6,64,128]{3,2,1,0:T(8,128)(2,1)}, bf16[2,6,64,128]{3,2,1,0:T(8,128)(2,1)}, u32[]{:S(2)}, u32[]{:S(2)}) collective-permute-start(bf16[2,6,64,128]{3,2,1,0:T(8,128)(2,1)} %get-tuple-element.29.cot), channel_id=1, source_target_pairs={{8,0},{16,8},{24,16},{32,24},{40,32},{48,40},{56,48},{64,56},{72,6... | collective-permute-start | bytes 589832 | tf_op jit(solution)/shard_map/ppermute | solution.py:277
  33.2 3.8 %copy-start.9 = (bf16[2,2,64,256]{3,2,1,0:T(8,128)(2,1)}, bf16[2,2,64,256]{3,2,1,0:T(8,128)(2,1)S(1)}, u32[]{:S(2)}) copy-start(bf16[2,2,64,256]{3,2,1,0:T(8,128)(2,1)S(1)} %collective-permute-done.4.bottom) | copy-start | bytes 393220
  37.0 0.7 copy-start.3
  37.7 0.8 copy-start.11
  38.5 16.5 %collective-permute-start.5 = (bf16[2,6,64,128]{3,2,1,0:T(8,128)(2,1)}, bf16[2,6,64,128]{3,2,1,0:T(8,128)(2,1)}, u32[]{:S(2)}, u32[]{:S(2)}) collective-permute-start(bf16[2,6,64,128]{3,2,1,0:T(8,128)(2,1)} %get-tuple-element.27.gone), channel_id=1, source_target_pairs={{0,8},{8,16},{16,24},{24,32},{32,40},{40,48},{48,56},{56,64},{64,7... | collective-permute-start | bytes 589832 | tf_op jit(solution)/shard_map/ppermute | solution.py:277
  48.7 8.9 %collective-permute-start.6 = (bf16[2,6,64,128]{3,2,1,0:T(8,128)(2,1)}, bf16[2,6,64,128]{3,2,1,0:T(8,128)(2,1)}, u32[]{:S(2)}, u32[]{:S(2)}) collective-permute-start(bf16[2,6,64,128]{3,2,1,0:T(8,128)(2,1)} %get-tuple-element.28), channel_id=1, source_target_pairs={{8,0},{16,8},{24,16},{32,24},{40,32},{48,40},{56,48},{64,56},{72,6... | collective-permute-start | bytes 589832 | tf_op jit(solution)/shard_map/ppermute | solution.py:277
  50.0 1.0 copy-start.4
  50.9 0.9 copy-start.10
  51.9 0.9 copy-start.14
  52.8 4.8 %copy-start.12 = (f32[2,6,64,128]{3,2,1,0:T(8,128)S(1)}, f32[2,6,64,128]{3,2,1,0:T(8,128)}, u32[]{:S(2)}) copy-start(f32[2,6,64,128]{3,2,1,0:T(8,128)} %copy-done.11) | copy-start | bytes 1179652
  62.0 2.5 %collective-permute-start.9 = (bf16[3456,128]{1,0:T(8,128)(2,1)S(1)}, bf16[3456,128]{1,0:T(8,128)(2,1)S(1)}, u32[]{:S(2)}, u32[]{:S(2)}) collective-permute-start(bf16[3456,128]{1,0:T(8,128)(2,1)S(1)} %get-tuple-element.37), channel_id=1, source_target_pairs={{0,1},{1,0},{2,3},{3,2},{4,5},{5,4},{6,7},{7,6},{8,9},{9,8},{10,11... | collective-permute-start | bytes 2654216 | tf_op jit(solution)/shard_map/ppermute | solution.py:272
  89.3 34.3 %copy-start.5 = (bf16[2,4,64,256]{3,2,1,0:T(8,128)(2,1)S(1)}, bf16[2,4,64,256]{3,2,1,0:T(8,128)(2,1)}, u32[]{:S(2)}) copy-start(bf16[2,4,64,256]{3,2,1,0:T(8,128)(2,1)} %copy-done.3) | copy-start | bytes 786436
  118.2 7.4 %collective-permute-start.10 = (bf16[3456,128]{1,0:T(8,128)(2,1)S(1)}, bf16[3456,128]{1,0:T(8,128)(2,1)S(1)}, u32[]{:S(2)}, u32[]{:S(2)}) collective-permute-start(bf16[3456,128]{1,0:T(8,128)(2,1)S(1)} %bitcast.9), channel_id=1, source_target_pairs={{0,1},{1,0},{2,3},{3,2},{4,5},{5,4},{6,7},{7,6},{8,9},{9,8},{10,11... | collective-permute-start | bytes 2654216 | tf_op jit(solution)/shard_map/ppermute | solution.py:272

commit v5 on v4

--- a/solution.py
+++ b/solution.py
@@ -17,17 +17,16 @@
     return jax.ShapeDtypeStruct(dims, dtype)
 
 
-def on_chip(body, outs, name, smem=0, scratch=(), grant=10):
+def on_chip(body, outs, smem=0, scratch=(), grant=8, far=False):
     def call(*args):
         specs = [pl.BlockSpec(memory_space=pltpu.SMEM)] * smem
-        specs += [pl.BlockSpec(memory_space=pltpu.VMEM)] * (len(args) - smem)
+        specs += [pl.BlockSpec(memory_space=pl.ANY if far else pltpu.VMEM)] * (len(args) - smem)
         return pl.pallas_call(
             body,
             out_shape=outs,
             in_specs=specs,
-            out_specs=[pl.BlockSpec(memory_space=pltpu.VMEM)] * len(outs),
+            out_specs=[pl.BlockSpec(memory_space=pl.ANY if far else pltpu.VMEM)] * len(outs),
             scratch_shapes=list(scratch),
-            name=name,
             compiler_params=pltpu.CompilerParams(vmem_limit_bytes=grant * MIB),
         )(*args)
 
@@ -36,10 +35,6 @@
 
 def dot(left, right):
     return jnp.dot(left, right, preferred_element_type=F32)
-
-
-def dot_tn(left, right):
-    return lax.dot_general(left, right, (((0,), (0,)), ((), ())), preferred_element_type=F32)
 
 
 def dot_nt(left, right):
@@ -67,10 +62,24 @@
     stage[0:8, :] = jnp.zeros((8, stage.shape[1]), F32)
 
 
-def edge_body(clip, cot, down):
-    down[0:4] = clip[:, 7]
-    down[4, 0:64] = cot[0, 3]
-    down[4, 64:128] = cot[1, 3]
+def edge_body(seg_at, core_at, clip, cot, down, up, corner, tail, arrived):
+    copies = [
+        pltpu.make_async_copy(source, target, arrived.at[i])
+        for i, (source, target) in enumerate(
+            (
+                (clip.at[:, 7], down.at[0:4]),
+                (cot.at[0, 3], down.at[4, 0:64]),
+                (cot.at[1, 3], down.at[4, 64:128]),
+                (cot.at[:, 0], up),
+                (clip.at[2:4, 7], corner),
+                (clip.at[2:4], tail),
+            )
+        )
+    ]
+    for one in copies:
+        one.start()
+    for one in copies:
+        one.wait()
 
 
 def windows_body(clip, taps, stage):
@@ -90,7 +99,7 @@
 
 
 def encode_body(
-    clip, taps, above, weight, cot, below, lat1, part, own0, tail, tops, rows6, stage
+    taps, above, weight, cot, below, lat1, part, own0, tops, rows6, stage
 ):
     start_stage(stage)
     for f in range(4):
@@ -106,12 +115,10 @@
     part[...] = (conv(2, 0) + conv(3, 1)).astype(part.dtype).reshape(4, 64, 256)
     lat1[...] = (conv(0, 0) + conv(1, 1) + conv(2, 2)).astype(BF16).reshape(4, 64, 256)
     own0[...] = conv(0, 2).reshape(4, 64, 256)
-    tail[:, 0] = above[2:4]
-    tail[:, 1:9] = clip[2:4]
     rows6[0, 0] = above[4, 0:64]
     rows6[1, 0] = above[4, 64:128]
     rows6[:, 1:5] = cot[...]
-    rows6[:, 5:6] = below[...]
+    rows6[:, 5] = below[...]
 
 
 def join_body(own0, part, lat1, lat, down, up):
@@ -152,17 +159,17 @@
     behind[...] = own[...].astype(behind.dtype)
 
 
-def turned_body(seg_at, tail, tops, taps, lat, top, bottom, turned, btops, btaps, wide, stage):
+def turned_body(seg_at, tail, corner, tops, taps, lat, top, bottom, turned, btops, btaps, wide, stage):
     seg = seg_at[0]
 
     @pl.when(seg == 0)
     def _():
         start_stage(stage)
         for f in range(2):
-            btops[f] = clip_windows(tail[f, 0], stage)
+            btops[f] = clip_windows(corner[f], stage)
 
             def one(r, carry, f=f):
-                btaps[f, r] = clip_windows(tail[f, r + 1], stage)
+                btaps[f, r] = clip_windows(tail[f, r], stage)
                 return carry
 
             lax.fori_loop(0, 8, one, 0)
@@ -284,11 +291,9 @@
 
 def summed(own, send):
     got = to_core(send)
-    (wide,) = on_chip(halves_body, [shape((16, 216, 128), BF16)], "halves")(own, got)
-    (thin,) = on_chip(second_body, [shape((4, 216, 128), BF16)], "second")(
-        exchanged(wide, ("x", "y"))
-    )
-    (wide,) = on_chip(third_body, [shape((16, 216, 128), BF16)], "third")(exchanged(thin, "z"))
+    (wide,) = on_chip(halves_body, [shape((16, 216, 128), BF16)])(own, got)
+    (thin,) = on_chip(second_body, [shape((4, 216, 128), BF16)])(exchanged(wide, ("x", "y")))
+    (wide,) = on_chip(third_body, [shape((16, 216, 128), BF16)])(exchanged(thin, "z"))
     half = exchanged(wide, ("x", "y")).reshape(3456, 128)
     return half, to_core(half)
 
@@ -298,26 +303,40 @@
     core = lax.axis_index("c")
 
     stage = pltpu.VMEM((136, 128), F32)
-    (down,) = on_chip(edge_body, [shape((5, 128, 128), BF16)], "edge")(clip_frames, out_grad)
+    seg = seg.reshape(1)
+    core_at = core.reshape(1)
+    down, up, corner, tail = on_chip(
+        edge_body,
+        [
+            shape((5, 128, 128), BF16),
+            shape((2, 64, 128), BF16),
+            shape((2, 128, 128), BF16),
+            shape((2, 8, 128, 128), BF16),
+        ],
+        2,
+        [pltpu.SemaphoreType.DMA((6,))],
+        60,
+        True,
+    )(seg, core_at, clip_frames, out_grad)
     above = by_rows(down, 1)
-    below = by_rows(out_grad[:, 0:1], -1)
-    (taps,) = on_chip(windows_body, [shape((4, 8, 64, 384), BF16)], "windows", scratch=[stage])(
-        clip_frames
-    )
-    lat1, part, own0, tail, tops, cot = on_chip(
+    below = by_rows(up, -1)
+    pairs = [(16 + t - 1, t) for t in range(1, 16)]
+    tail = lax.ppermute(tail, ("segment", "x", "z"), pairs)
+    pairs = [(t * 8 + r, t * 8 + 8 + r + 1) for t in range(15) for r in range(7)]
+    corner = lax.ppermute(corner, ("x", "z", "y", "c"), pairs)
+    (taps,) = on_chip(windows_body, [shape((4, 8, 64, 384), BF16)], scratch=[stage])(clip_frames)
+    lat1, part, own0, tops, cot = on_chip(
         encode_body,
         [
             shape((4, 64, 256), BF16),
             shape((4, 64, 256), PART),
             shape((4, 64, 256), F32),
-            shape((2, 9, 128, 128), BF16),
             shape((4, 64, 384), BF16),
             shape((2, 6, 64, 128), BF16),
         ],
-        "encode",
         scratch=[stage],
         grant=16,
-    )(clip_frames, taps, above, enc_weight, out_grad, below)
+    )(taps, above, enc_weight, out_grad, below)
     part = by_frames(part, 1)
     later_cot = by_frames(cot, -1)
     latent, down, up = on_chip(
@@ -327,28 +346,22 @@
             shape((2, 2, 64, 256), BF16),
             shape((2, 2, 64, 256), BF16),
         ],
-        "join",
     )(own0, part, lat1)
     top = by_rows(down, 1)
     bottom = by_rows(up, -1)
-    tail, _ = lax.optimization_barrier((tail, down))
-    tail = lax.ppermute(tail, ("segment", "x", "z"), [(16 + t - 1, t) for t in range(1, 16)])
     rows6 = (2, 6, 64, 128)
     own_part, behind, gone = on_chip(
         decode_body,
         [shape(rows6, F32), shape(rows6, PART), shape(rows6, PART)],
-        "decode",
         scratch=[pltpu.VMEM((2, 8, 64, 768), BF16)],
         grant=14,
     )(latent, top, bottom, dec_weight)
     from_behind = by_frames(gone, 1)
     from_later = by_frames(behind, -1)
-    seg = seg.reshape(1)
     tail, lat, _ = lax.optimization_barrier((tail, latent, gone))
     (turned,) = on_chip(
         turned_body,
         [shape((15, 384, 256), BF16)],
-        "turned",
         1,
         [
             pltpu.VMEM((2, 64, 384), BF16),
@@ -357,7 +370,7 @@
             stage,
         ],
         16,
-    )(seg, tail, tops, taps, lat, top, bottom)
+    )(seg, tail, corner, tops, taps, lat, top, bottom)
     lat_grad, own, send = on_chip(
         grads_body,
         [
@@ -365,7 +378,6 @@
             shape((3456, 128), F32),
             shape((3456, 128), BF16),
         ],
-        "grads",
         2,
         [
             pltpu.VMEM((6912, 128), F32),
@@ -373,7 +385,7 @@
             pltpu.VMEM((4, 6, 64, 384), BF16),
         ],
         24,
-    )(seg, core.reshape(1), own_part, from_behind, gone, from_later, cot, later_cot, dec_weight, turned)
+    )(seg, core_at, own_part, from_behind, gone, from_later, cot, later_cot, dec_weight, turned)
     latent_pair = jnp.where(seg[0] == 0, lat_grad, latent)[None]
     half, other = summed(own, send)
     whole = jnp.where(core == 0, jnp.stack([half, other]), jnp.stack([other, half]))
@@ -384,6 +396,7 @@
 def solution(mesh):
     fine = Mesh(mesh.devices.reshape(2, 4, 4, 4, 2), ("segment", "x", "z", "y", "c"))
     cells = P(("x", "z"), ("y", "c"), None, None)
+
     return jax.shard_map(
         on_device,
         mesh=fine,

time: 128 us -> 147 us (1.15)
  the two profiles are of different devices: /device:TPU:1 before, /device:TPU:33 now
where the time goes in v5:
time: 147 us; the launch traced here: 146 us
  blocking collectives  53.2 us (36%)
  starting transfers between devices  40.6 us (28%)
  Pallas kernels  33.9 us (23%)
  waiting for transfers between devices  14.9 us (10%)
  other arithmetic  2.96 us (2%)
    all_to_all x3, blocking collectives, exchanged(): return lax.all_to_all(array, axes, 0, 0, tiled=True)  53.2 us
    pallas_call x10, Pallas kernels, call(): pl.pallas_call(body, out_shape=outs, in_specs=specs, out_specs=[pl.BlockS...  33.9 us
    ppermute x4, starting transfers between devices, by_frames(): return lax.ppermute(array, ('x', 'z'), pairs)  14.9 us
    ppermute x4, starting transfers between devices, by_rows(): return lax.ppermute(array, ('y', 'c'), pairs)  10.5 us
    ppermute x1, starting transfers between devices, on_device(): corner = lax.ppermute(corner, ('x', 'z', 'y', 'c'), pairs)  6.71 us
    ppermute x4, waiting for transfers between devices, by_rows(): return lax.ppermute(array, ('y', 'c'), pairs)  6 us
    ppermute x2, starting transfers between devices, to_core(): return lax.ppermute(array, 'c', [(0, 1), (1, 0)])  4.82 us
    ppermute x1, starting transfers between devices, on_device(): tail = lax.ppermute(tail, ('segment', 'x', 'z'), pairs)  3.57 us
  transfers between devices with their start and end apart: 12, of which 6 were waited for; matrix products, arithmetic and copies ran while one was open for 0% of the time, Pallas kernels for 4%

profile of v5, /device:TPU:33, one launch (start us, length us, event | category | flops | bytes accessed | tf_op | source)
XLA Modules:
  0.0 146.4 jit_solution(8692851890073883576)
XLA Ops:
  0.7 25.0 %shard_map.60 = (bf16[5,128,128]{2,1,0:T(8,128)(2,1)}, bf16[2,64,128]{2,1,0:T(8,128)(2,1)}, bf16[2,128,128]{2,1,0:T(8,128)(2,1)}, bf16[2,8,128,128]{3,2,1,0:T(8,128)(2,1)}) custom-call(s32[1]{0:T(128)} %bitcast.seg_at, s32[1]{0:T(128)} %bitcast.1.core_at, bf16[4,8,128,128]{3,2,1,0:T(8,128)(2,1)} %clip.3, bf16[2,4,64,128]{3,2,1,0:T(8,128)(2,1)} %cot.3), custom_call_target="tpu_custom_call" | custom-call | tf_op jit(solution)/shard_map/pallas_call | solution.py:24
  25.7 3.8 %collective-permute-start = (bf16[5,128,128]{2,1,0:T(8,128)(2,1)}, bf16[5,128,128]{2,1,0:T(8,128)(2,1)S(1)}, u32[]{:S(2)}, u32[]{:S(2)}) collective-permute-start(bf16[5,128,128]{2,1,0:T(8,128)(2,1)} %get-tuple-element.22), channel_id=1, source_target_pairs={{0,1},{1,2},{2,3},{3,4},{4,5},{5,6},{6,7},{8,9},{9,10},{10,11},{11... | collective-permute-start | bytes 491528 | tf_op jit(solution)/shard_map/ppermute | solution.py:289
  29.4 3.6 %collective-permute-start.8 = (bf16[2,8,128,128]{3,2,1,0:T(8,128)(2,1)}, bf16[2,8,128,128]{3,2,1,0:T(8,128)(2,1)S(1)}, u32[]{:S(2)}, u32[]{:S(2)}) collective-permute-start(bf16[2,8,128,128]{3,2,1,0:T(8,128)(2,1)} %get-tuple-element.34), channel_id=1, source_target_pairs={{128,8},{136,16},{144,24},{152,32},{160,40},{168,48},{176,56},{184... | collective-permute-start | bytes 1572872 | tf_op jit(solution)/shard_map/ppermute | solution.py:324
  33.0 1.9 %collective-permute-start.1 = (bf16[2,64,128]{2,1,0:T(8,128)(2,1)}, bf16[2,64,128]{2,1,0:T(8,128)(2,1)S(1)}, u32[]{:S(2)}, u32[]{:S(2)}) collective-permute-start(bf16[2,64,128]{2,1,0:T(8,128)(2,1)} %get-tuple-element.23), channel_id=1, source_target_pairs={{1,0},{2,1},{3,2},{4,3},{5,4},{6,5},{7,6},{9,8},{10,9},{11,10},{12... | collective-permute-start | bytes 98312 | tf_op jit(solution)/shard_map/ppermute | solution.py:289
  34.9 0.5 shard_map.59.taps
  35.5 3.0 %collective-permute-done.1.below = bf16[2,64,128]{2,1,0:T(8,128)(2,1)S(1)} collective-permute-done((bf16[2,64,128]{2,1,0:T(8,128)(2,1)}, bf16[2,64,128]{2,1,0:T(8,128)(2,1)S(1)}, u32[]{:S(2)}, u32[]{:S(2)}) %collective-permute-start.1) | collective-permute-done | bytes 32800 | tf_op jit(solution)/shard_map/ppermute | solution.py:289
  38.5 1.4 shard_map.61
  39.9 6.2 %collective-permute-start.2 = (bf16[4,64,256]{2,1,0:T(8,128)(2,1)S(1)}, bf16[4,64,256]{2,1,0:T(8,128)(2,1)S(1)}, u32[]{:S(2)}, u32[]{:S(2)}) collective-permute-start(bf16[4,64,256]{2,1,0:T(8,128)(2,1)S(1)} %get-tuple-element.25), channel_id=1, source_target_pairs={{0,8},{8,16},{16,24},{24,32},{32,40},{40,48},{48,56},{56,64},{64,7... | collective-permute-start | bytes 393224 | tf_op jit(solution)/shard_map/ppermute | solution.py:284
  46.1 3.5 %collective-permute-done.2.part = bf16[4,64,256]{2,1,0:T(8,128)(2,1)S(1)} collective-permute-done((bf16[4,64,256]{2,1,0:T(8,128)(2,1)S(1)}, bf16[4,64,256]{2,1,0:T(8,128)(2,1)S(1)}, u32[]{:S(2)}, u32[]{:S(2)}) %collective-permute-start.2) | collective-permute-done | bytes 131104 | tf_op jit(solution)/shard_map/ppermute | solution.py:284
  49.7 2.9 %collective-permute-start.3 = (bf16[2,2,64,256]{3,2,1,0:T(8,128)(2,1)S(1)}, bf16[2,2,64,256]{3,2,1,0:T(8,128)(2,1)S(1)}, u32[]{:S(2)}, u32[]{:S(2)}) collective-permute-start(bf16[2,2,64,256]{3,2,1,0:T(8,128)(2,1)S(1)} %get-tuple-element.28), channel_id=1, source_target_pairs={{0,1},{1,2},{2,3},{3,4},{4,5},{5,6},{6,7},{8,9},{9,10},{10,11},{11... | collective-permute-start | bytes 393224 | tf_op jit(solution)/shard_map/ppermute | solution.py:289
  52.7 1.9 %collective-permute-start.4 = (bf16[2,2,64,256]{3,2,1,0:T(8,128)(2,1)S(1)}, bf16[2,2,64,256]{3,2,1,0:T(8,128)(2,1)S(1)}, u32[]{:S(2)}, u32[]{:S(2)}) collective-permute-start(bf16[2,2,64,256]{3,2,1,0:T(8,128)(2,1)S(1)} %get-tuple-element.29), channel_id=1, source_target_pairs={{1,0},{2,1},{3,2},{4,3},{5,4},{6,5},{7,6},{9,8},{10,9},{11,10},{12... | collective-permute-start | bytes 393224 | tf_op jit(solution)/shard_map/ppermute | solution.py:289
  54.6 1.3 collective-permute-start.7
  55.9 3.0 %collective-permute-done.4.bottom = bf16[2,2,64,256]{3,2,1,0:T(8,128)(2,1)S(1)} collective-permute-done((bf16[2,2,64,256]{3,2,1,0:T(8,128)(2,1)S(1)}, bf16[2,2,64,256]{3,2,1,0:T(8,128)(2,1)S(1)}, u32[]{:S(2)}, u32[]{:S(2)}) %collective-permute-start.4) | collective-permute-done | bytes 131104 | tf_op jit(solution)/shard_map/ppermute | solution.py:289
  58.9 3.1 %shard_map.63 = (f32[2,6,64,128]{3,2,1,0:T(8,128)S(1)}, bf16[2,6,64,128]{3,2,1,0:T(8,128)(2,1)S(1)}, bf16[2,6,64,128]{3,2,1,0:T(8,128)(2,1)S(1)}) custom-call(bf16[2,4,64,256]{3,2,1,0:T(8,128)(2,1)S(1)} %get-tuple-element.38.lat, bf16[2,2,64,256]{3,2,1,0:T(8,128)(2,1)S(1)} %collective-permute-done.3.top, ...), custom_call_target="tpu_custom_call" | custom-call | tf_op jit(solution)/shard_map/pallas_call | solution.py:24
  62.1 6.1 %collective-permute-start.5 = (bf16[2,6,64,128]{3,2,1,0:T(8,128)(2,1)S(1)}, bf16[2,6,64,128]{3,2,1,0:T(8,128)(2,1)S(1)}, u32[]{:S(2)}, u32[]{:S(2)}) collective-permute-start(bf16[2,6,64,128]{3,2,1,0:T(8,128)(2,1)S(1)} %get-tuple-element.31.gone), channel_id=1, source_target_pairs={{0,8},{8,16},{16,24},{24,32},{32,40},{40,48},{48,56},{56,64},{64,7... | collective-permute-start | bytes 589832 | tf_op jit(solution)/shard_map/ppermute | solution.py:284
  68.2 1.3 collective-permute-start.6
  69.5 6.7 %collective-permute-start.9 = (bf16[2,128,128]{2,1,0:T(8,128)(2,1)S(1)}, bf16[2,128,128]{2,1,0:T(8,128)(2,1)S(1)}, u32[]{:S(2)}, u32[]{:S(2)}) collective-permute-start(bf16[2,128,128]{2,1,0:T(8,128)(2,1)S(1)} %copy-done.4), channel_id=1, source_target_pairs={{0,9},{1,10},{2,11},{3,12},{4,13},{5,14},{6,15},{8,17},{9,18},{10,... | collective-permute-start | bytes 196616 | tf_op jit(solution)/shard_map/ppermute | solution.py:326
  76.2 2.0 %collective-permute-done.9.corner = bf16[2,128,128]{2,1,0:T(8,128)(2,1)S(1)} collective-permute-done((bf16[2,128,128]{2,1,0:T(8,128)(2,1)S(1)}, bf16[2,128,128]{2,1,0:T(8,128)(2,1)S(1)}, u32[]{:S(2)}, u32[]{:S(2)}) %collective-permute-start.9) | collective-permute-done | bytes 65568 | tf_op jit(solution)/shard_map/ppermute | solution.py:326
  78.2 0.8 shard_map.64.turned
  79.1 2.5 %shard_map.65 = (bf16[2,4,64,256]{3,2,1,0:T(8,128)(2,1)S(1)}, f32[3456,128]{1,0:T(8,128)S(1)}, bf16[3456,128]{1,0:T(8,128)(2,1)S(1)}) custom-call(s32[1]{0:T(128)} %bitcast.seg_at, s32[1]{0:T(128)} %bitcast.1.core_at, f32[2,6,64,128]{3,2,1,0:T(8,128)S(1)} %get-tuple-element.30.own_part, bf16[2,6,64,128]{3,2,1,0:T(8,128)(2,1)S(1)} %collective-permute-done.5.from_behind, ...), custom_call_target="tpu_custom_call" | custom-call | tf_op jit(solution)/shard_map/pallas_call | solution.py:24
  81.7 0.9 collective-permute-start.10
  82.6 2.1 %collective-permute-done.10.got = bf16[3456,128]{1,0:T(8,128)(2,1)S(1)} collective-permute-done((bf16[3456,128]{1,0:T(8,128)(2,1)S(1)}, bf16[3456,128]{1,0:T(8,128)(2,1)S(1)}, u32[]{:S(2)}, u32[]{:S(2)}) %collective-permute-start.10) | collective-permute-done | bytes 884768 | tf_op jit(solution)/shard_map/ppermute | solution.py:279
  84.7 0.2 shard_map.66
  84.9 26.5 %all_to_all.15.got = bf16[16,216,128]{2,1,0:T(8,128)(2,1)S(1)} all-to-all(bf16[16,216,128]{2,1,0:T(8,128)(2,1)S(1)} %shard_map.66), channel_id=1, replica_groups=mesh['segment'=2,'x'=4,'z'=4,'y'=4,'c'=2] {'x','y'}, dimensions={0} | all-to-all | bytes 1769472 | tf_op jit(solution)/shard_map/all_to_all | solution.py:275
  111.4 0.1 shard_map.67
  111.5 10.4 %all_to_all.16.got = bf16[4,216,128]{2,1,0:T(8,128)(2,1)S(1)} all-to-all(bf16[4,216,128]{2,1,0:T(8,128)(2,1)S(1)} %shard_map.67), channel_id=1, replica_groups=mesh['segment'=2,'x'=4,'z'=4,'y'=4,'c'=2] {'z'}, dimensions={0} | all-to-all | bytes 442368 | tf_op jit(solution)/shard_map/all_to_all | solution.py:275
  122.0 0.1 shard_map.68
  122.0 16.2 %all_to_all.17 = bf16[16,216,128]{2,1,0:T(8,128)(2,1)S(1)} all-to-all(bf16[16,216,128]{2,1,0:T(8,128)(2,1)S(1)} %shard_map.68), channel_id=1, replica_groups=mesh['segment'=2,'x'=4,'z'=4,'y'=4,'c'=2] {'x','y'}, dimensions={0} | all-to-all | bytes 1769472 | tf_op jit(solution)/shard_map/all_to_all | solution.py:275
  138.2 3.9 %collective-permute-start.11 = (bf16[3456,128]{1,0:T(8,128)(2,1)S(1)}, bf16[3456,128]{1,0:T(8,128)(2,1)S(1)}, u32[]{:S(2)}, u32[]{:S(2)}) collective-permute-start(bf16[3456,128]{1,0:T(8,128)(2,1)S(1)} %bitcast.9), channel_id=1, source_target_pairs={{0,1},{1,0},{2,3},{3,2},{4,5},{5,4},{6,7},{7,6},{8,9},{9,8},{10,11... | collective-permute-start | bytes 2654216 | tf_op jit(solution)/shard_map/ppermute | solution.py:279
  142.1 0.7 select_bitcast_fusion
  142.9 1.3 collective-permute-done.11
  144.2 2.2 %convert_multiply_fusion = f32[2,3456,128]{2,1,0:T(8,128)} fusion(bf16[1,3456,128]{2,1,0:T(8,128)(2,1)S(1)} %bitcast.11, bf16[1,3456,128]{2,1,0:T(8,128)(2,1)S(1)} %bitcast.10, pred[]{:T(512)S(6)} %eq.7), kind=kLoop, calls=%fused_computation | loop fusion | flops 4423680 | bytes 5308417 | tf_op jit(solution)/shard_map/mul | solution.py:392
  (17 shorter events, 0.1 us)
Async XLA Ops:
  0.6 34.3 %copy-start.1 = (bf16[4,8,128,128]{3,2,1,0:T(8,128)(2,1)S(1)}, bf16[4,8,128,128]{3,2,1,0:T(8,128)(2,1)}, u32[]{:S(2)}) copy-start(bf16[4,8,128,128]{3,2,1,0:T(8,128)(2,1)} %clip.3) | copy-start | bytes 3145732
  0.6 37.8 %copy-start.2 = (bf16[3,3,3,128,256]{4,3,2,1,0:T(8,128)(2,1)S(1)}, bf16[3,3,3,128,256]{4,3,2,1,0:T(8,128)(2,1)}, u32[]{:S(2)}) copy-start(bf16[3,3,3,128,256]{4,3,2,1,0:T(8,128)(2,1)} %weight.3) | copy-start | bytes 5308420
  0.7 37.8 %copy-start.3 = (bf16[2,4,64,128]{3,2,1,0:T(8,128)(2,1)S(1)}, bf16[2,4,64,128]{3,2,1,0:T(8,128)(2,1)}, u32[]{:S(2)}) copy-start(bf16[2,4,64,128]{3,2,1,0:T(8,128)(2,1)} %cot.3) | copy-start | bytes 393220
  25.7 12.8 %collective-permute-start = (bf16[5,128,128]{2,1,0:T(8,128)(2,1)}, bf16[5,128,128]{2,1,0:T(8,128)(2,1)S(1)}, u32[]{:S(2)}, u32[]{:S(2)}) collective-permute-start(bf16[5,128,128]{2,1,0:T(8,128)(2,1)} %get-tuple-element.22), channel_id=1, source_target_pairs={{0,1},{1,2},{2,3},{3,4},{4,5},{5,6},{6,7},{8,9},{9,10},{10,11},{11... | collective-permute-start | bytes 491528 | tf_op jit(solution)/shard_map/ppermute | solution.py:289
  29.4 46.8 %collective-permute-start.8 = (bf16[2,8,128,128]{3,2,1,0:T(8,128)(2,1)}, bf16[2,8,128,128]{3,2,1,0:T(8,128)(2,1)S(1)}, u32[]{:S(2)}, u32[]{:S(2)}) collective-permute-start(bf16[2,8,128,128]{3,2,1,0:T(8,128)(2,1)} %get-tuple-element.34), channel_id=1, source_target_pairs={{128,8},{136,16},{144,24},{152,32},{160,40},{168,48},{176,56},{184... | collective-permute-start | bytes 1572872 | tf_op jit(solution)/shard_map/ppermute | solution.py:324
  33.0 5.4 %collective-permute-start.1 = (bf16[2,64,128]{2,1,0:T(8,128)(2,1)}, bf16[2,64,128]{2,1,0:T(8,128)(2,1)S(1)}, u32[]{:S(2)}, u32[]{:S(2)}) collective-permute-start(bf16[2,64,128]{2,1,0:T(8,128)(2,1)} %get-tuple-element.23), channel_id=1, source_target_pairs={{1,0},{2,1},{3,2},{4,3},{5,4},{6,5},{7,6},{9,8},{10,9},{11,10},{12... | collective-permute-start | bytes 98312 | tf_op jit(solution)/shard_map/ppermute | solution.py:289
  35.5 23.5 %copy-start = (bf16[3,3,3,256,128]{4,3,2,1,0:T(8,128)(2,1)S(1)}, bf16[3,3,3,256,128]{4,3,2,1,0:T(8,128)(2,1)}, u32[]{:S(2)}) copy-start(bf16[3,3,3,256,128]{4,3,2,1,0:T(8,128)(2,1)} %weight.5) | copy-start | bytes 5308420
  39.9 29.6 %copy-start.4 = (bf16[2,128,128]{2,1,0:T(8,128)(2,1)S(1)}, bf16[2,128,128]{2,1,0:T(8,128)(2,1)}, u32[]{:S(2)}) copy-start(bf16[2,128,128]{2,1,0:T(8,128)(2,1)} %get-tuple-element.36) | copy-start | bytes 196612
  39.9 9.8 %collective-permute-start.2 = (bf16[4,64,256]{2,1,0:T(8,128)(2,1)S(1)}, bf16[4,64,256]{2,1,0:T(8,128)(2,1)S(1)}, u32[]{:S(2)}, u32[]{:S(2)}) collective-permute-start(bf16[4,64,256]{2,1,0:T(8,128)(2,1)S(1)} %get-tuple-element.25), channel_id=1, source_target_pairs={{0,8},{8,16},{16,24},{24,32},{32,40},{40,48},{48,56},{56,64},{64,7... | collective-permute-start | bytes 393224 | tf_op jit(solution)/shard_map/ppermute | solution.py:284
  49.7 6.2 %collective-permute-start.3 = (bf16[2,2,64,256]{3,2,1,0:T(8,128)(2,1)S(1)}, bf16[2,2,64,256]{3,2,1,0:T(8,128)(2,1)S(1)}, u32[]{:S(2)}, u32[]{:S(2)}) collective-permute-start(bf16[2,2,64,256]{3,2,1,0:T(8,128)(2,1)S(1)} %get-tuple-element.28), channel_id=1, source_target_pairs={{0,1},{1,2},{2,3},{3,4},{4,5},{5,6},{6,7},{8,9},{9,10},{10,11},{11... | collective-permute-start | bytes 393224 | tf_op jit(solution)/shard_map/ppermute | solution.py:289
  52.7 6.3 %collective-permute-start.4 = (bf16[2,2,64,256]{3,2,1,0:T(8,128)(2,1)S(1)}, bf16[2,2,64,256]{3,2,1,0:T(8,128)(2,1)S(1)}, u32[]{:S(2)}, u32[]{:S(2)}) collective-permute-start(bf16[2,2,64,256]{3,2,1,0:T(8,128)(2,1)S(1)} %get-tuple-element.29), channel_id=1, source_target_pairs={{1,0},{2,1},{3,2},{4,3},{5,4},{6,5},{7,6},{9,8},{10,9},{11,10},{12... | collective-permute-start | bytes 393224 | tf_op jit(solution)/shard_map/ppermute | solution.py:289
  54.6 24.5 %collective-permute-start.7 = (bf16[2,6,64,128]{3,2,1,0:T(8,128)(2,1)S(1)}, bf16[2,6,64,128]{3,2,1,0:T(8,128)(2,1)S(1)}, u32[]{:S(2)}, u32[]{:S(2)}) collective-permute-start(bf16[2,6,64,128]{3,2,1,0:T(8,128)(2,1)S(1)} %get-tuple-element.33.cot), channel_id=1, source_target_pairs={{8,0},{16,8},{24,16},{32,24},{40,32},{48,40},{56,48},{64,56},{72,6... | collective-permute-start | bytes 589832 | tf_op jit(solution)/shard_map/ppermute | solution.py:284
  62.1 17.0 %collective-permute-start.5 = (bf16[2,6,64,128]{3,2,1,0:T(8,128)(2,1)S(1)}, bf16[2,6,64,128]{3,2,1,0:T(8,128)(2,1)S(1)}, u32[]{:S(2)}, u32[]{:S(2)}) collective-permute-start(bf16[2,6,64,128]{3,2,1,0:T(8,128)(2,1)S(1)} %get-tuple-element.31.gone), channel_id=1, source_target_pairs={{0,8},{8,16},{16,24},{24,32},{32,40},{40,48},{48,56},{56,64},{64,7... | collective-permute-start | bytes 589832 | tf_op jit(solution)/shard_map/ppermute | solution.py:284
  68.2 10.9 %collective-permute-start.6 = (bf16[2,6,64,128]{3,2,1,0:T(8,128)(2,1)S(1)}, bf16[2,6,64,128]{3,2,1,0:T(8,128)(2,1)S(1)}, u32[]{:S(2)}, u32[]{:S(2)}) collective-permute-start(bf16[2,6,64,128]{3,2,1,0:T(8,128)(2,1)S(1)} %get-tuple-element.32), channel_id=1, source_target_pairs={{8,0},{16,8},{24,16},{32,24},{40,32},{48,40},{56,48},{64,56},{72,6... | collective-permute-start | bytes 589832 | tf_op jit(solution)/shard_map/ppermute | solution.py:284
  69.5 8.7 %collective-permute-start.9 = (bf16[2,128,128]{2,1,0:T(8,128)(2,1)S(1)}, bf16[2,128,128]{2,1,0:T(8,128)(2,1)S(1)}, u32[]{:S(2)}, u32[]{:S(2)}) collective-permute-start(bf16[2,128,128]{2,1,0:T(8,128)(2,1)S(1)} %copy-done.4), channel_id=1, source_target_pairs={{0,9},{1,10},{2,11},{3,12},{4,13},{5,14},{6,15},{8,17},{9,18},{10,... | collective-permute-start | bytes 196616 | tf_op jit(solution)/shard_map/ppermute | solution.py:326
  81.7 3.0 %collective-permute-start.10 = (bf16[3456,128]{1,0:T(8,128)(2,1)S(1)}, bf16[3456,128]{1,0:T(8,128)(2,1)S(1)}, u32[]{:S(2)}, u32[]{:S(2)}) collective-permute-start(bf16[3456,128]{1,0:T(8,128)(2,1)S(1)} %get-tuple-element.41), channel_id=1, source_target_pairs={{0,1},{1,0},{2,3},{3,2},{4,5},{5,4},{6,7},{7,6},{8,9},{9,8},{10,11... | collective-permute-start | bytes 2654216 | tf_op jit(solution)/shard_map/ppermute | solution.py:279
  138.2 5.9 %collective-permute-start.11 = (bf16[3456,128]{1,0:T(8,128)(2,1)S(1)}, bf16[3456,128]{1,0:T(8,128)(2,1)S(1)}, u32[]{:S(2)}, u32[]{:S(2)}) collective-permute-start(bf16[3456,128]{1,0:T(8,128)(2,1)S(1)} %bitcast.9), channel_id=1, source_target_pairs={{0,1},{1,0},{2,3},{3,2},{4,5},{5,4},{6,7},{7,6},{8,9},{9,8},{10,11... | collective-permute-start | bytes 2654216 | tf_op jit(solution)/shard_map/ppermute | solution.py:279

commit v6 on v5

--- a/solution.py
+++ b/solution.py
@@ -25,7 +25,7 @@
             body,
             out_shape=outs,
             in_specs=specs,
-            out_specs=[pl.BlockSpec(memory_space=pl.ANY if far else pltpu.VMEM)] * len(outs),
+            out_specs=[pl.BlockSpec(memory_space=pltpu.VMEM)] * len(outs),
             scratch_shapes=list(scratch),
             compiler_params=pltpu.CompilerParams(vmem_limit_bytes=grant * MIB),
         )(*args)
@@ -62,7 +62,7 @@
     stage[0:8, :] = jnp.zeros((8, stage.shape[1]), F32)
 
 
-def edge_body(seg_at, core_at, clip, cot, down, up, corner, tail, arrived):
+def edge_body(seg_at, core_at, clip, cot, down, up, tail, arrived):
     copies = [
         pltpu.make_async_copy(source, target, arrived.at[i])
         for i, (source, target) in enumerate(
@@ -71,7 +71,6 @@
                 (cot.at[0, 3], down.at[4, 0:64]),
                 (cot.at[1, 3], down.at[4, 64:128]),
                 (cot.at[:, 0], up),
-                (clip.at[2:4, 7], corner),
                 (clip.at[2:4], tail),
             )
         )
@@ -121,10 +120,12 @@
     rows6[:, 5] = below[...]
 
 
-def join_body(own0, part, lat1, lat, down, up):
+def join_body(own0, part, lat1, tail, lat, down, up):
     lat[0] = (own0[...] + part[...].astype(F32)).astype(BF16)
     lat[1] = lat1[...]
-    down[...] = lat[:, 2:4]
+    down[:, 0:2] = lat[:, 2:4]
+    down[:, 2, :, 0:128] = tail[:, 7, 0:64]
+    down[:, 2, :, 128:256] = tail[:, 7, 64:128]
     up[...] = lat[:, 0:2]
 
 
@@ -159,14 +160,15 @@
     behind[...] = own[...].astype(behind.dtype)
 
 
-def turned_body(seg_at, tail, corner, tops, taps, lat, top, bottom, turned, btops, btaps, wide, stage):
+def turned_body(seg_at, tail, tops, taps, lat, top, bottom, turned, btops, btaps, wide, stage):
     seg = seg_at[0]
 
     @pl.when(seg == 0)
     def _():
         start_stage(stage)
         for f in range(2):
-            btops[f] = clip_windows(corner[f], stage)
+            corner = jnp.concatenate([top[f, 2, :, 0:128], top[f, 2, :, 128:256]], axis=0)
+            btops[f] = clip_windows(corner, stage)
 
             def one(r, carry, f=f):
                 btaps[f, r] = clip_windows(tail[f, r], stage)
@@ -305,16 +307,15 @@
     stage = pltpu.VMEM((136, 128), F32)
     seg = seg.reshape(1)
     core_at = core.reshape(1)
-    down, up, corner, tail = on_chip(
+    down, up, tail = on_chip(
         edge_body,
         [
             shape((5, 128, 128), BF16),
             shape((2, 64, 128), BF16),
-            shape((2, 128, 128), BF16),
             shape((2, 8, 128, 128), BF16),
         ],
         2,
-        [pltpu.SemaphoreType.DMA((6,))],
+        [pltpu.SemaphoreType.DMA((5,))],
         60,
         True,
     )(seg, core_at, clip_frames, out_grad)
@@ -322,8 +323,6 @@
     below = by_rows(up, -1)
     pairs = [(16 + t - 1, t) for t in range(1, 16)]
     tail = lax.ppermute(tail, ("segment", "x", "z"), pairs)
-    pairs = [(t * 8 + r, t * 8 + 8 + r + 1) for t in range(15) for r in range(7)]
-    corner = lax.ppermute(corner, ("x", "z", "y", "c"), pairs)
     (taps,) = on_chip(windows_body, [shape((4, 8, 64, 384), BF16)], scratch=[stage])(clip_frames)
     lat1, part, own0, tops, cot = on_chip(
         encode_body,
@@ -343,10 +342,10 @@
         join_body,
         [
             shape((2, 4, 64, 256), BF16),
+            shape((2, 3, 64, 256), BF16),
             shape((2, 2, 64, 256), BF16),
-            shape((2, 2, 64, 256), BF16),
-        ],
-    )(own0, part, lat1)
+        ],
+    )(own0, part, lat1, tail)
     top = by_rows(down, 1)
     bottom = by_rows(up, -1)
     rows6 = (2, 6, 64, 128)
@@ -370,7 +369,7 @@
             stage,
         ],
         16,
-    )(seg, tail, corner, tops, taps, lat, top, bottom)
+    )(seg, tail, tops, taps, lat, top, bottom)
     lat_grad, own, send = on_chip(
         grads_body,
         [

time: 147 us -> 122 us (0.83)
  the two profiles are of different devices: /device:TPU:33 before, /device:TPU:1 now
where the time goes in v6:
time: 122 us
  blocking collectives  52.8 us (43%)
  starting transfers between devices  33.8 us (28%)
  waiting for transfers between devices  19.4 us (16%)
  Pallas kernels  12 us (10%)
  other arithmetic  2.96 us (2%)
    all_to_all x3, blocking collectives, exchanged(): return lax.all_to_all(array, axes, 0, 0, tiled=True)  52.8 us
    ppermute x4, starting transfers between devices, by_frames(): return lax.ppermute(array, ('x', 'z'), pairs)  16.6 us
    pallas_call x10, Pallas kernels, call(): pl.pallas_call(body, out_shape=outs, in_specs=specs, out_specs=[pl.BlockS...  12 us
    ppermute x4, starting transfers between devices, by_rows(): return lax.ppermute(array, ('y', 'c'), pairs)  11.4 us
    ppermute x4, waiting for transfers between devices, by_frames(): return lax.ppermute(array, ('x', 'z'), pairs)  9.66 us
    ppermute x4, waiting for transfers between devices, by_rows(): return lax.ppermute(array, ('y', 'c'), pairs)  6.01 us
    ppermute x2, starting transfers between devices, to_core(): return lax.ppermute(array, 'c', [(0, 1), (1, 0)])  5.04 us
    ppermute x2, waiting for transfers between devices, to_core(): return lax.ppermute(array, 'c', [(0, 1), (1, 0)])  3.73 us
  transfers between devices with their start and end apart: 11, of which 7 were waited for; matrix products, arithmetic and copies ran while one was open for 1% of the time, Pallas kernels for 5%

profile of v6, /device:TPU:1, one launch (start us, length us, event | category | flops | bytes accessed | tf_op | source)
XLA Modules:
  0.0 121.8 jit_solution(4960523566620458938)
XLA Ops:
  0.7 2.2 %shard_map.60 = (bf16[5,128,128]{2,1,0:T(8,128)(2,1)}, bf16[2,64,128]{2,1,0:T(8,128)(2,1)}, bf16[2,8,128,128]{3,2,1,0:T(8,128)(2,1)}) custom-call(s32[1]{0:T(128)} %bitcast.seg_at, s32[1]{0:T(128)} %bitcast.1.core_at, bf16[4,8,128,128]{3,2,1,0:T(8,128)(2,1)} %clip.3, bf16[2,4,64,128]{3,2,1,0:T(8,128)(2,1)} %cot.3), custom_call_target="tpu_custom_call" | custom-call | tf_op jit(solution)/shard_map/pallas_call | solution.py:24
  2.9 0.7 collective-permute-start.3
  3.6 4.6 %collective-permute-start = (bf16[5,128,128]{2,1,0:T(8,128)(2,1)}, bf16[5,128,128]{2,1,0:T(8,128)(2,1)S(1)}, u32[]{:S(2)}, u32[]{:S(2)}) collective-permute-start(bf16[5,128,128]{2,1,0:T(8,128)(2,1)} %get-tuple-element.21), channel_id=1, source_target_pairs={{0,1},{1,2},{2,3},{3,4},{4,5},{5,6},{6,7},{8,9},{9,10},{10,11},{11... | collective-permute-start | bytes 491528 | tf_op jit(solution)/shard_map/ppermute | solution.py:291
  8.2 1.9 %collective-permute-start.1 = (bf16[2,64,128]{2,1,0:T(8,128)(2,1)}, bf16[2,64,128]{2,1,0:T(8,128)(2,1)S(1)}, u32[]{:S(2)}, u32[]{:S(2)}) collective-permute-start(bf16[2,64,128]{2,1,0:T(8,128)(2,1)} %get-tuple-element.22), channel_id=1, source_target_pairs={{1,0},{2,1},{3,2},{4,3},{5,4},{6,5},{7,6},{9,8},{10,9},{11,10},{12... | collective-permute-start | bytes 98312 | tf_op jit(solution)/shard_map/ppermute | solution.py:291
  10.1 0.5 shard_map.59.taps
  10.7 3.0 %collective-permute-done.1.below = bf16[2,64,128]{2,1,0:T(8,128)(2,1)S(1)} collective-permute-done((bf16[2,64,128]{2,1,0:T(8,128)(2,1)}, bf16[2,64,128]{2,1,0:T(8,128)(2,1)S(1)}, u32[]{:S(2)}, u32[]{:S(2)}) %collective-permute-start.1) | collective-permute-done | bytes 32800 | tf_op jit(solution)/shard_map/ppermute | solution.py:291
  13.6 1.4 %shard_map.61 = (bf16[4,64,256]{2,1,0:T(8,128)(2,1)S(1)}, bf16[4,64,256]{2,1,0:T(8,128)(2,1)S(1)}, f32[4,64,256]{2,1,0:T(8,128)S(1)}, bf16[4,64,384]{2,1,0:T(8,128)(2,1)S(1)}, bf16[2,6,64,128]{3,2,1,0:T(8,128)(2,1)S(1)}) custom-call(bf16[4,8,64,384]{3,2,1,0:T(8,128)(2,1)S(1)} %shard_map.59.taps, bf16[5,128,128]{2,1,0:T(8,128)(2,1)S(1)} %collective-permute-done.above, ...), custom_call_target="tpu_custom_call" | custom-call | tf_op jit(solution)/shard_map/pallas_call | solution.py:24
  15.0 5.8 %collective-permute-start.2 = (bf16[4,64,256]{2,1,0:T(8,128)(2,1)S(1)}, bf16[4,64,256]{2,1,0:T(8,128)(2,1)S(1)}, u32[]{:S(2)}, u32[]{:S(2)}) collective-permute-start(bf16[4,64,256]{2,1,0:T(8,128)(2,1)S(1)} %get-tuple-element.24), channel_id=1, source_target_pairs={{0,8},{8,16},{16,24},{24,32},{32,40},{40,48},{48,56},{56,64},{64,7... | collective-permute-start | bytes 393224 | tf_op jit(solution)/shard_map/ppermute | solution.py:286
  20.8 1.9 %collective-permute-done.2.part = bf16[4,64,256]{2,1,0:T(8,128)(2,1)S(1)} collective-permute-done((bf16[4,64,256]{2,1,0:T(8,128)(2,1)S(1)}, bf16[4,64,256]{2,1,0:T(8,128)(2,1)S(1)}, u32[]{:S(2)}, u32[]{:S(2)}) %collective-permute-start.2) | collective-permute-done | bytes 131104 | tf_op jit(solution)/shard_map/ppermute | solution.py:286
  22.8 3.0 %collective-permute-start.4 = (bf16[2,3,64,256]{3,2,1,0:T(8,128)(2,1)S(1)}, bf16[2,3,64,256]{3,2,1,0:T(8,128)(2,1)S(1)}, u32[]{:S(2)}, u32[]{:S(2)}) collective-permute-start(bf16[2,3,64,256]{3,2,1,0:T(8,128)(2,1)S(1)} %get-tuple-element.28), channel_id=1, source_target_pairs={{0,1},{1,2},{2,3},{3,4},{4,5},{5,6},{6,7},{8,9},{9,10},{10,11},{11... | collective-permute-start | bytes 589832 | tf_op jit(solution)/shard_map/ppermute | solution.py:291
  25.9 1.9 %collective-permute-start.5 = (bf16[2,2,64,256]{3,2,1,0:T(8,128)(2,1)S(1)}, bf16[2,2,64,256]{3,2,1,0:T(8,128)(2,1)S(1)}, u32[]{:S(2)}, u32[]{:S(2)}) collective-permute-start(bf16[2,2,64,256]{3,2,1,0:T(8,128)(2,1)S(1)} %get-tuple-element.29), channel_id=1, source_target_pairs={{1,0},{2,1},{3,2},{4,3},{5,4},{6,5},{7,6},{9,8},{10,9},{11,10},{12... | collective-permute-start | bytes 393224 | tf_op jit(solution)/shard_map/ppermute | solution.py:291
  27.8 1.3 %collective-permute-start.8 = (bf16[2,6,64,128]{3,2,1,0:T(8,128)(2,1)S(1)}, bf16[2,6,64,128]{3,2,1,0:T(8,128)(2,1)S(1)}, u32[]{:S(2)}, u32[]{:S(2)}) collective-permute-start(bf16[2,6,64,128]{3,2,1,0:T(8,128)(2,1)S(1)} %get-tuple-element.33.cot), channel_id=1, source_target_pairs={{8,0},{16,8},{24,16},{32,24},{40,32},{48,40},{56,48},{64,56},{72,6... | collective-permute-start | bytes 589832 | tf_op jit(solution)/shard_map/ppermute | solution.py:286
  29.1 3.1 %collective-permute-done.5.bottom = bf16[2,2,64,256]{3,2,1,0:T(8,128)(2,1)S(1)} collective-permute-done((bf16[2,2,64,256]{3,2,1,0:T(8,128)(2,1)S(1)}, bf16[2,2,64,256]{3,2,1,0:T(8,128)(2,1)S(1)}, u32[]{:S(2)}, u32[]{:S(2)}) %collective-permute-start.5) | collective-permute-done | bytes 131104 | tf_op jit(solution)/shard_map/ppermute | solution.py:291
  32.2 3.1 %shard_map.63 = (f32[2,6,64,128]{3,2,1,0:T(8,128)S(1)}, bf16[2,6,64,128]{3,2,1,0:T(8,128)(2,1)S(1)}, bf16[2,6,64,128]{3,2,1,0:T(8,128)(2,1)S(1)}) custom-call(bf16[2,4,64,256]{3,2,1,0:T(8,128)(2,1)S(1)} %get-tuple-element.36.lat, bf16[2,3,64,256]{3,2,1,0:T(8,128)(2,1)S(1)} %collective-permute-done.4.top, ...), custom_call_target="tpu_custom_call" | custom-call | tf_op jit(solution)/shard_map/pallas_call | solution.py:24
  35.3 8.2 %collective-permute-start.6 = (bf16[2,6,64,128]{3,2,1,0:T(8,128)(2,1)S(1)}, bf16[2,6,64,128]{3,2,1,0:T(8,128)(2,1)S(1)}, u32[]{:S(2)}, u32[]{:S(2)}) collective-permute-start(bf16[2,6,64,128]{3,2,1,0:T(8,128)(2,1)S(1)} %get-tuple-element.31.gone), channel_id=1, source_target_pairs={{0,8},{8,16},{16,24},{24,32},{32,40},{40,48},{48,56},{56,64},{64,7... | collective-permute-start | bytes 589832 | tf_op jit(solution)/shard_map/ppermute | solution.py:286
  43.5 1.3 %collective-permute-start.7 = (bf16[2,6,64,128]{3,2,1,0:T(8,128)(2,1)S(1)}, bf16[2,6,64,128]{3,2,1,0:T(8,128)(2,1)S(1)}, u32[]{:S(2)}, u32[]{:S(2)}) collective-permute-start(bf16[2,6,64,128]{3,2,1,0:T(8,128)(2,1)S(1)} %get-tuple-element.32), channel_id=1, source_target_pairs={{8,0},{16,8},{24,16},{32,24},{40,32},{48,40},{56,48},{64,56},{72,6... | collective-permute-start | bytes 589832 | tf_op jit(solution)/shard_map/ppermute | solution.py:286
  44.8 1.1 shard_map.64.turned
  46.0 0.2 collective-permute-done.6.from_behind
  46.1 7.6 %collective-permute-done.7.from_later = bf16[2,6,64,128]{3,2,1,0:T(8,128)(2,1)S(1)} collective-permute-done((bf16[2,6,64,128]{3,2,1,0:T(8,128)(2,1)S(1)}, bf16[2,6,64,128]{3,2,1,0:T(8,128)(2,1)S(1)}, u32[]{:S(2)}, u32[]{:S(2)}) %collective-permute-start.7) | collective-permute-done | bytes 196640 | tf_op jit(solution)/shard_map/ppermute | solution.py:286
  53.7 3.2 %shard_map.65 = (bf16[2,4,64,256]{3,2,1,0:T(8,128)(2,1)S(1)}, f32[3456,128]{1,0:T(8,128)S(1)}, bf16[3456,128]{1,0:T(8,128)(2,1)S(1)}) custom-call(s32[1]{0:T(128)} %bitcast.seg_at, s32[1]{0:T(128)} %bitcast.1.core_at, f32[2,6,64,128]{3,2,1,0:T(8,128)S(1)} %get-tuple-element.30.own_part, bf16[2,6,64,128]{3,2,1,0:T(8,128)(2,1)S(1)} %collective-permute-done.6.from_behind, ...), custom_call_target="tpu_custom_call" | custom-call | tf_op jit(solution)/shard_map/pallas_call | solution.py:24
  56.8 0.1 collective-permute-start.9
  57.0 2.4 %collective-permute-done.9.got = bf16[3456,128]{1,0:T(8,128)(2,1)S(1)} collective-permute-done((bf16[3456,128]{1,0:T(8,128)(2,1)S(1)}, bf16[3456,128]{1,0:T(8,128)(2,1)S(1)}, u32[]{:S(2)}, u32[]{:S(2)}) %collective-permute-start.9) | collective-permute-done | bytes 884768 | tf_op jit(solution)/shard_map/ppermute | solution.py:281
  59.4 0.2 shard_map.66
  59.6 21.9 %all_to_all.15.got = bf16[16,216,128]{2,1,0:T(8,128)(2,1)S(1)} all-to-all(bf16[16,216,128]{2,1,0:T(8,128)(2,1)S(1)} %shard_map.66), channel_id=1, replica_groups=mesh['segment'=2,'x'=4,'z'=4,'y'=4,'c'=2] {'x','y'}, dimensions={0} | all-to-all | bytes 1769472 | tf_op jit(solution)/shard_map/all_to_all | solution.py:277
  81.5 0.1 shard_map.67
  81.6 16.1 %all_to_all.16.got = bf16[4,216,128]{2,1,0:T(8,128)(2,1)S(1)} all-to-all(bf16[4,216,128]{2,1,0:T(8,128)(2,1)S(1)} %shard_map.67), channel_id=1, replica_groups=mesh['segment'=2,'x'=4,'z'=4,'y'=4,'c'=2] {'z'}, dimensions={0} | all-to-all | bytes 442368 | tf_op jit(solution)/shard_map/all_to_all | solution.py:277
  97.7 0.1 shard_map.68
  97.7 14.9 %all_to_all.17 = bf16[16,216,128]{2,1,0:T(8,128)(2,1)S(1)} all-to-all(bf16[16,216,128]{2,1,0:T(8,128)(2,1)S(1)} %shard_map.68), channel_id=1, replica_groups=mesh['segment'=2,'x'=4,'z'=4,'y'=4,'c'=2] {'x','y'}, dimensions={0} | all-to-all | bytes 1769472 | tf_op jit(solution)/shard_map/all_to_all | solution.py:277
  112.6 4.9 %collective-permute-start.10 = (bf16[3456,128]{1,0:T(8,128)(2,1)S(1)}, bf16[3456,128]{1,0:T(8,128)(2,1)S(1)}, u32[]{:S(2)}, u32[]{:S(2)}) collective-permute-start(bf16[3456,128]{1,0:T(8,128)(2,1)S(1)} %bitcast.9), channel_id=1, source_target_pairs={{0,1},{1,0},{2,3},{3,2},{4,5},{5,4},{6,7},{7,6},{8,9},{9,8},{10,11... | collective-permute-start | bytes 2654216 | tf_op jit(solution)/shard_map/ppermute | solution.py:281
  117.6 0.7 select_bitcast_fusion
  118.3 1.3 %collective-permute-done.10 = bf16[3456,128]{1,0:T(8,128)(2,1)S(1)} collective-permute-done((bf16[3456,128]{1,0:T(8,128)(2,1)S(1)}, bf16[3456,128]{1,0:T(8,128)(2,1)S(1)}, u32[]{:S(2)}, u32[]{:S(2)}) %collective-permute-start.10) | collective-permute-done | bytes 884768 | tf_op jit(solution)/shard_map/ppermute | solution.py:281
  119.6 2.2 %convert_multiply_fusion = f32[2,3456,128]{2,1,0:T(8,128)} fusion(bf16[1,3456,128]{2,1,0:T(8,128)(2,1)S(1)} %bitcast.11, bf16[1,3456,128]{2,1,0:T(8,128)(2,1)S(1)} %bitcast.10, pred[]{:T(512)S(6)} %eq.7), kind=kLoop, calls=%fused_computation | loop fusion | flops 4423680 | bytes 5308417 | tf_op jit(solution)/shard_map/mul | solution.py:391
  (13 shorter events, 0.1 us)
Async XLA Ops:
  0.6 9.5 %copy-start.1 = (bf16[4,8,128,128]{3,2,1,0:T(8,128)(2,1)S(1)}, bf16[4,8,128,128]{3,2,1,0:T(8,128)(2,1)}, u32[]{:S(2)}) copy-start(bf16[4,8,128,128]{3,2,1,0:T(8,128)(2,1)} %clip.3) | copy-start | bytes 3145732
  0.6 13.0 %copy-start.2 = (bf16[3,3,3,128,256]{4,3,2,1,0:T(8,128)(2,1)S(1)}, bf16[3,3,3,128,256]{4,3,2,1,0:T(8,128)(2,1)}, u32[]{:S(2)}) copy-start(bf16[3,3,3,128,256]{4,3,2,1,0:T(8,128)(2,1)} %weight.3) | copy-start | bytes 5308420
  0.7 13.0 %copy-start.3 = (bf16[2,4,64,128]{3,2,1,0:T(8,128)(2,1)S(1)}, bf16[2,4,64,128]{3,2,1,0:T(8,128)(2,1)}, u32[]{:S(2)}) copy-start(bf16[2,4,64,128]{3,2,1,0:T(8,128)(2,1)} %cot.3) | copy-start | bytes 393220
  2.9 19.9 %collective-permute-start.3 = (bf16[2,8,128,128]{3,2,1,0:T(8,128)(2,1)}, bf16[2,8,128,128]{3,2,1,0:T(8,128)(2,1)S(1)}, u32[]{:S(2)}, u32[]{:S(2)}) collective-permute-start(bf16[2,8,128,128]{3,2,1,0:T(8,128)(2,1)} %get-tuple-element.26), channel_id=1, source_target_pairs={{128,8},{136,16},{144,24},{152,32},{160,40},{168,48},{176,56},{184... | collective-permute-start | bytes 1572872 | tf_op jit(solution)/shard_map/ppermute | solution.py:325
  3.6 10.0 %collective-permute-start = (bf16[5,128,128]{2,1,0:T(8,128)(2,1)}, bf16[5,128,128]{2,1,0:T(8,128)(2,1)S(1)}, u32[]{:S(2)}, u32[]{:S(2)}) collective-permute-start(bf16[5,128,128]{2,1,0:T(8,128)(2,1)} %get-tuple-element.21), channel_id=1, source_target_pairs={{0,1},{1,2},{2,3},{3,4},{4,5},{5,6},{6,7},{8,9},{9,10},{10,11},{11... | collective-permute-start | bytes 491528 | tf_op jit(solution)/shard_map/ppermute | solution.py:291
  8.2 5.4 %collective-permute-start.1 = (bf16[2,64,128]{2,1,0:T(8,128)(2,1)}, bf16[2,64,128]{2,1,0:T(8,128)(2,1)S(1)}, u32[]{:S(2)}, u32[]{:S(2)}) collective-permute-start(bf16[2,64,128]{2,1,0:T(8,128)(2,1)} %get-tuple-element.22), channel_id=1, source_target_pairs={{1,0},{2,1},{3,2},{4,3},{5,4},{6,5},{7,6},{9,8},{10,9},{11,10},{12... | collective-permute-start | bytes 98312 | tf_op jit(solution)/shard_map/ppermute | solution.py:291
  10.7 21.5 %copy-start = (bf16[3,3,3,256,128]{4,3,2,1,0:T(8,128)(2,1)S(1)}, bf16[3,3,3,256,128]{4,3,2,1,0:T(8,128)(2,1)}, u32[]{:S(2)}) copy-start(bf16[3,3,3,256,128]{4,3,2,1,0:T(8,128)(2,1)} %weight.5) | copy-start | bytes 5308420
  15.0 7.7 %collective-permute-start.2 = (bf16[4,64,256]{2,1,0:T(8,128)(2,1)S(1)}, bf16[4,64,256]{2,1,0:T(8,128)(2,1)S(1)}, u32[]{:S(2)}, u32[]{:S(2)}) collective-permute-start(bf16[4,64,256]{2,1,0:T(8,128)(2,1)S(1)} %get-tuple-element.24), channel_id=1, source_target_pairs={{0,8},{8,16},{16,24},{24,32},{32,40},{40,48},{48,56},{56,64},{64,7... | collective-permute-start | bytes 393224 | tf_op jit(solution)/shard_map/ppermute | solution.py:286
  22.8 9.3 %collective-permute-start.4 = (bf16[2,3,64,256]{3,2,1,0:T(8,128)(2,1)S(1)}, bf16[2,3,64,256]{3,2,1,0:T(8,128)(2,1)S(1)}, u32[]{:S(2)}, u32[]{:S(2)}) collective-permute-start(bf16[2,3,64,256]{3,2,1,0:T(8,128)(2,1)S(1)} %get-tuple-element.28), channel_id=1, source_target_pairs={{0,1},{1,2},{2,3},{3,4},{4,5},{5,6},{6,7},{8,9},{9,10},{10,11},{11... | collective-permute-start | bytes 589832 | tf_op jit(solution)/shard_map/ppermute | solution.py:291
  25.9 6.3 %collective-permute-start.5 = (bf16[2,2,64,256]{3,2,1,0:T(8,128)(2,1)S(1)}, bf16[2,2,64,256]{3,2,1,0:T(8,128)(2,1)S(1)}, u32[]{:S(2)}, u32[]{:S(2)}) collective-permute-start(bf16[2,2,64,256]{3,2,1,0:T(8,128)(2,1)S(1)} %get-tuple-element.29), channel_id=1, source_target_pairs={{1,0},{2,1},{3,2},{4,3},{5,4},{6,5},{7,6},{9,8},{10,9},{11,10},{12... | collective-permute-start | bytes 393224 | tf_op jit(solution)/shard_map/ppermute | solution.py:291
  27.8 18.2 %collective-permute-start.8 = (bf16[2,6,64,128]{3,2,1,0:T(8,128)(2,1)S(1)}, bf16[2,6,64,128]{3,2,1,0:T(8,128)(2,1)S(1)}, u32[]{:S(2)}, u32[]{:S(2)}) collective-permute-start(bf16[2,6,64,128]{3,2,1,0:T(8,128)(2,1)S(1)} %get-tuple-element.33.cot), channel_id=1, source_target_pairs={{8,0},{16,8},{24,16},{32,24},{40,32},{48,40},{56,48},{64,56},{72,6... | collective-permute-start | bytes 589832 | tf_op jit(solution)/shard_map/ppermute | solution.py:286
  35.3 10.8 %collective-permute-start.6 = (bf16[2,6,64,128]{3,2,1,0:T(8,128)(2,1)S(1)}, bf16[2,6,64,128]{3,2,1,0:T(8,128)(2,1)S(1)}, u32[]{:S(2)}, u32[]{:S(2)}) collective-permute-start(bf16[2,6,64,128]{3,2,1,0:T(8,128)(2,1)S(1)} %get-tuple-element.31.gone), channel_id=1, source_target_pairs={{0,8},{8,16},{16,24},{24,32},{32,40},{40,48},{48,56},{56,64},{64,7... | collective-permute-start | bytes 589832 | tf_op jit(solution)/shard_map/ppermute | solution.py:286
  43.5 10.2 %collective-permute-start.7 = (bf16[2,6,64,128]{3,2,1,0:T(8,128)(2,1)S(1)}, bf16[2,6,64,128]{3,2,1,0:T(8,128)(2,1)S(1)}, u32[]{:S(2)}, u32[]{:S(2)}) collective-permute-start(bf16[2,6,64,128]{3,2,1,0:T(8,128)(2,1)S(1)} %get-tuple-element.32), channel_id=1, source_target_pairs={{8,0},{16,8},{24,16},{32,24},{40,32},{48,40},{56,48},{64,56},{72,6... | collective-permute-start | bytes 589832 | tf_op jit(solution)/shard_map/ppermute | solution.py:286
  56.8 2.5 %collective-permute-start.9 = (bf16[3456,128]{1,0:T(8,128)(2,1)S(1)}, bf16[3456,128]{1,0:T(8,128)(2,1)S(1)}, u32[]{:S(2)}, u32[]{:S(2)}) collective-permute-start(bf16[3456,128]{1,0:T(8,128)(2,1)S(1)} %get-tuple-element.39), channel_id=1, source_target_pairs={{0,1},{1,0},{2,3},{3,2},{4,5},{5,4},{6,7},{7,6},{8,9},{9,8},{10,11... | collective-permute-start | bytes 2654216 | tf_op jit(solution)/shard_map/ppermute | solution.py:281
  112.6 7.0 %collective-permute-start.10 = (bf16[3456,128]{1,0:T(8,128)(2,1)S(1)}, bf16[3456,128]{1,0:T(8,128)(2,1)S(1)}, u32[]{:S(2)}, u32[]{:S(2)}) collective-permute-start(bf16[3456,128]{1,0:T(8,128)(2,1)S(1)} %bitcast.9), channel_id=1, source_target_pairs={{0,1},{1,0},{2,3},{3,2},{4,5},{5,4},{6,7},{7,6},{8,9},{9,8},{10,11... | collective-permute-start | bytes 2654216 | tf_op jit(solution)/shard_map/ppermute | solution.py:281

commit v7 on v6

--- a/solution.py
+++ b/solution.py
@@ -17,10 +17,10 @@
     return jax.ShapeDtypeStruct(dims, dtype)
 
 
-def on_chip(body, outs, smem=0, scratch=(), grant=8, far=False):
+def on_chip(body, outs, smem=0, scratch=(), grant=8):
     def call(*args):
         specs = [pl.BlockSpec(memory_space=pltpu.SMEM)] * smem
-        specs += [pl.BlockSpec(memory_space=pl.ANY if far else pltpu.VMEM)] * (len(args) - smem)
+        specs += [pl.BlockSpec(memory_space=pltpu.VMEM)] * (len(args) - smem)
         return pl.pallas_call(
             body,
             out_shape=outs,
@@ -62,23 +62,9 @@
     stage[0:8, :] = jnp.zeros((8, stage.shape[1]), F32)
 
 
-def edge_body(seg_at, core_at, clip, cot, down, up, tail, arrived):
-    copies = [
-        pltpu.make_async_copy(source, target, arrived.at[i])
-        for i, (source, target) in enumerate(
-            (
-                (clip.at[:, 7], down.at[0:4]),
-                (cot.at[0, 3], down.at[4, 0:64]),
-                (cot.at[1, 3], down.at[4, 64:128]),
-                (cot.at[:, 0], up),
-                (clip.at[2:4], tail),
-            )
-        )
-    ]
-    for one in copies:
-        one.start()
-    for one in copies:
-        one.wait()
+def edge_body(seg_at, core_at, clip, down, tail):
+    down[...] = clip[:, 7]
+    tail[...] = clip[2:4]
 
 
 def windows_body(clip, taps, stage):
@@ -98,7 +84,7 @@
 
 
 def encode_body(
-    taps, above, weight, cot, below, lat1, part, own0, tops, rows6, stage
+    taps, above, weight, lat1, part, own0, tops, stage
 ):
     start_stage(stage)
     for f in range(4):
@@ -114,19 +100,19 @@
     part[...] = (conv(2, 0) + conv(3, 1)).astype(part.dtype).reshape(4, 64, 256)
     lat1[...] = (conv(0, 0) + conv(1, 1) + conv(2, 2)).astype(BF16).reshape(4, 64, 256)
     own0[...] = conv(0, 2).reshape(4, 64, 256)
-    rows6[0, 0] = above[4, 0:64]
-    rows6[1, 0] = above[4, 64:128]
-    rows6[:, 1:5] = cot[...]
-    rows6[:, 5] = below[...]
-
-
-def join_body(own0, part, lat1, tail, lat, down, up):
+
+
+def join_body(own0, part, lat1, tail, cot, later_cot, lat, down, up):
     lat[0] = (own0[...] + part[...].astype(F32)).astype(BF16)
     lat[1] = lat1[...]
     down[:, 0:2] = lat[:, 2:4]
     down[:, 2, :, 0:128] = tail[:, 7, 0:64]
     down[:, 2, :, 128:256] = tail[:, 7, 64:128]
-    up[...] = lat[:, 0:2]
+    down[:, 3, :, 0:128] = cot[:, 3]
+    down[:, 3, :, 128:256] = later_cot[:, 3]
+    up[:, 0:2] = lat[:, 0:2]
+    up[:, 2, :, 0:128] = cot[:, 0]
+    up[:, 2, :, 128:256] = later_cot[:, 0]
 
 
 def fill_latent(lat, top, bottom, wide):
@@ -191,18 +177,26 @@
 
 
 def grads_body(
-    seg_at, core_at, own_part, from_behind, gone, from_later, cot, later_cot, weight, turned,
+    seg_at, core_at, own_part, from_behind, gone, from_later, cot, later_cot, top, bottom,
+    weight, turned,
     lat_grad, own, send, gathered, slopes, rim,
 ):
     seg = seg_at[0]
     core = core_at[0]
 
-    def slope_of(pre, grad):
-        sigm = jax.nn.sigmoid(pre)
-        return (grad.astype(F32) * sigm * (1.0 + pre * (1.0 - sigm))).astype(BF16)
-
-    slopes[0:2] = slope_of(own_part[...] + from_behind[...].astype(F32), cot[...])
-    slopes[2:4] = slope_of(from_later[...].astype(F32) + gone[...].astype(F32), later_cot[...])
+    def slope_at(start, rows, pre, grad):
+        sigm = jax.nn.sigmoid(pre[:, rows])
+        scaled = grad.astype(F32) * sigm * (1.0 + pre[:, rows] * (1.0 - sigm))
+        slopes[start : start + 2, rows] = scaled.astype(BF16)
+
+    for start, one, other, mid, lanes in (
+        (0, own_part, from_behind, cot, slice(0, 128)),
+        (2, from_later, gone, later_cot, slice(128, 256)),
+    ):
+        pre = one[...].astype(F32) + other[...].astype(F32)
+        slope_at(start, slice(0, 1), pre, top[:, 3:4, :, lanes])
+        slope_at(start, slice(1, 5), pre, mid[...])
+        slope_at(start, slice(5, 6), pre, bottom[:, 2:3, :, lanes])
 
     @pl.when(seg == 0)
     def _():
@@ -291,13 +285,60 @@
     return lax.ppermute(array, ("y", "c"), pairs)
 
 
+def pair_body(seg_at, lat_grad, latent, pair):
+    pair[...] = jnp.where(seg_at[0] == 0, lat_grad[...], latent[...])
+
+
+def scaled_body(core_at, half, out):
+    out[0] = half[...].astype(F32) * (1.0 / math.sqrt(32 * 32 * 64))
+
+
+def half_written(core_at, half):
+    return pl.pallas_call(
+        scaled_body,
+        out_shape=shape((2, 3456, 128), F32),
+        grid_spec=pltpu.PrefetchScalarGridSpec(
+            num_scalar_prefetch=1,
+            grid=(4,),
+            in_specs=[pl.BlockSpec((864, 128), lambda i, core: (i, 0))],
+            out_specs=pl.BlockSpec((1, 864, 128), lambda i, core: (core[0], i, 0)),
+        ),
+        name="half_written",
+        compiler_params=pltpu.CompilerParams(vmem_limit_bytes=8 * MIB),
+    )(core_at, half)
+
+
+def other_body(core_at, half, written, out):
+    scaled_body(core_at, half, out)
+
+
+def other_written(core_at, half, written):
+    return pl.pallas_call(
+        other_body,
+        out_shape=shape((2, 3456, 128), F32),
+        grid_spec=pltpu.PrefetchScalarGridSpec(
+            num_scalar_prefetch=1,
+            grid=(4,),
+            in_specs=[
+                pl.BlockSpec((864, 128), lambda i, core: (i, 0)),
+                pl.BlockSpec(memory_space=pl.ANY),
+            ],
+            out_specs=pl.BlockSpec((1, 864, 128), lambda i, core: (1 - core[0], i, 0)),
+        ),
+        input_output_aliases={2: 0},
+        name="other_written",
+        compiler_params=pltpu.CompilerParams(vmem_limit_bytes=8 * MIB),
+    )(core_at, half, written)
+
+
 def summed(own, send):
     got = to_core(send)
     (wide,) = on_chip(halves_body, [shape((16, 216, 128), BF16)])(own, got)
     (thin,) = on_chip(second_body, [shape((4, 216, 128), BF16)])(exchanged(wide, ("x", "y")))
     (wide,) = on_chip(third_body, [shape((16, 216, 128), BF16)])(exchanged(thin, "z"))
     half = exchanged(wide, ("x", "y")).reshape(3456, 128)
-    return half, to_core(half)
+    other = to_core(half)
+    return half, other
 
 
 def on_device(clip_frames, enc_weight, dec_weight, out_grad):
@@ -307,45 +348,34 @@
     stage = pltpu.VMEM((136, 128), F32)
     seg = seg.reshape(1)
     core_at = core.reshape(1)
-    down, up, tail = on_chip(
-        edge_body,
-        [
-            shape((5, 128, 128), BF16),
-            shape((2, 64, 128), BF16),
-            shape((2, 8, 128, 128), BF16),
-        ],
-        2,
-        [pltpu.SemaphoreType.DMA((5,))],
-        60,
-        True,
-    )(seg, core_at, clip_frames, out_grad)
+    down, tail = on_chip(
+        edge_body, [shape((4, 128, 128), BF16), shape((2, 8, 128, 128), BF16)], 2
+    )(seg, core_at, clip_frames)
     above = by_rows(down, 1)
-    below = by_rows(up, -1)
     pairs = [(16 + t - 1, t) for t in range(1, 16)]
     tail = lax.ppermute(tail, ("segment", "x", "z"), pairs)
     (taps,) = on_chip(windows_body, [shape((4, 8, 64, 384), BF16)], scratch=[stage])(clip_frames)
-    lat1, part, own0, tops, cot = on_chip(
+    lat1, part, own0, tops = on_chip(
         encode_body,
         [
             shape((4, 64, 256), BF16),
             shape((4, 64, 256), PART),
             shape((4, 64, 256), F32),
             shape((4, 64, 384), BF16),
-            shape((2, 6, 64, 128), BF16),
         ],
         scratch=[stage],
         grant=16,
-    )(taps, above, enc_weight, out_grad, below)
+    )(taps, above, enc_weight)
     part = by_frames(part, 1)
-    later_cot = by_frames(cot, -1)
+    later_cot = by_frames(out_grad, -1)
     latent, down, up = on_chip(
         join_body,
         [
             shape((2, 4, 64, 256), BF16),
+            shape((2, 4, 64, 256), BF16),
             shape((2, 3, 64, 256), BF16),
-            shape((2, 2, 64, 256), BF16),
         ],
-    )(own0, part, lat1, tail)
+    )(own0, part, lat1, tail, out_grad, later_cot)
     top = by_rows(down, 1)
     bottom = by_rows(up, -1)
     rows6 = (2, 6, 64, 128)
@@ -384,12 +414,12 @@
             pltpu.VMEM((4, 6, 64, 384), BF16),
         ],
         24,
-    )(seg, core_at, own_part, from_behind, gone, from_later, cot, later_cot, dec_weight, turned)
-    latent_pair = jnp.where(seg[0] == 0, lat_grad, latent)[None]
+    )(seg, core_at, own_part, from_behind, gone, from_later, out_grad, later_cot, top, bottom, dec_weight, turned)
+    (latent_pair,) = on_chip(pair_body, [shape((2, 4, 64, 256), BF16)], 1)(seg, lat_grad, latent)
     half, other = summed(own, send)
-    whole = jnp.where(core == 0, jnp.stack([half, other]), jnp.stack([other, half]))
-    weight_grads = whole.reshape(27, 32768).astype(F32) * (1.0 / math.sqrt(32 * 32 * 64))
-    return latent_pair, weight_grads[None]
+    grads = half_written(core_at, half)
+    grads = other_written(core_at, other, grads)
+    return latent_pair[None], grads.reshape(1, 27, 32768)
 
 
 def solution(mesh):

time: 122 us -> 122 us (level)
  waiting for transfers between devices: 19.4 us -> 11.8 us
  blocking collectives: 52.8 us -> 59.9 us
  other arithmetic: 2.96 us -> 0 us
  Pallas kernels: 12 us -> 14 us
    all_to_all x3, blocking collectives: 52.8 us -> 59.9 us  [exchanged(): return lax.all_to_all(array, axes, 0, 0, tiled=True)]
    ppermute x4, waiting for transfers between devices: 9.66 us -> 4.26 us  [by_frames(): return lax.ppermute(array, ('x', 'z'), pairs)]
    pallas_call x0 -> x2, Pallas kernels: none -> 3.46 us  [the longest x1 1.73 us: other_written(): pl.pallas_call(other_body, out_shape=shape((2, 3456, 128), F32), grid_spe...]
    mul x1 -> x0, other arithmetic: 2.23 us -> none  [on_device(): whole.reshape(27, 32768).astype(F32) * (1.0 / math.sqrt(32 * 32 * 64))]
    ppermute x4, starting transfers between devices: 16.6 us -> 18.2 us  [by_frames(): return lax.ppermute(array, ('x', 'z'), pairs)]
    pallas_call x10 -> x11, Pallas kernels: 12 us -> 10.6 us  [call(): pl.pallas_call(body, out_shape=outs, in_specs=specs, out_specs=[pl.BlockS...]
    ppermute x2, waiting for transfers between devices: 3.73 us -> 2.42 us  [to_core(): return lax.ppermute(array, 'c', [(0, 1), (1, 0)])]
    ppermute x4 -> x3, waiting for transfers between devices: 6.01 us -> 5.12 us  [by_rows(): return lax.ppermute(array, ('y', 'c'), pairs)]
  transfers between devices with their start and end apart: 11 -> 10, of which waited for: 7 -> 6; matrix products, arithmetic and copies ran while one was open for 1% -> 0% of each run, Pallas kernels for 5% -> 5%
where the time goes in v7:
time: 122 us; the launch traced here: 121 us
  blocking collectives  59.9 us (49%)
  starting transfers between devices  33.7 us (28%)
  Pallas kernels  14 us (11%)
  waiting for transfers between devices  11.8 us (10%)
  local copies, waits for them, and re-layouts  1.23 us (1%)
    all_to_all x3, blocking collectives, exchanged(): return lax.all_to_all(array, axes, 0, 0, tiled=True)  59.9 us
    ppermute x4, starting transfers between devices, by_frames(): return lax.ppermute(array, ('x', 'z'), pairs)  18.2 us
    pallas_call x11, Pallas kernels, call(): pl.pallas_call(body, out_shape=outs, in_specs=specs, out_specs=[pl.BlockS...  10.6 us
    ppermute x3, starting transfers between devices, by_rows(): return lax.ppermute(array, ('y', 'c'), pairs)  10.6 us
    ppermute x3, waiting for transfers between devices, by_rows(): return lax.ppermute(array, ('y', 'c'), pairs)  5.12 us
    ppermute x4, waiting for transfers between devices, by_frames(): return lax.ppermute(array, ('x', 'z'), pairs)  4.26 us
    ppermute x2, starting transfers between devices, to_core(): return lax.ppermute(array, 'c', [(0, 1), (1, 0)])  4.06 us
  transfers between devices with their start and end apart: 10, of which 6 were waited for; matrix products, arithmetic and copies ran while one was open for 0% of the time, Pallas kernels for 5%

profile of v7, /device:TPU:1, one launch (start us, length us, event | category | flops | bytes accessed | tf_op | source)
XLA Modules:
  0.0 121.5 jit_solution(13191092714809400717)
XLA Ops:
  0.6 1.2 %copy-done.1 = bf16[4,8,128,128]{3,2,1,0:T(8,128)(2,1)S(1)} copy-done((bf16[4,8,128,128]{3,2,1,0:T(8,128)(2,1)S(1)}, bf16[4,8,128,128]{3,2,1,0:T(8,128)(2,1)}, u32[]{:S(2)}) %copy-start.1) | copy-done | bytes 1048600
  1.9 0.8 collective-permute-start.2
  2.7 4.6 %collective-permute-start = (bf16[4,128,128]{2,1,0:T(8,128)(2,1)S(1)}, bf16[4,128,128]{2,1,0:T(8,128)(2,1)S(1)}, u32[]{:S(2)}, u32[]{:S(2)}) collective-permute-start(bf16[4,128,128]{2,1,0:T(8,128)(2,1)S(1)} %get-tuple-element.19), channel_id=1, source_target_pairs={{0,1},{1,2},{2,3},{3,4},{4,5},{5,6},{6,7},{8,9},{9,10},{10,11},{11... | collective-permute-start | bytes 393224 | tf_op jit(solution)/shard_map/ppermute | solution.py:285
  7.3 1.3 %collective-permute-start.3 = (bf16[2,4,64,128]{3,2,1,0:T(8,128)(2,1)}, bf16[2,4,64,128]{3,2,1,0:T(8,128)(2,1)S(1)}, u32[]{:S(2)}, u32[]{:S(2)}) collective-permute-start(bf16[2,4,64,128]{3,2,1,0:T(8,128)(2,1)} %cot.3), channel_id=1, source_target_pairs={{8,0},{16,8},{24,16},{32,24},{40,32},{48,40},{56,48},{64,56},{72,6... | collective-permute-start | bytes 393224 | tf_op jit(solution)/shard_map/ppermute | solution.py:280
  8.6 0.5 shard_map.59.taps
  9.2 0.1 collective-permute-done.above
  9.3 1.4 %shard_map.61 = (bf16[4,64,256]{2,1,0:T(8,128)(2,1)S(1)}, bf16[4,64,256]{2,1,0:T(8,128)(2,1)S(1)}, f32[4,64,256]{2,1,0:T(8,128)S(1)}, bf16[4,64,384]{2,1,0:T(8,128)(2,1)S(1)}) custom-call(bf16[4,8,64,384]{3,2,1,0:T(8,128)(2,1)S(1)} %shard_map.59.taps, bf16[4,128,128]{2,1,0:T(8,128)(2,1)S(1)} %collective-permute-done.above, ...), custom_call_target="tpu_custom_call" | custom-call | tf_op jit(solution)/shard_map/pallas_call | solution.py:24
  10.7 6.1 %collective-permute-start.1 = (bf16[4,64,256]{2,1,0:T(8,128)(2,1)S(1)}, bf16[4,64,256]{2,1,0:T(8,128)(2,1)S(1)}, u32[]{:S(2)}, u32[]{:S(2)}) collective-permute-start(bf16[4,64,256]{2,1,0:T(8,128)(2,1)S(1)} %get-tuple-element.21), channel_id=1, source_target_pairs={{0,8},{8,16},{16,24},{24,32},{32,40},{40,48},{48,56},{56,64},{64,7... | collective-permute-start | bytes 393224 | tf_op jit(solution)/shard_map/ppermute | solution.py:280
  16.8 2.7 %collective-permute-done.1.part = bf16[4,64,256]{2,1,0:T(8,128)(2,1)S(1)} collective-permute-done((bf16[4,64,256]{2,1,0:T(8,128)(2,1)S(1)}, bf16[4,64,256]{2,1,0:T(8,128)(2,1)S(1)}, u32[]{:S(2)}, u32[]{:S(2)}) %collective-permute-start.1) | collective-permute-done | bytes 131104 | tf_op jit(solution)/shard_map/ppermute | solution.py:280
  19.5 0.1 shard_map.62
  19.6 4.1 %collective-permute-start.4 = (bf16[2,4,64,256]{3,2,1,0:T(8,128)(2,1)S(1)}, bf16[2,4,64,256]{3,2,1,0:T(8,128)(2,1)S(1)}, u32[]{:S(2)}, u32[]{:S(2)}) collective-permute-start(bf16[2,4,64,256]{3,2,1,0:T(8,128)(2,1)S(1)} %get-tuple-element.25), channel_id=1, source_target_pairs={{0,1},{1,2},{2,3},{3,4},{4,5},{5,6},{6,7},{8,9},{9,10},{10,11},{11... | collective-permute-start | bytes 786440 | tf_op jit(solution)/shard_map/ppermute | solution.py:285
  23.7 1.9 %collective-permute-start.5 = (bf16[2,3,64,256]{3,2,1,0:T(8,128)(2,1)S(1)}, bf16[2,3,64,256]{3,2,1,0:T(8,128)(2,1)S(1)}, u32[]{:S(2)}, u32[]{:S(2)}) collective-permute-start(bf16[2,3,64,256]{3,2,1,0:T(8,128)(2,1)S(1)} %get-tuple-element.26), channel_id=1, source_target_pairs={{1,0},{2,1},{3,2},{4,3},{5,4},{6,5},{7,6},{9,8},{10,9},{11,10},{12... | collective-permute-start | bytes 589832 | tf_op jit(solution)/shard_map/ppermute | solution.py:285
  25.6 5.1 %collective-permute-done.5.bottom = bf16[2,3,64,256]{3,2,1,0:T(8,128)(2,1)S(1)} collective-permute-done((bf16[2,3,64,256]{3,2,1,0:T(8,128)(2,1)S(1)}, bf16[2,3,64,256]{3,2,1,0:T(8,128)(2,1)S(1)}, u32[]{:S(2)}, u32[]{:S(2)}) %collective-permute-start.5) | collective-permute-done | bytes 196640 | tf_op jit(solution)/shard_map/ppermute | solution.py:285
  30.7 3.1 %shard_map.63 = (f32[2,6,64,128]{3,2,1,0:T(8,128)S(1)}, bf16[2,6,64,128]{3,2,1,0:T(8,128)(2,1)S(1)}, bf16[2,6,64,128]{3,2,1,0:T(8,128)(2,1)S(1)}) custom-call(bf16[2,4,64,256]{3,2,1,0:T(8,128)(2,1)S(1)} %get-tuple-element.32.lat.latent, bf16[2,4,64,256]{3,2,1,0:T(8,128)(2,1)S(1)} %collective-permute-done.4.top, ...), custom_call_target="tpu_custom_call" | custom-call | tf_op jit(solution)/shard_map/pallas_call | solution.py:24
  33.8 1.3 %collective-permute-start.7 = (bf16[2,6,64,128]{3,2,1,0:T(8,128)(2,1)S(1)}, bf16[2,6,64,128]{3,2,1,0:T(8,128)(2,1)S(1)}, u32[]{:S(2)}, u32[]{:S(2)}) collective-permute-start(bf16[2,6,64,128]{3,2,1,0:T(8,128)(2,1)S(1)} %get-tuple-element.29), channel_id=1, source_target_pairs={{8,0},{16,8},{24,16},{32,24},{40,32},{48,40},{56,48},{64,56},{72,6... | collective-permute-start | bytes 589832 | tf_op jit(solution)/shard_map/ppermute | solution.py:280
  35.1 9.5 %collective-permute-start.6 = (bf16[2,6,64,128]{3,2,1,0:T(8,128)(2,1)S(1)}, bf16[2,6,64,128]{3,2,1,0:T(8,128)(2,1)S(1)}, u32[]{:S(2)}, u32[]{:S(2)}) collective-permute-start(bf16[2,6,64,128]{3,2,1,0:T(8,128)(2,1)S(1)} %get-tuple-element.28.gone), channel_id=1, source_target_pairs={{0,8},{8,16},{16,24},{24,32},{32,40},{40,48},{48,56},{56,64},{64,7... | collective-permute-start | bytes 589832 | tf_op jit(solution)/shard_map/ppermute | solution.py:280
  44.7 1.1 shard_map.64.turned
  45.8 0.8 collective-permute-done.7.from_later
  46.6 0.7 collective-permute-done.6.from_behind
  47.3 3.1 %shard_map.65 = (bf16[2,4,64,256]{3,2,1,0:T(8,128)(2,1)S(1)}, f32[3456,128]{1,0:T(8,128)S(1)}, bf16[3456,128]{1,0:T(8,128)(2,1)S(1)}) custom-call(s32[1]{0:T(128)} %bitcast.seg_at, s32[1]{0:T(128)} %bitcast.1.core_at, f32[2,6,64,128]{3,2,1,0:T(8,128)S(1)} %get-tuple-element.27.own_part, bf16[2,6,64,128]{3,2,1,0:T(8,128)(2,1)S(1)} %collective-permute-done.6.from_behind, ...), custom_call_target="tpu_custom_call" | custom-call | tf_op jit(solution)/shard_map/pallas_call | solution.py:24
  50.5 0.1 collective-permute-start.8
  50.6 2.4 %collective-permute-done.8.got = bf16[3456,128]{1,0:T(8,128)(2,1)S(1)} collective-permute-done((bf16[3456,128]{1,0:T(8,128)(2,1)S(1)}, bf16[3456,128]{1,0:T(8,128)(2,1)S(1)}, u32[]{:S(2)}, u32[]{:S(2)}) %collective-permute-start.8) | collective-permute-done | bytes 884768 | tf_op jit(solution)/shard_map/ppermute | solution.py:275
  53.0 0.2 shard_map.67
  53.2 33.7 %all_to_all.15.got = bf16[16,216,128]{2,1,0:T(8,128)(2,1)S(1)} all-to-all(bf16[16,216,128]{2,1,0:T(8,128)(2,1)S(1)} %shard_map.67), channel_id=1, replica_groups=mesh['segment'=2,'x'=4,'z'=4,'y'=4,'c'=2] {'x','y'}, dimensions={0} | all-to-all | bytes 1769472 | tf_op jit(solution)/shard_map/all_to_all | solution.py:271
  86.9 0.1 shard_map.68
  87.0 10.4 %all_to_all.16.got = bf16[4,216,128]{2,1,0:T(8,128)(2,1)S(1)} all-to-all(bf16[4,216,128]{2,1,0:T(8,128)(2,1)S(1)} %shard_map.68), channel_id=1, replica_groups=mesh['segment'=2,'x'=4,'z'=4,'y'=4,'c'=2] {'z'}, dimensions={0} | all-to-all | bytes 442368 | tf_op jit(solution)/shard_map/all_to_all | solution.py:271
  97.5 0.1 shard_map.69
  97.5 15.8 %all_to_all.17 = bf16[16,216,128]{2,1,0:T(8,128)(2,1)S(1)} all-to-all(bf16[16,216,128]{2,1,0:T(8,128)(2,1)S(1)} %shard_map.69), channel_id=1, replica_groups=mesh['segment'=2,'x'=4,'z'=4,'y'=4,'c'=2] {'x','y'}, dimensions={0} | all-to-all | bytes 1769472 | tf_op jit(solution)/shard_map/all_to_all | solution.py:271
  113.3 4.0 %collective-permute-start.9 = (bf16[3456,128]{1,0:T(8,128)(2,1)S(1)}, bf16[3456,128]{1,0:T(8,128)(2,1)S(1)}, u32[]{:S(2)}, u32[]{:S(2)}) collective-permute-start(bf16[3456,128]{1,0:T(8,128)(2,1)S(1)} %bitcast.5), channel_id=1, source_target_pairs={{0,1},{1,0},{2,3},{3,2},{4,5},{5,4},{6,7},{7,6},{8,9},{9,8},{10,11... | collective-permute-start | bytes 2654216 | tf_op jit(solution)/shard_map/ppermute | solution.py:275
  117.3 0.7 shard_map.66
  118.0 1.7 %half_written.1.written = f32[2,3456,128]{2,1,0:T(8,128)} custom-call(s32[1]{0:T(128)} %bitcast.1.core_at, bf16[3456,128]{1,0:T(8,128)(2,1)S(1)} %bitcast.6), custom_call_target="tpu_custom_call" | custom-call | tf_op jit(solution)/shard_map/half_written/pallas_call | solution.py:297
  119.8 1.7 %other_written.1 = f32[2,3456,128]{2,1,0:T(8,128)} custom-call(s32[1]{0:T(128)} %bitcast.1.core_at, bf16[3456,128]{1,0:T(8,128)(2,1)S(1)} %collective-permute-done.9.half, f32[2,3456,128]{2,1,0:T(8,128)} %half_written.1.written), custom_call_target="tpu_custom_call", output_to_operand_aliasing={{}: (2, {})} | custom-call | tf_op jit(solution)/shard_map/other_written/pallas_call | solution.py:316
  (12 shorter events, 0.1 us)
Async XLA Ops:
  0.6 1.2 %copy-start.1 = (bf16[4,8,128,128]{3,2,1,0:T(8,128)(2,1)S(1)}, bf16[4,8,128,128]{3,2,1,0:T(8,128)(2,1)}, u32[]{:S(2)}) copy-start(bf16[4,8,128,128]{3,2,1,0:T(8,128)(2,1)} %clip.3) | copy-start | bytes 3145732
  1.9 7.4 %copy-start.2 = (bf16[3,3,3,128,256]{4,3,2,1,0:T(8,128)(2,1)S(1)}, bf16[3,3,3,128,256]{4,3,2,1,0:T(8,128)(2,1)}, u32[]{:S(2)}) copy-start(bf16[3,3,3,128,256]{4,3,2,1,0:T(8,128)(2,1)} %weight.3) | copy-start | bytes 5308420
  1.9 17.6 %collective-permute-start.2 = (bf16[2,8,128,128]{3,2,1,0:T(8,128)(2,1)S(1)}, bf16[2,8,128,128]{3,2,1,0:T(8,128)(2,1)S(1)}, u32[]{:S(2)}, u32[]{:S(2)}) collective-permute-start(bf16[2,8,128,128]{3,2,1,0:T(8,128)(2,1)S(1)} %get-tuple-element.23), channel_id=1, source_target_pairs={{128,8},{136,16},{144,24},{152,32},{160,40},{168,48},{176,56},{184... | collective-permute-start | bytes 1572872 | tf_op jit(solution)/shard_map/ppermute | solution.py:356
  2.7 6.5 %collective-permute-start = (bf16[4,128,128]{2,1,0:T(8,128)(2,1)S(1)}, bf16[4,128,128]{2,1,0:T(8,128)(2,1)S(1)}, u32[]{:S(2)}, u32[]{:S(2)}) collective-permute-start(bf16[4,128,128]{2,1,0:T(8,128)(2,1)S(1)} %get-tuple-element.19), channel_id=1, source_target_pairs={{0,1},{1,2},{2,3},{3,4},{4,5},{5,6},{6,7},{8,9},{9,10},{10,11},{11... | collective-permute-start | bytes 393224 | tf_op jit(solution)/shard_map/ppermute | solution.py:285
  7.3 9.4 %collective-permute-start.3 = (bf16[2,4,64,128]{3,2,1,0:T(8,128)(2,1)}, bf16[2,4,64,128]{3,2,1,0:T(8,128)(2,1)S(1)}, u32[]{:S(2)}, u32[]{:S(2)}) collective-permute-start(bf16[2,4,64,128]{3,2,1,0:T(8,128)(2,1)} %cot.3), channel_id=1, source_target_pairs={{8,0},{16,8},{24,16},{32,24},{40,32},{48,40},{56,48},{64,56},{72,6... | collective-permute-start | bytes 393224 | tf_op jit(solution)/shard_map/ppermute | solution.py:280
  9.2 10.4 %copy-start.3 = (bf16[2,4,64,128]{3,2,1,0:T(8,128)(2,1)S(1)}, bf16[2,4,64,128]{3,2,1,0:T(8,128)(2,1)}, u32[]{:S(2)}) copy-start(bf16[2,4,64,128]{3,2,1,0:T(8,128)(2,1)} %cot.3) | copy-start | bytes 393220
  9.2 21.5 %copy-start = (bf16[3,3,3,256,128]{4,3,2,1,0:T(8,128)(2,1)S(1)}, bf16[3,3,3,256,128]{4,3,2,1,0:T(8,128)(2,1)}, u32[]{:S(2)}) copy-start(bf16[3,3,3,256,128]{4,3,2,1,0:T(8,128)(2,1)} %weight.5) | copy-start | bytes 5308420
  10.7 8.9 %collective-permute-start.1 = (bf16[4,64,256]{2,1,0:T(8,128)(2,1)S(1)}, bf16[4,64,256]{2,1,0:T(8,128)(2,1)S(1)}, u32[]{:S(2)}, u32[]{:S(2)}) collective-permute-start(bf16[4,64,256]{2,1,0:T(8,128)(2,1)S(1)} %get-tuple-element.21), channel_id=1, source_target_pairs={{0,8},{8,16},{16,24},{24,32},{32,40},{40,48},{48,56},{56,64},{64,7... | collective-permute-start | bytes 393224 | tf_op jit(solution)/shard_map/ppermute | solution.py:280
  19.6 11.1 %collective-permute-start.4 = (bf16[2,4,64,256]{3,2,1,0:T(8,128)(2,1)S(1)}, bf16[2,4,64,256]{3,2,1,0:T(8,128)(2,1)S(1)}, u32[]{:S(2)}, u32[]{:S(2)}) collective-permute-start(bf16[2,4,64,256]{3,2,1,0:T(8,128)(2,1)S(1)} %get-tuple-element.25), channel_id=1, source_target_pairs={{0,1},{1,2},{2,3},{3,4},{4,5},{5,6},{6,7},{8,9},{9,10},{10,11},{11... | collective-permute-start | bytes 786440 | tf_op jit(solution)/shard_map/ppermute | solution.py:285
  23.7 7.0 %collective-permute-start.5 = (bf16[2,3,64,256]{3,2,1,0:T(8,128)(2,1)S(1)}, bf16[2,3,64,256]{3,2,1,0:T(8,128)(2,1)S(1)}, u32[]{:S(2)}, u32[]{:S(2)}) collective-permute-start(bf16[2,3,64,256]{3,2,1,0:T(8,128)(2,1)S(1)} %get-tuple-element.26), channel_id=1, source_target_pairs={{1,0},{2,1},{3,2},{4,3},{5,4},{6,5},{7,6},{9,8},{10,9},{11,10},{12... | collective-permute-start | bytes 589832 | tf_op jit(solution)/shard_map/ppermute | solution.py:285
  33.8 12.8 %collective-permute-start.7 = (bf16[2,6,64,128]{3,2,1,0:T(8,128)(2,1)S(1)}, bf16[2,6,64,128]{3,2,1,0:T(8,128)(2,1)S(1)}, u32[]{:S(2)}, u32[]{:S(2)}) collective-permute-start(bf16[2,6,64,128]{3,2,1,0:T(8,128)(2,1)S(1)} %get-tuple-element.29), channel_id=1, source_target_pairs={{8,0},{16,8},{24,16},{32,24},{40,32},{48,40},{56,48},{64,56},{72,6... | collective-permute-start | bytes 589832 | tf_op jit(solution)/shard_map/ppermute | solution.py:280
  35.1 12.2 %collective-permute-start.6 = (bf16[2,6,64,128]{3,2,1,0:T(8,128)(2,1)S(1)}, bf16[2,6,64,128]{3,2,1,0:T(8,128)(2,1)S(1)}, u32[]{:S(2)}, u32[]{:S(2)}) collective-permute-start(bf16[2,6,64,128]{3,2,1,0:T(8,128)(2,1)S(1)} %get-tuple-element.28.gone), channel_id=1, source_target_pairs={{0,8},{8,16},{16,24},{24,32},{32,40},{40,48},{48,56},{56,64},{64,7... | collective-permute-start | bytes 589832 | tf_op jit(solution)/shard_map/ppermute | solution.py:280
  50.5 2.5 %collective-permute-start.8 = (bf16[3456,128]{1,0:T(8,128)(2,1)S(1)}, bf16[3456,128]{1,0:T(8,128)(2,1)S(1)}, u32[]{:S(2)}, u32[]{:S(2)}) collective-permute-start(bf16[3456,128]{1,0:T(8,128)(2,1)S(1)} %get-tuple-element.35), channel_id=1, source_target_pairs={{0,1},{1,0},{2,3},{3,2},{4,5},{5,4},{6,7},{7,6},{8,9},{9,8},{10,11... | collective-permute-start | bytes 2654216 | tf_op jit(solution)/shard_map/ppermute | solution.py:275
  113.3 6.4 %collective-permute-start.9 = (bf16[3456,128]{1,0:T(8,128)(2,1)S(1)}, bf16[3456,128]{1,0:T(8,128)(2,1)S(1)}, u32[]{:S(2)}, u32[]{:S(2)}) collective-permute-start(bf16[3456,128]{1,0:T(8,128)(2,1)S(1)} %bitcast.5), channel_id=1, source_target_pairs={{0,1},{1,0},{2,3},{3,2},{4,5},{5,4},{6,7},{7,6},{8,9},{9,8},{10,11... | collective-permute-start | bytes 2654216 | tf_op jit(solution)/shard_map/ppermute | solution.py:275

commit v8 on v7

--- a/solution.py
+++ b/solution.py
@@ -62,9 +62,8 @@
     stage[0:8, :] = jnp.zeros((8, stage.shape[1]), F32)
 
 
-def edge_body(seg_at, core_at, clip, down, tail):
+def edge_body(seg_at, core_at, clip, down):
     down[...] = clip[:, 7]
-    tail[...] = clip[2:4]
 
 
 def windows_body(clip, taps, stage):
@@ -84,7 +83,7 @@
 
 
 def encode_body(
-    taps, above, weight, lat1, part, own0, tops, stage
+    clip, taps, above, weight, lat1, part, own0, tops, tail, stage
 ):
     start_stage(stage)
     for f in range(4):
@@ -100,16 +99,16 @@
     part[...] = (conv(2, 0) + conv(3, 1)).astype(part.dtype).reshape(4, 64, 256)
     lat1[...] = (conv(0, 0) + conv(1, 1) + conv(2, 2)).astype(BF16).reshape(4, 64, 256)
     own0[...] = conv(0, 2).reshape(4, 64, 256)
-
-
-def join_body(own0, part, lat1, tail, cot, later_cot, lat, down, up):
+    tail[:, 0] = above[2:4]
+    tail[:, 1:9] = clip[2:4]
+
+
+def join_body(own0, part, lat1, cot, later_cot, lat, down, up):
     lat[0] = (own0[...] + part[...].astype(F32)).astype(BF16)
     lat[1] = lat1[...]
     down[:, 0:2] = lat[:, 2:4]
-    down[:, 2, :, 0:128] = tail[:, 7, 0:64]
-    down[:, 2, :, 128:256] = tail[:, 7, 64:128]
-    down[:, 3, :, 0:128] = cot[:, 3]
-    down[:, 3, :, 128:256] = later_cot[:, 3]
+    down[:, 2, :, 0:128] = cot[:, 3]
+    down[:, 2, :, 128:256] = later_cot[:, 3]
     up[:, 0:2] = lat[:, 0:2]
     up[:, 2, :, 0:128] = cot[:, 0]
     up[:, 2, :, 128:256] = later_cot[:, 0]
@@ -153,11 +152,10 @@
     def _():
         start_stage(stage)
         for f in range(2):
-            corner = jnp.concatenate([top[f, 2, :, 0:128], top[f, 2, :, 128:256]], axis=0)
-            btops[f] = clip_windows(corner, stage)
+            btops[f] = clip_windows(tail[f, 0], stage)
 
             def one(r, carry, f=f):
-                btaps[f, r] = clip_windows(tail[f, r], stage)
+                btaps[f, r] = clip_windows(tail[f, r + 1], stage)
                 return carry
 
             lax.fori_loop(0, 8, one, 0)
@@ -194,7 +192,7 @@
         (2, from_later, gone, later_cot, slice(128, 256)),
     ):
         pre = one[...].astype(F32) + other[...].astype(F32)
-        slope_at(start, slice(0, 1), pre, top[:, 3:4, :, lanes])
+        slope_at(start, slice(0, 1), pre, top[:, 2:3, :, lanes])
         slope_at(start, slice(1, 5), pre, mid[...])
         slope_at(start, slice(5, 6), pre, bottom[:, 2:3, :, lanes])
 
@@ -348,36 +346,35 @@
     stage = pltpu.VMEM((136, 128), F32)
     seg = seg.reshape(1)
     core_at = core.reshape(1)
-    down, tail = on_chip(
-        edge_body, [shape((4, 128, 128), BF16), shape((2, 8, 128, 128), BF16)], 2
-    )(seg, core_at, clip_frames)
+    (down,) = on_chip(edge_body, [shape((4, 128, 128), BF16)], 2)(seg, core_at, clip_frames)
     above = by_rows(down, 1)
-    pairs = [(16 + t - 1, t) for t in range(1, 16)]
-    tail = lax.ppermute(tail, ("segment", "x", "z"), pairs)
     (taps,) = on_chip(windows_body, [shape((4, 8, 64, 384), BF16)], scratch=[stage])(clip_frames)
-    lat1, part, own0, tops = on_chip(
+    lat1, part, own0, tops, tail = on_chip(
         encode_body,
         [
             shape((4, 64, 256), BF16),
             shape((4, 64, 256), PART),
             shape((4, 64, 256), F32),
             shape((4, 64, 384), BF16),
+            shape((2, 9, 128, 128), BF16),
         ],
         scratch=[stage],
         grant=16,
-    )(taps, above, enc_weight)
+    )(clip_frames, taps, above, enc_weight)
     part = by_frames(part, 1)
     later_cot = by_frames(out_grad, -1)
     latent, down, up = on_chip(
         join_body,
         [
             shape((2, 4, 64, 256), BF16),
-            shape((2, 4, 64, 256), BF16),
+            shape((2, 3, 64, 256), BF16),
             shape((2, 3, 64, 256), BF16),
         ],
-    )(own0, part, lat1, tail, out_grad, later_cot)
+    )(own0, part, lat1, out_grad, later_cot)
     top = by_rows(down, 1)
     bottom = by_rows(up, -1)
+    pairs = [(16 + t - 1, t) for t in range(1, 16)]
+    tail = lax.ppermute(tail, ("segment", "x", "z"), pairs)
     rows6 = (2, 6, 64, 128)
     own_part, behind, gone = on_chip(
         decode_body,

time: 122 us -> 124 us (1.016)
  the two profiles are of different devices: /device:TPU:1 before, /device:TPU:33 now
where the time goes in v8:
time: 124 us; the launch traced here: 123 us
  blocking collectives  53.5 us (43%)
  starting transfers between devices  35.1 us (28%)
  waiting for transfers between devices  19.3 us (16%)
  Pallas kernels  13.1 us (11%)
  local copies, waits for them, and re-layouts  1.24 us (1%)
    all_to_all x3, blocking collectives, exchanged(): return lax.all_to_all(array, axes, 0, 0, tiled=True)  53.5 us
    ppermute x4, starting transfers between devices, by_frames(): return lax.ppermute(array, ('x', 'z'), pairs)  16.1 us
    ppermute x3, starting transfers between devices, by_rows(): return lax.ppermute(array, ('y', 'c'), pairs)  11.3 us
    ppermute x4, waiting for transfers between devices, by_frames(): return lax.ppermute(array, ('x', 'z'), pairs)  10.5 us
    pallas_call x11, Pallas kernels, call(): pl.pallas_call(body, out_shape=outs, in_specs=specs, out_specs=[pl.BlockS...  9.66 us
    ppermute x3, waiting for transfers between devices, by_rows(): return lax.ppermute(array, ('y', 'c'), pairs)  6.42 us
    ppermute x2, starting transfers between devices, to_core(): return lax.ppermute(array, 'c', [(0, 1), (1, 0)])  4.17 us
    ppermute x1, starting transfers between devices, on_device(): tail = lax.ppermute(tail, ('segment', 'x', 'z'), pairs)  3.58 us
  transfers between devices with their start and end apart: 10, of which 8 were waited for; matrix products, arithmetic and copies ran while one was open for 0% of the time, Pallas kernels for 6%

profile of v8, /device:TPU:33, one launch (start us, length us, event | category | flops | bytes accessed | tf_op | source)
XLA Modules:
  0.0 123.1 jit_solution(693138868624033044)
XLA Ops:
  0.6 1.2 copy-done
  1.9 4.0 %collective-permute-start = (bf16[4,128,128]{2,1,0:T(8,128)(2,1)S(1)}, bf16[4,128,128]{2,1,0:T(8,128)(2,1)S(1)}, u32[]{:S(2)}, u32[]{:S(2)}) collective-permute-start(bf16[4,128,128]{2,1,0:T(8,128)(2,1)S(1)} %shard_map.60), channel_id=1, source_target_pairs={{0,1},{1,2},{2,3},{3,4},{4,5},{5,6},{6,7},{8,9},{9,10},{10,11},{11... | collective-permute-start | bytes 393224 | tf_op jit(solution)/shard_map/ppermute | solution.py:283
  5.9 0.5 shard_map.59.taps
  6.5 1.4 %collective-permute-done.above = bf16[4,128,128]{2,1,0:T(8,128)(2,1)S(1)} collective-permute-done((bf16[4,128,128]{2,1,0:T(8,128)(2,1)S(1)}, bf16[4,128,128]{2,1,0:T(8,128)(2,1)S(1)}, u32[]{:S(2)}, u32[]{:S(2)}) %collective-permute-start) | collective-permute-done | bytes 131104 | tf_op jit(solution)/shard_map/ppermute | solution.py:283
  7.8 1.4 %shard_map.61 = (bf16[4,64,256]{2,1,0:T(8,128)(2,1)S(1)}, bf16[4,64,256]{2,1,0:T(8,128)(2,1)S(1)}, f32[4,64,256]{2,1,0:T(8,128)S(1)}, bf16[4,64,384]{2,1,0:T(8,128)(2,1)S(1)}, bf16[2,9,128,128]{3,2,1,0:T(8,128)(2,1)S(1)}) custom-call(bf16[4,8,128,128]{3,2,1,0:T(8,128)(2,1)S(1)} %copy-done.1, bf16[4,8,64,384]{3,2,1,0:T(8,128)(2,1)S(1)} %shard_map.59.taps, ...), custom_call_target="tpu_custom_call" | custom-call | tf_op jit(solution)/shard_map/pallas_call | solution.py:24
  9.2 3.6 %collective-permute-start.7 = (bf16[2,9,128,128]{3,2,1,0:T(8,128)(2,1)S(1)}, bf16[2,9,128,128]{3,2,1,0:T(8,128)(2,1)S(1)}, u32[]{:S(2)}, u32[]{:S(2)}) collective-permute-start(bf16[2,9,128,128]{3,2,1,0:T(8,128)(2,1)S(1)} %get-tuple-element.27), channel_id=1, source_target_pairs={{128,8},{136,16},{144,24},{152,32},{160,40},{168,48},{176,56},{184... | collective-permute-start | bytes 1769480 | tf_op jit(solution)/shard_map/ppermute | solution.py:377
  12.8 1.3 %collective-permute-start.2 = (bf16[2,4,64,128]{3,2,1,0:T(8,128)(2,1)S(1)}, bf16[2,4,64,128]{3,2,1,0:T(8,128)(2,1)S(1)}, u32[]{:S(2)}, u32[]{:S(2)}) collective-permute-start(bf16[2,4,64,128]{3,2,1,0:T(8,128)(2,1)S(1)} %copy-done.4), channel_id=1, source_target_pairs={{8,0},{16,8},{24,16},{32,24},{40,32},{48,40},{56,48},{64,56},{72,6... | collective-permute-start | bytes 393224 | tf_op jit(solution)/shard_map/ppermute | solution.py:278
  14.1 6.7 %collective-permute-start.1 = (bf16[4,64,256]{2,1,0:T(8,128)(2,1)S(1)}, bf16[4,64,256]{2,1,0:T(8,128)(2,1)S(1)}, u32[]{:S(2)}, u32[]{:S(2)}) collective-permute-start(bf16[4,64,256]{2,1,0:T(8,128)(2,1)S(1)} %get-tuple-element.19), channel_id=1, source_target_pairs={{0,8},{8,16},{16,24},{24,32},{32,40},{40,48},{48,56},{56,64},{64,7... | collective-permute-start | bytes 393224 | tf_op jit(solution)/shard_map/ppermute | solution.py:278
  20.9 1.6 %collective-permute-done.2.later_cot = bf16[2,4,64,128]{3,2,1,0:T(8,128)(2,1)S(1)} collective-permute-done((bf16[2,4,64,128]{3,2,1,0:T(8,128)(2,1)S(1)}, bf16[2,4,64,128]{3,2,1,0:T(8,128)(2,1)S(1)}, u32[]{:S(2)}, u32[]{:S(2)}) %collective-permute-start.2) | collective-permute-done | bytes 131104 | tf_op jit(solution)/shard_map/ppermute | solution.py:278
  22.5 7.2 %collective-permute-done.1.part = bf16[4,64,256]{2,1,0:T(8,128)(2,1)S(1)} collective-permute-done((bf16[4,64,256]{2,1,0:T(8,128)(2,1)S(1)}, bf16[4,64,256]{2,1,0:T(8,128)(2,1)S(1)}, u32[]{:S(2)}, u32[]{:S(2)}) %collective-permute-start.1) | collective-permute-done | bytes 131104 | tf_op jit(solution)/shard_map/ppermute | solution.py:278
  29.8 5.3 %collective-permute-start.3 = (bf16[2,3,64,256]{3,2,1,0:T(8,128)(2,1)S(1)}, bf16[2,3,64,256]{3,2,1,0:T(8,128)(2,1)S(1)}, u32[]{:S(2)}, u32[]{:S(2)}) collective-permute-start(bf16[2,3,64,256]{3,2,1,0:T(8,128)(2,1)S(1)} %get-tuple-element.22), channel_id=1, source_target_pairs={{0,1},{1,2},{2,3},{3,4},{4,5},{5,6},{6,7},{8,9},{9,10},{10,11},{11... | collective-permute-start | bytes 589832 | tf_op jit(solution)/shard_map/ppermute | solution.py:283
  35.1 1.9 %collective-permute-start.4 = (bf16[2,3,64,256]{3,2,1,0:T(8,128)(2,1)S(1)}, bf16[2,3,64,256]{3,2,1,0:T(8,128)(2,1)S(1)}, u32[]{:S(2)}, u32[]{:S(2)}) collective-permute-start(bf16[2,3,64,256]{3,2,1,0:T(8,128)(2,1)S(1)} %get-tuple-element.23), channel_id=1, source_target_pairs={{1,0},{2,1},{3,2},{4,3},{5,4},{6,5},{7,6},{9,8},{10,9},{11,10},{12... | collective-permute-start | bytes 589832 | tf_op jit(solution)/shard_map/ppermute | solution.py:283
  37.0 0.7 collective-permute-done.3.top
  37.7 4.4 %collective-permute-done.4.bottom = bf16[2,3,64,256]{3,2,1,0:T(8,128)(2,1)S(1)} collective-permute-done((bf16[2,3,64,256]{3,2,1,0:T(8,128)(2,1)S(1)}, bf16[2,3,64,256]{3,2,1,0:T(8,128)(2,1)S(1)}, u32[]{:S(2)}, u32[]{:S(2)}) %collective-permute-start.4) | collective-permute-done | bytes 196640 | tf_op jit(solution)/shard_map/ppermute | solution.py:283
  42.1 3.1 %shard_map.63 = (f32[2,6,64,128]{3,2,1,0:T(8,128)S(1)}, bf16[2,6,64,128]{3,2,1,0:T(8,128)(2,1)S(1)}, bf16[2,6,64,128]{3,2,1,0:T(8,128)(2,1)S(1)}) custom-call(bf16[2,4,64,256]{3,2,1,0:T(8,128)(2,1)S(1)} %get-tuple-element.30.lat.latent, bf16[2,3,64,256]{3,2,1,0:T(8,128)(2,1)S(1)} %collective-permute-done.3.top, ...), custom_call_target="tpu_custom_call" | custom-call | tf_op jit(solution)/shard_map/pallas_call | solution.py:24
  45.2 1.3 %collective-permute-start.6 = (bf16[2,6,64,128]{3,2,1,0:T(8,128)(2,1)S(1)}, bf16[2,6,64,128]{3,2,1,0:T(8,128)(2,1)S(1)}, u32[]{:S(2)}, u32[]{:S(2)}) collective-permute-start(bf16[2,6,64,128]{3,2,1,0:T(8,128)(2,1)S(1)} %get-tuple-element.26), channel_id=1, source_target_pairs={{8,0},{16,8},{24,16},{32,24},{40,32},{48,40},{56,48},{64,56},{72,6... | collective-permute-start | bytes 589832 | tf_op jit(solution)/shard_map/ppermute | solution.py:278
  46.5 6.7 %collective-permute-start.5 = (bf16[2,6,64,128]{3,2,1,0:T(8,128)(2,1)S(1)}, bf16[2,6,64,128]{3,2,1,0:T(8,128)(2,1)S(1)}, u32[]{:S(2)}, u32[]{:S(2)}) collective-permute-start(bf16[2,6,64,128]{3,2,1,0:T(8,128)(2,1)S(1)} %get-tuple-element.25.gone), channel_id=1, source_target_pairs={{0,8},{8,16},{16,24},{24,32},{32,40},{40,48},{48,56},{56,64},{64,7... | collective-permute-start | bytes 589832 | tf_op jit(solution)/shard_map/ppermute | solution.py:278
  53.3 0.9 shard_map.64.turned
  54.2 0.2 collective-permute-done.6.from_later
  54.4 1.5 %collective-permute-done.5.from_behind = bf16[2,6,64,128]{3,2,1,0:T(8,128)(2,1)S(1)} collective-permute-done((bf16[2,6,64,128]{3,2,1,0:T(8,128)(2,1)S(1)}, bf16[2,6,64,128]{3,2,1,0:T(8,128)(2,1)S(1)}, u32[]{:S(2)}, u32[]{:S(2)}) %collective-permute-start.5) | collective-permute-done | bytes 196640 | tf_op jit(solution)/shard_map/ppermute | solution.py:278
  55.9 2.5 %shard_map.65 = (bf16[2,4,64,256]{3,2,1,0:T(8,128)(2,1)S(1)}, f32[3456,128]{1,0:T(8,128)S(1)}, bf16[3456,128]{1,0:T(8,128)(2,1)S(1)}) custom-call(s32[1]{0:T(128)} %bitcast.seg_at, s32[1]{0:T(128)} %bitcast.1.core_at, f32[2,6,64,128]{3,2,1,0:T(8,128)S(1)} %get-tuple-element.24.own_part, bf16[2,6,64,128]{3,2,1,0:T(8,128)(2,1)S(1)} %collective-permute-done.5.from_behind, ...), custom_call_target="tpu_custom_call" | custom-call | tf_op jit(solution)/shard_map/pallas_call | solution.py:24
  58.4 0.1 collective-permute-start.8
  58.5 2.4 %collective-permute-done.8.got = bf16[3456,128]{1,0:T(8,128)(2,1)S(1)} collective-permute-done((bf16[3456,128]{1,0:T(8,128)(2,1)S(1)}, bf16[3456,128]{1,0:T(8,128)(2,1)S(1)}, u32[]{:S(2)}, u32[]{:S(2)}) %collective-permute-start.8) | collective-permute-done | bytes 884768 | tf_op jit(solution)/shard_map/ppermute | solution.py:273
  60.9 0.2 shard_map.67
  61.1 27.0 %all_to_all.15.got = bf16[16,216,128]{2,1,0:T(8,128)(2,1)S(1)} all-to-all(bf16[16,216,128]{2,1,0:T(8,128)(2,1)S(1)} %shard_map.67), channel_id=1, replica_groups=mesh['segment'=2,'x'=4,'z'=4,'y'=4,'c'=2] {'x','y'}, dimensions={0} | all-to-all | bytes 1769472 | tf_op jit(solution)/shard_map/all_to_all | solution.py:269
  88.2 0.1 shard_map.68
  88.3 10.4 %all_to_all.16.got = bf16[4,216,128]{2,1,0:T(8,128)(2,1)S(1)} all-to-all(bf16[4,216,128]{2,1,0:T(8,128)(2,1)S(1)} %shard_map.68), channel_id=1, replica_groups=mesh['segment'=2,'x'=4,'z'=4,'y'=4,'c'=2] {'z'}, dimensions={0} | all-to-all | bytes 442368 | tf_op jit(solution)/shard_map/all_to_all | solution.py:269
  98.8 16.0 %all_to_all.17 = bf16[16,216,128]{2,1,0:T(8,128)(2,1)S(1)} all-to-all(bf16[16,216,128]{2,1,0:T(8,128)(2,1)S(1)} %shard_map.69), channel_id=1, replica_groups=mesh['segment'=2,'x'=4,'z'=4,'y'=4,'c'=2] {'x','y'}, dimensions={0} | all-to-all | bytes 1769472 | tf_op jit(solution)/shard_map/all_to_all | solution.py:269
  114.8 4.1 %collective-permute-start.9 = (bf16[3456,128]{1,0:T(8,128)(2,1)S(1)}, bf16[3456,128]{1,0:T(8,128)(2,1)S(1)}, u32[]{:S(2)}, u32[]{:S(2)}) collective-permute-start(bf16[3456,128]{1,0:T(8,128)(2,1)S(1)} %bitcast.5), channel_id=1, source_target_pairs={{0,1},{1,0},{2,3},{3,2},{4,5},{5,4},{6,7},{7,6},{8,9},{9,8},{10,11... | collective-permute-start | bytes 2654216 | tf_op jit(solution)/shard_map/ppermute | solution.py:273
  118.9 0.7 shard_map.66
  119.6 1.7 %half_written.1.written = f32[2,3456,128]{2,1,0:T(8,128)} custom-call(s32[1]{0:T(128)} %bitcast.1.core_at, bf16[3456,128]{1,0:T(8,128)(2,1)S(1)} %bitcast.6), custom_call_target="tpu_custom_call" | custom-call | tf_op jit(solution)/shard_map/half_written/pallas_call | solution.py:295
  121.4 1.7 %other_written.1 = f32[2,3456,128]{2,1,0:T(8,128)} custom-call(s32[1]{0:T(128)} %bitcast.1.core_at, bf16[3456,128]{1,0:T(8,128)(2,1)S(1)} %collective-permute-done.9.half, f32[2,3456,128]{2,1,0:T(8,128)} %half_written.1.written), custom_call_target="tpu_custom_call", output_to_operand_aliasing={{}: (2, {})} | custom-call | tf_op jit(solution)/shard_map/other_written/pallas_call | solution.py:314
  (14 shorter events, 0.2 us)
Async XLA Ops:
  0.6 1.2 copy-start
  1.9 6.0 %copy-start.1 = (bf16[4,8,128,128]{3,2,1,0:T(8,128)(2,1)S(1)}, bf16[4,8,128,128]{3,2,1,0:T(8,128)(2,1)}, u32[]{:S(2)}) copy-start(bf16[4,8,128,128]{3,2,1,0:T(8,128)(2,1)} %clip.5) | copy-start | bytes 3145732
  1.9 6.0 %copy-start.3 = (bf16[3,3,3,128,256]{4,3,2,1,0:T(8,128)(2,1)S(1)}, bf16[3,3,3,128,256]{4,3,2,1,0:T(8,128)(2,1)}, u32[]{:S(2)}) copy-start(bf16[3,3,3,128,256]{4,3,2,1,0:T(8,128)(2,1)} %weight.3) | copy-start | bytes 5308420
  1.9 6.0 %collective-permute-start = (bf16[4,128,128]{2,1,0:T(8,128)(2,1)S(1)}, bf16[4,128,128]{2,1,0:T(8,128)(2,1)S(1)}, u32[]{:S(2)}, u32[]{:S(2)}) collective-permute-start(bf16[4,128,128]{2,1,0:T(8,128)(2,1)S(1)} %shard_map.60), channel_id=1, source_target_pairs={{0,1},{1,2},{2,3},{3,4},{4,5},{5,6},{6,7},{8,9},{9,10},{10,11},{11... | collective-permute-start | bytes 393224 | tf_op jit(solution)/shard_map/ppermute | solution.py:283
  6.5 6.4 %copy-start.4 = (bf16[2,4,64,128]{3,2,1,0:T(8,128)(2,1)S(1)}, bf16[2,4,64,128]{3,2,1,0:T(8,128)(2,1)}, u32[]{:S(2)}) copy-start(bf16[2,4,64,128]{3,2,1,0:T(8,128)(2,1)} %cot.3) | copy-start | bytes 393220
  6.5 35.6 %copy-start.2 = (bf16[3,3,3,256,128]{4,3,2,1,0:T(8,128)(2,1)S(1)}, bf16[3,3,3,256,128]{4,3,2,1,0:T(8,128)(2,1)}, u32[]{:S(2)}) copy-start(bf16[3,3,3,256,128]{4,3,2,1,0:T(8,128)(2,1)} %weight.5) | copy-start | bytes 5308420
  9.2 44.1 %collective-permute-start.7 = (bf16[2,9,128,128]{3,2,1,0:T(8,128)(2,1)S(1)}, bf16[2,9,128,128]{3,2,1,0:T(8,128)(2,1)S(1)}, u32[]{:S(2)}, u32[]{:S(2)}) collective-permute-start(bf16[2,9,128,128]{3,2,1,0:T(8,128)(2,1)S(1)} %get-tuple-element.27), channel_id=1, source_target_pairs={{128,8},{136,16},{144,24},{152,32},{160,40},{168,48},{176,56},{184... | collective-permute-start | bytes 1769480 | tf_op jit(solution)/shard_map/ppermute | solution.py:377
  12.8 9.6 %collective-permute-start.2 = (bf16[2,4,64,128]{3,2,1,0:T(8,128)(2,1)S(1)}, bf16[2,4,64,128]{3,2,1,0:T(8,128)(2,1)S(1)}, u32[]{:S(2)}, u32[]{:S(2)}) collective-permute-start(bf16[2,4,64,128]{3,2,1,0:T(8,128)(2,1)S(1)} %copy-done.4), channel_id=1, source_target_pairs={{8,0},{16,8},{24,16},{32,24},{40,32},{48,40},{56,48},{64,56},{72,6... | collective-permute-start | bytes 393224 | tf_op jit(solution)/shard_map/ppermute | solution.py:278
  14.1 15.6 %collective-permute-start.1 = (bf16[4,64,256]{2,1,0:T(8,128)(2,1)S(1)}, bf16[4,64,256]{2,1,0:T(8,128)(2,1)S(1)}, u32[]{:S(2)}, u32[]{:S(2)}) collective-permute-start(bf16[4,64,256]{2,1,0:T(8,128)(2,1)S(1)} %get-tuple-element.19), channel_id=1, source_target_pairs={{0,8},{8,16},{16,24},{24,32},{32,40},{40,48},{48,56},{56,64},{64,7... | collective-permute-start | bytes 393224 | tf_op jit(solution)/shard_map/ppermute | solution.py:278
  29.8 7.9 %collective-permute-start.3 = (bf16[2,3,64,256]{3,2,1,0:T(8,128)(2,1)S(1)}, bf16[2,3,64,256]{3,2,1,0:T(8,128)(2,1)S(1)}, u32[]{:S(2)}, u32[]{:S(2)}) collective-permute-start(bf16[2,3,64,256]{3,2,1,0:T(8,128)(2,1)S(1)} %get-tuple-element.22), channel_id=1, source_target_pairs={{0,1},{1,2},{2,3},{3,4},{4,5},{5,6},{6,7},{8,9},{9,10},{10,11},{11... | collective-permute-start | bytes 589832 | tf_op jit(solution)/shard_map/ppermute | solution.py:283
  35.1 7.0 %collective-permute-start.4 = (bf16[2,3,64,256]{3,2,1,0:T(8,128)(2,1)S(1)}, bf16[2,3,64,256]{3,2,1,0:T(8,128)(2,1)S(1)}, u32[]{:S(2)}, u32[]{:S(2)}) collective-permute-start(bf16[2,3,64,256]{3,2,1,0:T(8,128)(2,1)S(1)} %get-tuple-element.23), channel_id=1, source_target_pairs={{1,0},{2,1},{3,2},{4,3},{5,4},{6,5},{7,6},{9,8},{10,9},{11,10},{12... | collective-permute-start | bytes 589832 | tf_op jit(solution)/shard_map/ppermute | solution.py:283
  45.2 9.2 %collective-permute-start.6 = (bf16[2,6,64,128]{3,2,1,0:T(8,128)(2,1)S(1)}, bf16[2,6,64,128]{3,2,1,0:T(8,128)(2,1)S(1)}, u32[]{:S(2)}, u32[]{:S(2)}) collective-permute-start(bf16[2,6,64,128]{3,2,1,0:T(8,128)(2,1)S(1)} %get-tuple-element.26), channel_id=1, source_target_pairs={{8,0},{16,8},{24,16},{32,24},{40,32},{48,40},{56,48},{64,56},{72,6... | collective-permute-start | bytes 589832 | tf_op jit(solution)/shard_map/ppermute | solution.py:278
  46.5 9.3 %collective-permute-start.5 = (bf16[2,6,64,128]{3,2,1,0:T(8,128)(2,1)S(1)}, bf16[2,6,64,128]{3,2,1,0:T(8,128)(2,1)S(1)}, u32[]{:S(2)}, u32[]{:S(2)}) collective-permute-start(bf16[2,6,64,128]{3,2,1,0:T(8,128)(2,1)S(1)} %get-tuple-element.25.gone), channel_id=1, source_target_pairs={{0,8},{8,16},{16,24},{24,32},{32,40},{40,48},{48,56},{56,64},{64,7... | collective-permute-start | bytes 589832 | tf_op jit(solution)/shard_map/ppermute | solution.py:278
  58.4 2.5 %collective-permute-start.8 = (bf16[3456,128]{1,0:T(8,128)(2,1)S(1)}, bf16[3456,128]{1,0:T(8,128)(2,1)S(1)}, u32[]{:S(2)}, u32[]{:S(2)}) collective-permute-start(bf16[3456,128]{1,0:T(8,128)(2,1)S(1)} %get-tuple-element.33), channel_id=1, source_target_pairs={{0,1},{1,0},{2,3},{3,2},{4,5},{5,4},{6,7},{7,6},{8,9},{9,8},{10,11... | collective-permute-start | bytes 2654216 | tf_op jit(solution)/shard_map/ppermute | solution.py:273
  114.8 6.5 %collective-permute-start.9 = (bf16[3456,128]{1,0:T(8,128)(2,1)S(1)}, bf16[3456,128]{1,0:T(8,128)(2,1)S(1)}, u32[]{:S(2)}, u32[]{:S(2)}) collective-permute-start(bf16[3456,128]{1,0:T(8,128)(2,1)S(1)} %bitcast.5), channel_id=1, source_target_pairs={{0,1},{1,0},{2,3},{3,2},{4,5},{5,4},{6,7},{7,6},{8,9},{9,8},{10,11... | collective-permute-start | bytes 2654216 | tf_op jit(solution)/shard_map/ppermute | solution.py:273

commit v9 on v8

--- a/solution.py
+++ b/solution.py
@@ -89,16 +89,18 @@
     for f in range(4):
         tops[f] = clip_windows(above[f], stage)
 
-    def conv(f, a):
+    def conv(frames, a):
         total = None
         for b in range(3):
-            term = dot(clip_im2col(tops, taps, f, b), weight[a, b].reshape(384, 256))
+            rows = jnp.concatenate([clip_im2col(tops, taps, f, b) for f in frames], axis=0)
+            term = dot(rows, weight[a, b].reshape(384, 256))
             total = term if total is None else total + term
-        return total
-
-    part[...] = (conv(2, 0) + conv(3, 1)).astype(part.dtype).reshape(4, 64, 256)
-    lat1[...] = (conv(0, 0) + conv(1, 1) + conv(2, 2)).astype(BF16).reshape(4, 64, 256)
-    own0[...] = conv(0, 2).reshape(4, 64, 256)
+        return total[0:256], total[256:512]
+
+    (one, two), (three, four), (five, six) = conv((0, 2), 0), conv((1, 3), 1), conv((0, 2), 2)
+    part[...] = (two + four).astype(part.dtype).reshape(4, 64, 256)
+    lat1[...] = (one + three + six).astype(BF16).reshape(4, 64, 256)
+    own0[...] = five.reshape(4, 64, 256)
     tail[:, 0] = above[2:4]
     tail[:, 1:9] = clip[2:4]
 
@@ -130,18 +132,19 @@
 def decode_body(lat, top, bottom, weight, own, behind, part, wide):
     fill_latent(lat, top, bottom, wide)
 
-    def conv(f, a):
+    def conv(a):
         total = None
         for b in range(3):
-            window = wide[f, b : b + 6].reshape(384, 768)
+            window = wide[:, b : b + 6].reshape(768, 768)
             term = dot(window, weight[a, b].reshape(768, 128))
             total = term if total is None else total + term
-        return total
-
-    part[0] = (conv(0, 0) + conv(1, 1)).astype(part.dtype).reshape(6, 64, 128)
-    part[1] = conv(1, 0).astype(part.dtype).reshape(6, 64, 128)
-    own[0] = conv(0, 2).reshape(6, 64, 128)
-    own[1] = (conv(0, 1) + conv(1, 2)).reshape(6, 64, 128)
+        return total.reshape(2, 6, 64, 128)
+
+    one, two, three = conv(0), conv(1), conv(2)
+    part[0] = (one[0] + two[1]).astype(part.dtype)
+    part[1] = one[1].astype(part.dtype)
+    own[0] = three[0]
+    own[1] = two[0] + three[1]
     behind[...] = own[...].astype(behind.dtype)
 
 
@@ -202,18 +205,16 @@
             for r in range(6):
                 left, same, right = neighbour_cols(slopes[f, r])
                 rim[f, r] = jnp.concatenate([right, same, left], axis=1)
-        grads = []
-        for t in range(2):
-            total = None
-            for a in range(3):
-                for b in range(3):
-                    window = rim[t + 2 - a, 2 - b : 6 - b].reshape(256, 384)
-                    side = jnp.concatenate([weight[a, b, c] for c in range(3)], axis=1)
-                    term = dot_nt(window, side)
-                    total = term if total is None else total + term
-            grad = total.astype(BF16)
-            lat_grad[t] = grad.reshape(4, 64, 256)
-            grads.append(grad)
+        total = None
+        for a in range(3):
+            for b in range(3):
+                window = rim[2 - a : 4 - a, 2 - b : 6 - b].reshape(512, 384)
+                side = jnp.concatenate([weight[a, b, c] for c in range(3)], axis=1)
+                term = dot_nt(window, side)
+                total = term if total is None else total + term
+        grad = total.astype(BF16)
+        lat_grad[...] = grad.reshape(2, 4, 64, 256)
+        grads = (grad[0:256], grad[256:512])
         for a in range(3):
             for b in range(3):
                 total = dot(turned[a * 3 + b], grads[0]) + dot(turned[(a + 2) * 3 + b], grads[1])
@@ -287,46 +288,36 @@
     pair[...] = jnp.where(seg_at[0] == 0, lat_grad[...], latent[...])
 
 
-def scaled_body(core_at, half, out):
-    out[0] = half[...].astype(F32) * (1.0 / math.sqrt(32 * 32 * 64))
-
-
-def half_written(core_at, half):
+def write_half(at, half, out, held, sent):
+    copies = []
+    for i in range(4):
+        rows = pl.ds(864 * i, 864)
+        held[rows, :] = half[rows, :].astype(F32) * (1.0 / math.sqrt(32 * 32 * 64))
+        copies.append(pltpu.make_async_copy(held.at[rows], out.at[at, rows], sent.at[i]))
+        copies[-1].start()
+    for one in copies:
+        one.wait()
+
+
+def half_body(core_at, half, out, held, sent):
+    write_half(core_at[0], half, out, held, sent)
+
+
+def other_body(core_at, half, written, out, held, sent):
+    write_half(1 - core_at[0], half, out, held, sent)
+
+
+def written(body, core_at, half, *given):
+    specs = [pl.BlockSpec(memory_space=pltpu.SMEM), pl.BlockSpec(memory_space=pltpu.VMEM)]
     return pl.pallas_call(
-        scaled_body,
+        body,
         out_shape=shape((2, 3456, 128), F32),
-        grid_spec=pltpu.PrefetchScalarGridSpec(
-            num_scalar_prefetch=1,
-            grid=(4,),
-            in_specs=[pl.BlockSpec((864, 128), lambda i, core: (i, 0))],
-            out_specs=pl.BlockSpec((1, 864, 128), lambda i, core: (core[0], i, 0)),
-        ),
-        name="half_written",
+        in_specs=specs + [pl.BlockSpec(memory_space=pl.ANY)] * len(given),
+        out_specs=pl.BlockSpec(memory_space=pl.ANY),
+        scratch_shapes=[pltpu.VMEM((3456, 128), F32), pltpu.SemaphoreType.DMA((4,))],
+        input_output_aliases={2: 0} if given else {},
         compiler_params=pltpu.CompilerParams(vmem_limit_bytes=8 * MIB),
-    )(core_at, half)
-
-
-def other_body(core_at, half, written, out):
-    scaled_body(core_at, half, out)
-
-
-def other_written(core_at, half, written):
-    return pl.pallas_call(
-        other_body,
-        out_shape=shape((2, 3456, 128), F32),
-        grid_spec=pltpu.PrefetchScalarGridSpec(
-            num_scalar_prefetch=1,
-            grid=(4,),
-            in_specs=[
-                pl.BlockSpec((864, 128), lambda i, core: (i, 0)),
-                pl.BlockSpec(memory_space=pl.ANY),
-            ],
-            out_specs=pl.BlockSpec((1, 864, 128), lambda i, core: (1 - core[0], i, 0)),
-        ),
-        input_output_aliases={2: 0},
-        name="other_written",
-        compiler_params=pltpu.CompilerParams(vmem_limit_bytes=8 * MIB),
-    )(core_at, half, written)
+    )(core_at, half, *given)
 
 
 def summed(own, send):
@@ -414,8 +405,8 @@
     )(seg, core_at, own_part, from_behind, gone, from_later, out_grad, later_cot, top, bottom, dec_weight, turned)
     (latent_pair,) = on_chip(pair_body, [shape((2, 4, 64, 256), BF16)], 1)(seg, lat_grad, latent)
     half, other = summed(own, send)
-    grads = half_written(core_at, half)
-    grads = other_written(core_at, other, grads)
+    grads = written(half_body, core_at, half)
+    grads = written(other_body, core_at, other, grads)
     return latent_pair[None], grads.reshape(1, 27, 32768)
 
 

time: 124 us -> 123 us (level)
  transfers between devices with their start and end apart: 10 -> 10, of which waited for: 8 -> 9; matrix products, arithmetic and copies ran while one was open for 0% -> 0% of each run, Pallas kernels for 6% -> 5%
where the time goes in v9:
time: 123 us; the launch traced here: 122 us
  blocking collectives  53.5 us (43%)
  starting transfers between devices  35.1 us (29%)
  waiting for transfers between devices  19.4 us (16%)
  Pallas kernels  12.2 us (10%)
  local copies, waits for them, and re-layouts  1.24 us (1%)
    all_to_all x3, blocking collectives, exchanged(): return lax.all_to_all(array, axes, 0, 0, tiled=True)  53.5 us
    ppermute x4, starting transfers between devices, by_frames(): return lax.ppermute(array, ('x', 'z'), pairs)  16.1 us
    ppermute x3, starting transfers between devices, by_rows(): return lax.ppermute(array, ('y', 'c'), pairs)  11.3 us
    ppermute x4, waiting for transfers between devices, by_frames(): return lax.ppermute(array, ('x', 'z'), pairs)  10.5 us
    pallas_call x11, Pallas kernels, call(): pl.pallas_call(body, out_shape=outs, in_specs=specs, out_specs=[pl.BlockS...  9.69 us
    ppermute x3, waiting for transfers between devices, by_rows(): return lax.ppermute(array, ('y', 'c'), pairs)  6.42 us
    ppermute x2, starting transfers between devices, to_core(): return lax.ppermute(array, 'c', [(0, 1), (1, 0)])  4.17 us
    ppermute x1, starting transfers between devices, on_device(): tail = lax.ppermute(tail, ('segment', 'x', 'z'), pairs)  3.58 us
  transfers between devices with their start and end apart: 10, of which 9 were waited for; matrix products, arithmetic and copies ran while one was open for 0% of the time, Pallas kernels for 5%

profile of v9, /device:TPU:33, one launch (start us, length us, event | category | flops | bytes accessed | tf_op | source)
XLA Modules:
  0.0 122.3 jit_solution(13519237814507730854)
XLA Ops:
  0.6 1.2 copy-done
  1.9 4.0 %collective-permute-start = (bf16[4,128,128]{2,1,0:T(8,128)(2,1)S(1)}, bf16[4,128,128]{2,1,0:T(8,128)(2,1)S(1)}, u32[]{:S(2)}, u32[]{:S(2)}) collective-permute-start(bf16[4,128,128]{2,1,0:T(8,128)(2,1)S(1)} %shard_map.60), channel_id=1, source_target_pairs={{0,1},{1,2},{2,3},{3,4},{4,5},{5,6},{6,7},{8,9},{9,10},{10,11},{11... | collective-permute-start | bytes 393224 | tf_op jit(solution)/shard_map/ppermute | solution.py:284
  5.9 0.5 shard_map.59.taps
  6.5 1.4 %collective-permute-done.above = bf16[4,128,128]{2,1,0:T(8,128)(2,1)S(1)} collective-permute-done((bf16[4,128,128]{2,1,0:T(8,128)(2,1)S(1)}, bf16[4,128,128]{2,1,0:T(8,128)(2,1)S(1)}, u32[]{:S(2)}, u32[]{:S(2)}) %collective-permute-start) | collective-permute-done | bytes 131104 | tf_op jit(solution)/shard_map/ppermute | solution.py:284
  7.8 1.4 %shard_map.61 = (bf16[4,64,256]{2,1,0:T(8,128)(2,1)S(1)}, bf16[4,64,256]{2,1,0:T(8,128)(2,1)S(1)}, f32[4,64,256]{2,1,0:T(8,128)S(1)}, bf16[4,64,384]{2,1,0:T(8,128)(2,1)S(1)}, bf16[2,9,128,128]{3,2,1,0:T(8,128)(2,1)S(1)}) custom-call(bf16[4,8,128,128]{3,2,1,0:T(8,128)(2,1)S(1)} %copy-done.1, bf16[4,8,64,384]{3,2,1,0:T(8,128)(2,1)S(1)} %shard_map.59.taps, ...), custom_call_target="tpu_custom_call" | custom-call | tf_op jit(solution)/shard_map/pallas_call | solution.py:24
  9.3 3.6 %collective-permute-start.7 = (bf16[2,9,128,128]{3,2,1,0:T(8,128)(2,1)S(1)}, bf16[2,9,128,128]{3,2,1,0:T(8,128)(2,1)S(1)}, u32[]{:S(2)}, u32[]{:S(2)}) collective-permute-start(bf16[2,9,128,128]{3,2,1,0:T(8,128)(2,1)S(1)} %get-tuple-element.27), channel_id=1, source_target_pairs={{128,8},{136,16},{144,24},{152,32},{160,40},{168,48},{176,56},{184... | collective-permute-start | bytes 1769480 | tf_op jit(solution)/shard_map/ppermute | solution.py:368
  12.9 1.3 %collective-permute-start.2 = (bf16[2,4,64,128]{3,2,1,0:T(8,128)(2,1)S(1)}, bf16[2,4,64,128]{3,2,1,0:T(8,128)(2,1)S(1)}, u32[]{:S(2)}, u32[]{:S(2)}) collective-permute-start(bf16[2,4,64,128]{3,2,1,0:T(8,128)(2,1)S(1)} %copy-done.4), channel_id=1, source_target_pairs={{8,0},{16,8},{24,16},{32,24},{40,32},{48,40},{56,48},{64,56},{72,6... | collective-permute-start | bytes 393224 | tf_op jit(solution)/shard_map/ppermute | solution.py:279
  14.2 6.7 %collective-permute-start.1 = (bf16[4,64,256]{2,1,0:T(8,128)(2,1)S(1)}, bf16[4,64,256]{2,1,0:T(8,128)(2,1)S(1)}, u32[]{:S(2)}, u32[]{:S(2)}) collective-permute-start(bf16[4,64,256]{2,1,0:T(8,128)(2,1)S(1)} %get-tuple-element.19), channel_id=1, source_target_pairs={{0,8},{8,16},{16,24},{24,32},{32,40},{40,48},{48,56},{56,64},{64,7... | collective-permute-start | bytes 393224 | tf_op jit(solution)/shard_map/ppermute | solution.py:279
  20.9 1.6 %collective-permute-done.2.later_cot = bf16[2,4,64,128]{3,2,1,0:T(8,128)(2,1)S(1)} collective-permute-done((bf16[2,4,64,128]{3,2,1,0:T(8,128)(2,1)S(1)}, bf16[2,4,64,128]{3,2,1,0:T(8,128)(2,1)S(1)}, u32[]{:S(2)}, u32[]{:S(2)}) %collective-permute-start.2) | collective-permute-done | bytes 131104 | tf_op jit(solution)/shard_map/ppermute | solution.py:279
  22.5 7.2 %collective-permute-done.1.part = bf16[4,64,256]{2,1,0:T(8,128)(2,1)S(1)} collective-permute-done((bf16[4,64,256]{2,1,0:T(8,128)(2,1)S(1)}, bf16[4,64,256]{2,1,0:T(8,128)(2,1)S(1)}, u32[]{:S(2)}, u32[]{:S(2)}) %collective-permute-start.1) | collective-permute-done | bytes 131104 | tf_op jit(solution)/shard_map/ppermute | solution.py:279
  29.8 5.3 %collective-permute-start.3 = (bf16[2,3,64,256]{3,2,1,0:T(8,128)(2,1)S(1)}, bf16[2,3,64,256]{3,2,1,0:T(8,128)(2,1)S(1)}, u32[]{:S(2)}, u32[]{:S(2)}) collective-permute-start(bf16[2,3,64,256]{3,2,1,0:T(8,128)(2,1)S(1)} %get-tuple-element.22), channel_id=1, source_target_pairs={{0,1},{1,2},{2,3},{3,4},{4,5},{5,6},{6,7},{8,9},{9,10},{10,11},{11... | collective-permute-start | bytes 589832 | tf_op jit(solution)/shard_map/ppermute | solution.py:284
  35.1 1.9 %collective-permute-start.4 = (bf16[2,3,64,256]{3,2,1,0:T(8,128)(2,1)S(1)}, bf16[2,3,64,256]{3,2,1,0:T(8,128)(2,1)S(1)}, u32[]{:S(2)}, u32[]{:S(2)}) collective-permute-start(bf16[2,3,64,256]{3,2,1,0:T(8,128)(2,1)S(1)} %get-tuple-element.23), channel_id=1, source_target_pairs={{1,0},{2,1},{3,2},{4,3},{5,4},{6,5},{7,6},{9,8},{10,9},{11,10},{12... | collective-permute-start | bytes 589832 | tf_op jit(solution)/shard_map/ppermute | solution.py:284
  37.1 0.7 collective-permute-done.3.top
  37.7 4.4 %collective-permute-done.4.bottom = bf16[2,3,64,256]{3,2,1,0:T(8,128)(2,1)S(1)} collective-permute-done((bf16[2,3,64,256]{3,2,1,0:T(8,128)(2,1)S(1)}, bf16[2,3,64,256]{3,2,1,0:T(8,128)(2,1)S(1)}, u32[]{:S(2)}, u32[]{:S(2)}) %collective-permute-start.4) | collective-permute-done | bytes 196640 | tf_op jit(solution)/shard_map/ppermute | solution.py:284
  42.1 3.2 %shard_map.63 = (f32[2,6,64,128]{3,2,1,0:T(8,128)S(1)}, bf16[2,6,64,128]{3,2,1,0:T(8,128)(2,1)S(1)}, bf16[2,6,64,128]{3,2,1,0:T(8,128)(2,1)S(1)}) custom-call(bf16[2,4,64,256]{3,2,1,0:T(8,128)(2,1)S(1)} %get-tuple-element.30.lat.latent, bf16[2,3,64,256]{3,2,1,0:T(8,128)(2,1)S(1)} %collective-permute-done.3.top, ...), custom_call_target="tpu_custom_call" | custom-call | tf_op jit(solution)/shard_map/pallas_call | solution.py:24
  45.3 1.3 %collective-permute-start.6 = (bf16[2,6,64,128]{3,2,1,0:T(8,128)(2,1)S(1)}, bf16[2,6,64,128]{3,2,1,0:T(8,128)(2,1)S(1)}, u32[]{:S(2)}, u32[]{:S(2)}) collective-permute-start(bf16[2,6,64,128]{3,2,1,0:T(8,128)(2,1)S(1)} %get-tuple-element.26), channel_id=1, source_target_pairs={{8,0},{16,8},{24,16},{32,24},{40,32},{48,40},{56,48},{64,56},{72,6... | collective-permute-start | bytes 589832 | tf_op jit(solution)/shard_map/ppermute | solution.py:279
  46.6 6.7 %collective-permute-start.5 = (bf16[2,6,64,128]{3,2,1,0:T(8,128)(2,1)S(1)}, bf16[2,6,64,128]{3,2,1,0:T(8,128)(2,1)S(1)}, u32[]{:S(2)}, u32[]{:S(2)}) collective-permute-start(bf16[2,6,64,128]{3,2,1,0:T(8,128)(2,1)S(1)} %get-tuple-element.25.gone), channel_id=1, source_target_pairs={{0,8},{8,16},{16,24},{24,32},{32,40},{40,48},{48,56},{56,64},{64,7... | collective-permute-start | bytes 589832 | tf_op jit(solution)/shard_map/ppermute | solution.py:279
  53.3 0.9 shard_map.64.turned
  54.2 0.2 collective-permute-done.6.from_later
  54.4 1.5 %collective-permute-done.5.from_behind = bf16[2,6,64,128]{3,2,1,0:T(8,128)(2,1)S(1)} collective-permute-done((bf16[2,6,64,128]{3,2,1,0:T(8,128)(2,1)S(1)}, bf16[2,6,64,128]{3,2,1,0:T(8,128)(2,1)S(1)}, u32[]{:S(2)}, u32[]{:S(2)}) %collective-permute-start.5) | collective-permute-done | bytes 196640 | tf_op jit(solution)/shard_map/ppermute | solution.py:279
  55.9 2.5 %shard_map.65 = (bf16[2,4,64,256]{3,2,1,0:T(8,128)(2,1)S(1)}, f32[3456,128]{1,0:T(8,128)S(1)}, bf16[3456,128]{1,0:T(8,128)(2,1)S(1)}) custom-call(s32[1]{0:T(128)} %bitcast.seg_at, s32[1]{0:T(128)} %bitcast.1.core_at, f32[2,6,64,128]{3,2,1,0:T(8,128)S(1)} %get-tuple-element.24.own_part, bf16[2,6,64,128]{3,2,1,0:T(8,128)(2,1)S(1)} %collective-permute-done.5.from_behind, ...), custom_call_target="tpu_custom_call" | custom-call | tf_op jit(solution)/shard_map/pallas_call | solution.py:24
  58.4 0.1 collective-permute-start.8
  58.5 2.4 %collective-permute-done.8.got = bf16[3456,128]{1,0:T(8,128)(2,1)S(1)} collective-permute-done((bf16[3456,128]{1,0:T(8,128)(2,1)S(1)}, bf16[3456,128]{1,0:T(8,128)(2,1)S(1)}, u32[]{:S(2)}, u32[]{:S(2)}) %collective-permute-start.8) | collective-permute-done | bytes 884768 | tf_op jit(solution)/shard_map/ppermute | solution.py:274
  61.0 0.2 shard_map.67
  61.2 27.0 %all_to_all.15.got = bf16[16,216,128]{2,1,0:T(8,128)(2,1)S(1)} all-to-all(bf16[16,216,128]{2,1,0:T(8,128)(2,1)S(1)} %shard_map.67), channel_id=1, replica_groups=mesh['segment'=2,'x'=4,'z'=4,'y'=4,'c'=2] {'x','y'}, dimensions={0} | all-to-all | bytes 1769472 | tf_op jit(solution)/shard_map/all_to_all | solution.py:270
  88.2 0.1 shard_map.68
  88.3 10.4 %all_to_all.16.got = bf16[4,216,128]{2,1,0:T(8,128)(2,1)S(1)} all-to-all(bf16[4,216,128]{2,1,0:T(8,128)(2,1)S(1)} %shard_map.68), channel_id=1, replica_groups=mesh['segment'=2,'x'=4,'z'=4,'y'=4,'c'=2] {'z'}, dimensions={0} | all-to-all | bytes 442368 | tf_op jit(solution)/shard_map/all_to_all | solution.py:270
  98.8 16.0 %all_to_all.17 = bf16[16,216,128]{2,1,0:T(8,128)(2,1)S(1)} all-to-all(bf16[16,216,128]{2,1,0:T(8,128)(2,1)S(1)} %shard_map.69), channel_id=1, replica_groups=mesh['segment'=2,'x'=4,'z'=4,'y'=4,'c'=2] {'x','y'}, dimensions={0} | all-to-all | bytes 1769472 | tf_op jit(solution)/shard_map/all_to_all | solution.py:270
  114.9 4.1 %collective-permute-start.9 = (bf16[3456,128]{1,0:T(8,128)(2,1)S(1)}, bf16[3456,128]{1,0:T(8,128)(2,1)S(1)}, u32[]{:S(2)}, u32[]{:S(2)}) collective-permute-start(bf16[3456,128]{1,0:T(8,128)(2,1)S(1)} %bitcast.5), channel_id=1, source_target_pairs={{0,1},{1,0},{2,3},{3,2},{4,5},{5,4},{6,7},{7,6},{8,9},{9,8},{10,11... | collective-permute-start | bytes 2654216 | tf_op jit(solution)/shard_map/ppermute | solution.py:274
  118.9 0.7 shard_map.66
  119.7 1.3 %shard_map.70.written = f32[2,3456,128]{2,1,0:T(8,128)} custom-call(s32[1]{0:T(128)} %bitcast.1.core_at, bf16[3456,128]{1,0:T(8,128)(2,1)S(1)} %bitcast.6), custom_call_target="tpu_custom_call" | custom-call | tf_op jit(solution)/shard_map/pallas_call | solution.py:312
  121.0 1.3 %shard_map.71 = f32[2,3456,128]{2,1,0:T(8,128)} custom-call(s32[1]{0:T(128)} %bitcast.1.core_at, bf16[3456,128]{1,0:T(8,128)(2,1)S(1)} %collective-permute-done.9.half, f32[2,3456,128]{2,1,0:T(8,128)} %shard_map.70.written), custom_call_target="tpu_custom_call", output_to_operand_aliasing={{}: (2, {})} | custom-call | tf_op jit(solution)/shard_map/pallas_call | solution.py:312
  (14 shorter events, 0.2 us)
Async XLA Ops:
  0.6 1.2 %copy-start = (bf16[4,8,128,128]{3,2,1,0:T(8,128)(2,1)S(1)}, bf16[4,8,128,128]{3,2,1,0:T(8,128)(2,1)}, u32[]{:S(2)}) copy-start(bf16[4,8,128,128]{3,2,1,0:T(8,128)(2,1)} %clip.5) | copy-start | bytes 3145732
  1.9 6.0 %copy-start.1 = (bf16[4,8,128,128]{3,2,1,0:T(8,128)(2,1)S(1)}, bf16[4,8,128,128]{3,2,1,0:T(8,128)(2,1)}, u32[]{:S(2)}) copy-start(bf16[4,8,128,128]{3,2,1,0:T(8,128)(2,1)} %clip.5) | copy-start | bytes 3145732
  1.9 6.0 %copy-start.3 = (bf16[3,3,3,128,256]{4,3,2,1,0:T(8,128)(2,1)S(1)}, bf16[3,3,3,128,256]{4,3,2,1,0:T(8,128)(2,1)}, u32[]{:S(2)}) copy-start(bf16[3,3,3,128,256]{4,3,2,1,0:T(8,128)(2,1)} %weight.3) | copy-start | bytes 5308420
  1.9 6.0 %collective-permute-start = (bf16[4,128,128]{2,1,0:T(8,128)(2,1)S(1)}, bf16[4,128,128]{2,1,0:T(8,128)(2,1)S(1)}, u32[]{:S(2)}, u32[]{:S(2)}) collective-permute-start(bf16[4,128,128]{2,1,0:T(8,128)(2,1)S(1)} %shard_map.60), channel_id=1, source_target_pairs={{0,1},{1,2},{2,3},{3,4},{4,5},{5,6},{6,7},{8,9},{9,10},{10,11},{11... | collective-permute-start | bytes 393224 | tf_op jit(solution)/shard_map/ppermute | solution.py:284
  6.5 6.4 %copy-start.4 = (bf16[2,4,64,128]{3,2,1,0:T(8,128)(2,1)S(1)}, bf16[2,4,64,128]{3,2,1,0:T(8,128)(2,1)}, u32[]{:S(2)}) copy-start(bf16[2,4,64,128]{3,2,1,0:T(8,128)(2,1)} %cot.3) | copy-start | bytes 393220
  6.5 35.6 %copy-start.2 = (bf16[3,3,3,256,128]{4,3,2,1,0:T(8,128)(2,1)S(1)}, bf16[3,3,3,256,128]{4,3,2,1,0:T(8,128)(2,1)}, u32[]{:S(2)}) copy-start(bf16[3,3,3,256,128]{4,3,2,1,0:T(8,128)(2,1)} %weight.5) | copy-start | bytes 5308420
  9.3 44.1 %collective-permute-start.7 = (bf16[2,9,128,128]{3,2,1,0:T(8,128)(2,1)S(1)}, bf16[2,9,128,128]{3,2,1,0:T(8,128)(2,1)S(1)}, u32[]{:S(2)}, u32[]{:S(2)}) collective-permute-start(bf16[2,9,128,128]{3,2,1,0:T(8,128)(2,1)S(1)} %get-tuple-element.27), channel_id=1, source_target_pairs={{128,8},{136,16},{144,24},{152,32},{160,40},{168,48},{176,56},{184... | collective-permute-start | bytes 1769480 | tf_op jit(solution)/shard_map/ppermute | solution.py:368
  12.9 9.6 %collective-permute-start.2 = (bf16[2,4,64,128]{3,2,1,0:T(8,128)(2,1)S(1)}, bf16[2,4,64,128]{3,2,1,0:T(8,128)(2,1)S(1)}, u32[]{:S(2)}, u32[]{:S(2)}) collective-permute-start(bf16[2,4,64,128]{3,2,1,0:T(8,128)(2,1)S(1)} %copy-done.4), channel_id=1, source_target_pairs={{8,0},{16,8},{24,16},{32,24},{40,32},{48,40},{56,48},{64,56},{72,6... | collective-permute-start | bytes 393224 | tf_op jit(solution)/shard_map/ppermute | solution.py:279
  14.2 15.6 %collective-permute-start.1 = (bf16[4,64,256]{2,1,0:T(8,128)(2,1)S(1)}, bf16[4,64,256]{2,1,0:T(8,128)(2,1)S(1)}, u32[]{:S(2)}, u32[]{:S(2)}) collective-permute-start(bf16[4,64,256]{2,1,0:T(8,128)(2,1)S(1)} %get-tuple-element.19), channel_id=1, source_target_pairs={{0,8},{8,16},{16,24},{24,32},{32,40},{40,48},{48,56},{56,64},{64,7... | collective-permute-start | bytes 393224 | tf_op jit(solution)/shard_map/ppermute | solution.py:279
  29.8 7.9 %collective-permute-start.3 = (bf16[2,3,64,256]{3,2,1,0:T(8,128)(2,1)S(1)}, bf16[2,3,64,256]{3,2,1,0:T(8,128)(2,1)S(1)}, u32[]{:S(2)}, u32[]{:S(2)}) collective-permute-start(bf16[2,3,64,256]{3,2,1,0:T(8,128)(2,1)S(1)} %get-tuple-element.22), channel_id=1, source_target_pairs={{0,1},{1,2},{2,3},{3,4},{4,5},{5,6},{6,7},{8,9},{9,10},{10,11},{11... | collective-permute-start | bytes 589832 | tf_op jit(solution)/shard_map/ppermute | solution.py:284
  35.1 7.0 %collective-permute-start.4 = (bf16[2,3,64,256]{3,2,1,0:T(8,128)(2,1)S(1)}, bf16[2,3,64,256]{3,2,1,0:T(8,128)(2,1)S(1)}, u32[]{:S(2)}, u32[]{:S(2)}) collective-permute-start(bf16[2,3,64,256]{3,2,1,0:T(8,128)(2,1)S(1)} %get-tuple-element.23), channel_id=1, source_target_pairs={{1,0},{2,1},{3,2},{4,3},{5,4},{6,5},{7,6},{9,8},{10,9},{11,10},{12... | collective-permute-start | bytes 589832 | tf_op jit(solution)/shard_map/ppermute | solution.py:284
  45.3 9.2 %collective-permute-start.6 = (bf16[2,6,64,128]{3,2,1,0:T(8,128)(2,1)S(1)}, bf16[2,6,64,128]{3,2,1,0:T(8,128)(2,1)S(1)}, u32[]{:S(2)}, u32[]{:S(2)}) collective-permute-start(bf16[2,6,64,128]{3,2,1,0:T(8,128)(2,1)S(1)} %get-tuple-element.26), channel_id=1, source_target_pairs={{8,0},{16,8},{24,16},{32,24},{40,32},{48,40},{56,48},{64,56},{72,6... | collective-permute-start | bytes 589832 | tf_op jit(solution)/shard_map/ppermute | solution.py:279
  46.6 9.3 %collective-permute-start.5 = (bf16[2,6,64,128]{3,2,1,0:T(8,128)(2,1)S(1)}, bf16[2,6,64,128]{3,2,1,0:T(8,128)(2,1)S(1)}, u32[]{:S(2)}, u32[]{:S(2)}) collective-permute-start(bf16[2,6,64,128]{3,2,1,0:T(8,128)(2,1)S(1)} %get-tuple-element.25.gone), channel_id=1, source_target_pairs={{0,8},{8,16},{16,24},{24,32},{32,40},{40,48},{48,56},{56,64},{64,7... | collective-permute-start | bytes 589832 | tf_op jit(solution)/shard_map/ppermute | solution.py:279
  58.4 2.5 %collective-permute-start.8 = (bf16[3456,128]{1,0:T(8,128)(2,1)S(1)}, bf16[3456,128]{1,0:T(8,128)(2,1)S(1)}, u32[]{:S(2)}, u32[]{:S(2)}) collective-permute-start(bf16[3456,128]{1,0:T(8,128)(2,1)S(1)} %get-tuple-element.33), channel_id=1, source_target_pairs={{0,1},{1,0},{2,3},{3,2},{4,5},{5,4},{6,7},{7,6},{8,9},{9,8},{10,11... | collective-permute-start | bytes 2654216 | tf_op jit(solution)/shard_map/ppermute | solution.py:274
  114.9 6.1 %collective-permute-start.9 = (bf16[3456,128]{1,0:T(8,128)(2,1)S(1)}, bf16[3456,128]{1,0:T(8,128)(2,1)S(1)}, u32[]{:S(2)}, u32[]{:S(2)}) collective-permute-start(bf16[3456,128]{1,0:T(8,128)(2,1)S(1)} %bitcast.5), channel_id=1, source_target_pairs={{0,1},{1,0},{2,3},{3,2},{4,5},{5,4},{6,7},{7,6},{8,9},{9,8},{10,11... | collective-permute-start | bytes 2654216 | tf_op jit(solution)/shard_map/ppermute | solution.py:274

commit v10 on v4

--- a/solution.py
+++ b/solution.py
@@ -17,7 +17,7 @@
     return jax.ShapeDtypeStruct(dims, dtype)
 
 
-def on_chip(body, outs, name, smem=0, scratch=(), grant=10):
+def on_chip(body, outs, smem=0, scratch=(), grant=8):
     def call(*args):
         specs = [pl.BlockSpec(memory_space=pltpu.SMEM)] * smem
         specs += [pl.BlockSpec(memory_space=pltpu.VMEM)] * (len(args) - smem)
@@ -27,7 +27,6 @@
             in_specs=specs,
             out_specs=[pl.BlockSpec(memory_space=pltpu.VMEM)] * len(outs),
             scratch_shapes=list(scratch),
-            name=name,
             compiler_params=pltpu.CompilerParams(vmem_limit_bytes=grant * MIB),
         )(*args)
 
@@ -36,10 +35,6 @@
 
 def dot(left, right):
     return jnp.dot(left, right, preferred_element_type=F32)
-
-
-def dot_tn(left, right):
-    return lax.dot_general(left, right, (((0,), (0,)), ((), ())), preferred_element_type=F32)
 
 
 def dot_nt(left, right):
@@ -67,10 +62,11 @@
     stage[0:8, :] = jnp.zeros((8, stage.shape[1]), F32)
 
 
-def edge_body(clip, cot, down):
+def edge_body(seg_at, core_at, clip, cot, down, up):
     down[0:4] = clip[:, 7]
     down[4, 0:64] = cot[0, 3]
     down[4, 64:128] = cot[1, 3]
+    up[...] = cot[:, 0]
 
 
 def windows_body(clip, taps, stage):
@@ -90,7 +86,7 @@
 
 
 def encode_body(
-    clip, taps, above, weight, cot, below, lat1, part, own0, tail, tops, rows6, stage
+    clip, taps, above, weight, cot, below, lat1, part, own0, tops, tail, rows6, stage
 ):
     start_stage(stage)
     for f in range(4):
@@ -111,7 +107,7 @@
     rows6[0, 0] = above[4, 0:64]
     rows6[1, 0] = above[4, 64:128]
     rows6[:, 1:5] = cot[...]
-    rows6[:, 5:6] = below[...]
+    rows6[:, 5] = below[...]
 
 
 def join_body(own0, part, lat1, lat, down, up):
@@ -282,15 +278,50 @@
     return lax.ppermute(array, ("y", "c"), pairs)
 
 
+def pair_body(seg_at, lat_grad, latent, pair):
+    pair[...] = jnp.where(seg_at[0] == 0, lat_grad[...], latent[...])
+
+
+def write_half(at, half, out, held, sent):
+    copies = []
+    for i in range(4):
+        rows = pl.ds(864 * i, 864)
+        held[rows, :] = half[rows, :].astype(F32) * (1.0 / math.sqrt(32 * 32 * 64))
+        copies.append(pltpu.make_async_copy(held.at[rows], out.at[at, rows], sent.at[i]))
+        copies[-1].start()
+    for one in copies:
+        one.wait()
+
+
+def half_body(core_at, half, out, held, sent):
+    write_half(core_at[0], half, out, held, sent)
+
+
+def other_body(core_at, half, written, out, held, sent):
+    write_half(1 - core_at[0], half, out, held, sent)
+
+
+def written(body, core_at, half, *given):
+    specs = [pl.BlockSpec(memory_space=pltpu.SMEM), pl.BlockSpec(memory_space=pltpu.VMEM)]
+    return pl.pallas_call(
+        body,
+        out_shape=shape((2, 3456, 128), F32),
+        in_specs=specs + [pl.BlockSpec(memory_space=pl.ANY)] * len(given),
+        out_specs=pl.BlockSpec(memory_space=pl.ANY),
+        scratch_shapes=[pltpu.VMEM((3456, 128), F32), pltpu.SemaphoreType.DMA((4,))],
+        input_output_aliases={2: 0} if given else {},
+        compiler_params=pltpu.CompilerParams(vmem_limit_bytes=8 * MIB),
+    )(core_at, half, *given)
+
+
 def summed(own, send):
     got = to_core(send)
-    (wide,) = on_chip(halves_body, [shape((16, 216, 128), BF16)], "halves")(own, got)
-    (thin,) = on_chip(second_body, [shape((4, 216, 128), BF16)], "second")(
-        exchanged(wide, ("x", "y"))
-    )
-    (wide,) = on_chip(third_body, [shape((16, 216, 128), BF16)], "third")(exchanged(thin, "z"))
+    (wide,) = on_chip(halves_body, [shape((16, 216, 128), BF16)])(own, got)
+    (thin,) = on_chip(second_body, [shape((4, 216, 128), BF16)])(exchanged(wide, ("x", "y")))
+    (wide,) = on_chip(third_body, [shape((16, 216, 128), BF16)])(exchanged(thin, "z"))
     half = exchanged(wide, ("x", "y")).reshape(3456, 128)
-    return half, to_core(half)
+    other = to_core(half)
+    return half, other
 
 
 def on_device(clip_frames, enc_weight, dec_weight, out_grad):
@@ -298,23 +329,24 @@
     core = lax.axis_index("c")
 
     stage = pltpu.VMEM((136, 128), F32)
-    (down,) = on_chip(edge_body, [shape((5, 128, 128), BF16)], "edge")(clip_frames, out_grad)
+    seg = seg.reshape(1)
+    core_at = core.reshape(1)
+    down, up = on_chip(
+        edge_body, [shape((5, 128, 128), BF16), shape((2, 64, 128), BF16)], 2
+    )(seg, core_at, clip_frames, out_grad)
     above = by_rows(down, 1)
-    below = by_rows(out_grad[:, 0:1], -1)
-    (taps,) = on_chip(windows_body, [shape((4, 8, 64, 384), BF16)], "windows", scratch=[stage])(
-        clip_frames
-    )
-    lat1, part, own0, tail, tops, cot = on_chip(
+    below = by_rows(up, -1)
+    (taps,) = on_chip(windows_body, [shape((4, 8, 64, 384), BF16)], scratch=[stage])(clip_frames)
+    lat1, part, own0, tops, tail, cot = on_chip(
         encode_body,
         [
             shape((4, 64, 256), BF16),
             shape((4, 64, 256), PART),
             shape((4, 64, 256), F32),
+            shape((4, 64, 384), BF16),
             shape((2, 9, 128, 128), BF16),
-            shape((4, 64, 384), BF16),
             shape((2, 6, 64, 128), BF16),
         ],
-        "encode",
         scratch=[stage],
         grant=16,
     )(clip_frames, taps, above, enc_weight, out_grad, below)
@@ -327,28 +359,24 @@
             shape((2, 2, 64, 256), BF16),
             shape((2, 2, 64, 256), BF16),
         ],
-        "join",
     )(own0, part, lat1)
     top = by_rows(down, 1)
     bottom = by_rows(up, -1)
-    tail, _ = lax.optimization_barrier((tail, down))
-    tail = lax.ppermute(tail, ("segment", "x", "z"), [(16 + t - 1, t) for t in range(1, 16)])
+    pairs = [(16 + t - 1, t) for t in range(1, 16)]
+    tail = lax.ppermute(tail, ("segment", "x", "z"), pairs)
     rows6 = (2, 6, 64, 128)
     own_part, behind, gone = on_chip(
         decode_body,
         [shape(rows6, F32), shape(rows6, PART), shape(rows6, PART)],
-        "decode",
         scratch=[pltpu.VMEM((2, 8, 64, 768), BF16)],
         grant=14,
     )(latent, top, bottom, dec_weight)
     from_behind = by_frames(gone, 1)
     from_later = by_frames(behind, -1)
-    seg = seg.reshape(1)
     tail, lat, _ = lax.optimization_barrier((tail, latent, gone))
     (turned,) = on_chip(
         turned_body,
         [shape((15, 384, 256), BF16)],
-        "turned",
         1,
         [
             pltpu.VMEM((2, 64, 384), BF16),
@@ -365,7 +393,6 @@
             shape((3456, 128), F32),
             shape((3456, 128), BF16),
         ],
-        "grads",
         2,
         [
             pltpu.VMEM((6912, 128), F32),
@@ -373,17 +400,18 @@
             pltpu.VMEM((4, 6, 64, 384), BF16),
         ],
         24,
-    )(seg, core.reshape(1), own_part, from_behind, gone, from_later, cot, later_cot, dec_weight, turned)
-    latent_pair = jnp.where(seg[0] == 0, lat_grad, latent)[None]
+    )(seg, core_at, own_part, from_behind, gone, from_later, cot, later_cot, dec_weight, turned)
+    (latent_pair,) = on_chip(pair_body, [shape((2, 4, 64, 256), BF16)], 1)(seg, lat_grad, latent)
     half, other = summed(own, send)
-    whole = jnp.where(core == 0, jnp.stack([half, other]), jnp.stack([other, half]))
-    weight_grads = whole.reshape(27, 32768).astype(F32) * (1.0 / math.sqrt(32 * 32 * 64))
-    return latent_pair, weight_grads[None]
+    grads = written(half_body, core_at, half)
+    grads = written(other_body, core_at, other, grads)
+    return latent_pair[None], grads.reshape(1, 27, 32768)
 
 
 def solution(mesh):
     fine = Mesh(mesh.devices.reshape(2, 4, 4, 4, 2), ("segment", "x", "z", "y", "c"))
     cells = P(("x", "z"), ("y", "c"), None, None)
+
     return jax.shard_map(
         on_device,
         mesh=fine,

time: 128 us -> 127 us (level)
  the two profiles are of different devices: /device:TPU:1 before, /device:TPU:33 now
where the time goes in v10:
time: 127 us
  blocking collectives  55.9 us (44%)
  starting transfers between devices  34.6 us (27%)
  waiting for transfers between devices  20.9 us (16%)
  Pallas kernels  12.2 us (10%)
  local copies, waits for them, and re-layouts  2.14 us (2%)
    all_to_all x3, blocking collectives, exchanged(): return lax.all_to_all(array, axes, 0, 0, tiled=True)  55.9 us
    ppermute x4, starting transfers between devices, by_frames(): return lax.ppermute(array, ('x', 'z'), pairs)  15.5 us
    ppermute x4, waiting for transfers between devices, by_frames(): return lax.ppermute(array, ('x', 'z'), pairs)  12.6 us
    ppermute x4, starting transfers between devices, by_rows(): return lax.ppermute(array, ('y', 'c'), pairs)  11.6 us
    pallas_call x11, Pallas kernels, call(): pl.pallas_call(body, out_shape=outs, in_specs=specs, out_specs=[pl.BlockS...  9.65 us
    ppermute x4, waiting for transfers between devices, by_rows(): return lax.ppermute(array, ('y', 'c'), pairs)  5.8 us
    ppermute x2, starting transfers between devices, to_core(): return lax.ppermute(array, 'c', [(0, 1), (1, 0)])  3.99 us
    ppermute x1, starting transfers between devices, on_device(): tail = lax.ppermute(tail, ('segment', 'x', 'z'), pairs)  3.58 us
  transfers between devices with their start and end apart: 11, of which 7 were waited for; matrix products, arithmetic and copies ran while one was open for 0% of the time, Pallas kernels for 5%

profile of v10, /device:TPU:33, one launch (start us, length us, event | category | flops | bytes accessed | tf_op | source)
XLA Modules:
  0.0 126.6 jit_solution(5184200712981244468)
XLA Ops:
  0.6 1.2 copy-done
  1.9 0.9 copy-done.4
  2.8 4.0 %collective-permute-start = (bf16[5,128,128]{2,1,0:T(8,128)(2,1)S(1)}, bf16[5,128,128]{2,1,0:T(8,128)(2,1)S(1)}, u32[]{:S(2)}, u32[]{:S(2)}) collective-permute-start(bf16[5,128,128]{2,1,0:T(8,128)(2,1)S(1)} %get-tuple-element.21), channel_id=1, source_target_pairs={{0,1},{1,2},{2,3},{3,4},{4,5},{5,6},{6,7},{8,9},{9,10},{10,11},{11... | collective-permute-start | bytes 491528 | tf_op jit(solution)/shard_map/ppermute | solution.py:278
  6.8 1.9 %collective-permute-start.1 = (bf16[2,64,128]{2,1,0:T(8,128)(2,1)S(1)}, bf16[2,64,128]{2,1,0:T(8,128)(2,1)S(1)}, u32[]{:S(2)}, u32[]{:S(2)}) collective-permute-start(bf16[2,64,128]{2,1,0:T(8,128)(2,1)S(1)} %get-tuple-element.22), channel_id=1, source_target_pairs={{1,0},{2,1},{3,2},{4,3},{5,4},{6,5},{7,6},{9,8},{10,9},{11,10},{12... | collective-permute-start | bytes 98312 | tf_op jit(solution)/shard_map/ppermute | solution.py:278
  8.8 0.5 shard_map.59.taps
  9.3 2.7 %collective-permute-done.1.below = bf16[2,64,128]{2,1,0:T(8,128)(2,1)S(1)} collective-permute-done((bf16[2,64,128]{2,1,0:T(8,128)(2,1)S(1)}, bf16[2,64,128]{2,1,0:T(8,128)(2,1)S(1)}, u32[]{:S(2)}, u32[]{:S(2)}) %collective-permute-start.1) | collective-permute-done | bytes 32800 | tf_op jit(solution)/shard_map/ppermute | solution.py:278
  12.1 1.4 %shard_map.61 = (bf16[4,64,256]{2,1,0:T(8,128)(2,1)S(1)}, bf16[4,64,256]{2,1,0:T(8,128)(2,1)S(1)}, f32[4,64,256]{2,1,0:T(8,128)S(1)}, bf16[4,64,384]{2,1,0:T(8,1...) custom-call(bf16[4,8,128,128]{3,2,1,0:T(8,128)(2,1)S(1)} %copy-done.1, ...), custom_call_target="tpu_custom_call" | custom-call | tf_op jit(solution)/shard_map/pallas_call | solution.py:24
  13.5 3.6 %collective-permute-start.8 = (bf16[2,9,128,128]{3,2,1,0:T(8,128)(2,1)S(1)}, bf16[2,9,128,128]{3,2,1,0:T(8,128)(2,1)S(1)}, u32[]{:S(2)}, u32[]{:S(2)}) collective-permute-start(bf16[2,9,128,128]{3,2,1,0:T(8,128)(2,1)S(1)} %get-tuple-element.33), channel_id=1, source_target_pairs={{128,8},{136,16},{144,24},{152,32},{160,40},{168,48},{176,56},{184... | collective-permute-start | bytes 1769480 | tf_op jit(solution)/shard_map/ppermute | solution.py:366
  17.1 6.1 %collective-permute-start.2 = (bf16[4,64,256]{2,1,0:T(8,128)(2,1)S(1)}, bf16[4,64,256]{2,1,0:T(8,128)(2,1)S(1)}, u32[]{:S(2)}, u32[]{:S(2)}) collective-permute-start(bf16[4,64,256]{2,1,0:T(8,128)(2,1)S(1)} %get-tuple-element.24), channel_id=1, source_target_pairs={{0,8},{8,16},{16,24},{24,32},{32,40},{40,48},{48,56},{56,64},{64,7... | collective-permute-start | bytes 393224 | tf_op jit(solution)/shard_map/ppermute | solution.py:273
  23.2 10.9 %collective-permute-done.2.part = bf16[4,64,256]{2,1,0:T(8,128)(2,1)S(1)} collective-permute-done((bf16[4,64,256]{2,1,0:T(8,128)(2,1)S(1)}, bf16[4,64,256]{2,1,0:T(8,128)(2,1)S(1)}, u32[]{:S(2)}, u32[]{:S(2)}) %collective-permute-start.2) | collective-permute-done | bytes 131104 | tf_op jit(solution)/shard_map/ppermute | solution.py:273
  34.2 3.7 %collective-permute-start.3 = (bf16[2,2,64,256]{3,2,1,0:T(8,128)(2,1)S(1)}, bf16[2,2,64,256]{3,2,1,0:T(8,128)(2,1)S(1)}, u32[]{:S(2)}, u32[]{:S(2)}) collective-permute-start(bf16[2,2,64,256]{3,2,1,0:T(8,128)(2,1)S(1)} %get-tuple-element.27), channel_id=1, source_target_pairs={{0,1},{1,2},{2,3},{3,4},{4,5},{5,6},{6,7},{8,9},{9,10},{10,11},{11... | collective-permute-start | bytes 393224 | tf_op jit(solution)/shard_map/ppermute | solution.py:278
  37.9 1.9 %collective-permute-start.4 = (bf16[2,2,64,256]{3,2,1,0:T(8,128)(2,1)S(1)}, bf16[2,2,64,256]{3,2,1,0:T(8,128)(2,1)S(1)}, u32[]{:S(2)}, u32[]{:S(2)}) collective-permute-start(bf16[2,2,64,256]{3,2,1,0:T(8,128)(2,1)S(1)} %get-tuple-element.28), channel_id=1, source_target_pairs={{1,0},{2,1},{3,2},{4,3},{5,4},{6,5},{7,6},{9,8},{10,9},{11,10},{12... | collective-permute-start | bytes 393224 | tf_op jit(solution)/shard_map/ppermute | solution.py:278
  39.8 1.3 %collective-permute-start.7 = (bf16[2,6,64,128]{3,2,1,0:T(8,128)(2,1)S(1)}, bf16[2,6,64,128]{3,2,1,0:T(8,128)(2,1)S(1)}, u32[]{:S(2)}, u32[]{:S(2)}) collective-permute-start(bf16[2,6,64,128]{3,2,1,0:T(8,128)(2,1)S(1)} %get-tuple-element.32.cot), channel_id=1, source_target_pairs={{8,0},{16,8},{24,16},{32,24},{40,32},{48,40},{56,48},{64,56},{72,6... | collective-permute-start | bytes 589832 | tf_op jit(solution)/shard_map/ppermute | solution.py:273
  41.1 3.0 %collective-permute-done.4.bottom = bf16[2,2,64,256]{3,2,1,0:T(8,128)(2,1)S(1)} collective-permute-done((bf16[2,2,64,256]{3,2,1,0:T(8,128)(2,1)S(1)}, bf16[2,2,64,256]{3,2,1,0:T(8,128)(2,1)S(1)}, u32[]{:S(2)}, u32[]{:S(2)}) %collective-permute-start.4) | collective-permute-done | bytes 131104 | tf_op jit(solution)/shard_map/ppermute | solution.py:278
  44.2 3.1 %shard_map.63 = (f32[2,6,64,128]{3,2,1,0:T(8,128)S(1)}, bf16[2,6,64,128]{3,2,1,0:T(8,128)(2,1)S(1)}, bf16[2,6,64,128]{3,2,1,0:T(8,128)(2,1)S(1)}) custom-call(bf16[2,4,64,256]{3,2,1,0:T(8,128)(2,1)S(1)} %get-tuple-element.36.lat.latent, bf16[2,2,64,256]{3,2,1,0:T(8,128)(2,1)S(1)} %collective-permute-done.3.top, ...), custom_call_target="tpu_custom_call" | custom-call | tf_op jit(solution)/shard_map/pallas_call | solution.py:24
  47.3 1.3 %collective-permute-start.6 = (bf16[2,6,64,128]{3,2,1,0:T(8,128)(2,1)S(1)}, bf16[2,6,64,128]{3,2,1,0:T(8,128)(2,1)S(1)}, u32[]{:S(2)}, u32[]{:S(2)}) collective-permute-start(bf16[2,6,64,128]{3,2,1,0:T(8,128)(2,1)S(1)} %get-tuple-element.31), channel_id=1, source_target_pairs={{8,0},{16,8},{24,16},{32,24},{40,32},{48,40},{56,48},{64,56},{72,6... | collective-permute-start | bytes 589832 | tf_op jit(solution)/shard_map/ppermute | solution.py:273
  48.6 6.8 %collective-permute-start.5 = (bf16[2,6,64,128]{3,2,1,0:T(8,128)(2,1)S(1)}, bf16[2,6,64,128]{3,2,1,0:T(8,128)(2,1)S(1)}, u32[]{:S(2)}, u32[]{:S(2)}) collective-permute-start(bf16[2,6,64,128]{3,2,1,0:T(8,128)(2,1)S(1)} %get-tuple-element.30.gone), channel_id=1, source_target_pairs={{0,8},{8,16},{16,24},{24,32},{32,40},{40,48},{48,56},{56,64},{64,7... | collective-permute-start | bytes 589832 | tf_op jit(solution)/shard_map/ppermute | solution.py:273
  55.4 0.9 shard_map.64.turned
  56.3 0.2 collective-permute-done.6.from_later
  56.5 1.5 %collective-permute-done.5.from_behind = bf16[2,6,64,128]{3,2,1,0:T(8,128)(2,1)S(1)} collective-permute-done((bf16[2,6,64,128]{3,2,1,0:T(8,128)(2,1)S(1)}, bf16[2,6,64,128]{3,2,1,0:T(8,128)(2,1)S(1)}, u32[]{:S(2)}, u32[]{:S(2)}) %collective-permute-start.5) | collective-permute-done | bytes 196640 | tf_op jit(solution)/shard_map/ppermute | solution.py:273
  58.0 2.5 %shard_map.65 = (bf16[2,4,64,256]{3,2,1,0:T(8,128)(2,1)S(1)}, f32[3456,128]{1,0:T(8,128)S(1)}, bf16[3456,128]{1,0:T(8,128)(2,1)S(1)}) custom-call(s32[1]{0:T(128)} %bitcast.seg_at, s32[1]{0:T(128)} %bitcast.1.core_at, f32[2,6,64,128]{3,2,1,0:T(8,128)S(1)} %get-tuple-element.29.own_part, bf16[2,6,64,128]{3,2,1,0:T(8,128)(2,1)S(1)} %collective-permute-done.5.from_behind, ...), custom_call_target="tpu_custom_call" | custom-call | tf_op jit(solution)/shard_map/pallas_call | solution.py:24
  60.5 0.1 collective-permute-start.9
  60.6 2.4 %collective-permute-done.9.got = bf16[3456,128]{1,0:T(8,128)(2,1)S(1)} collective-permute-done((bf16[3456,128]{1,0:T(8,128)(2,1)S(1)}, bf16[3456,128]{1,0:T(8,128)(2,1)S(1)}, u32[]{:S(2)}, u32[]{:S(2)}) %collective-permute-start.9) | collective-permute-done | bytes 884768 | tf_op jit(solution)/shard_map/ppermute | solution.py:268
  63.0 0.2 shard_map.67
  63.2 29.3 %all_to_all.15.got = bf16[16,216,128]{2,1,0:T(8,128)(2,1)S(1)} all-to-all(bf16[16,216,128]{2,1,0:T(8,128)(2,1)S(1)} %shard_map.67), channel_id=1, replica_groups=mesh['segment'=2,'x'=4,'z'=4,'y'=4,'c'=2] {'x','y'}, dimensions={0} | all-to-all | bytes 1769472 | tf_op jit(solution)/shard_map/all_to_all | solution.py:264
  92.5 0.1 shard_map.68
  92.6 10.4 %all_to_all.16.got = bf16[4,216,128]{2,1,0:T(8,128)(2,1)S(1)} all-to-all(bf16[4,216,128]{2,1,0:T(8,128)(2,1)S(1)} %shard_map.68), channel_id=1, replica_groups=mesh['segment'=2,'x'=4,'z'=4,'y'=4,'c'=2] {'z'}, dimensions={0} | all-to-all | bytes 442368 | tf_op jit(solution)/shard_map/all_to_all | solution.py:264
  103.1 16.2 %all_to_all.17 = bf16[16,216,128]{2,1,0:T(8,128)(2,1)S(1)} all-to-all(bf16[16,216,128]{2,1,0:T(8,128)(2,1)S(1)} %shard_map.69), channel_id=1, replica_groups=mesh['segment'=2,'x'=4,'z'=4,'y'=4,'c'=2] {'x','y'}, dimensions={0} | all-to-all | bytes 1769472 | tf_op jit(solution)/shard_map/all_to_all | solution.py:264
  119.3 3.9 %collective-permute-start.10 = (bf16[3456,128]{1,0:T(8,128)(2,1)S(1)}, bf16[3456,128]{1,0:T(8,128)(2,1)S(1)}, u32[]{:S(2)}, u32[]{:S(2)}) collective-permute-start(bf16[3456,128]{1,0:T(8,128)(2,1)S(1)} %bitcast.5), channel_id=1, source_target_pairs={{0,1},{1,0},{2,3},{3,2},{4,5},{5,4},{6,7},{7,6},{8,9},{9,8},{10,11... | collective-permute-start | bytes 2654216 | tf_op jit(solution)/shard_map/ppermute | solution.py:268
  123.2 0.7 shard_map.66
  124.0 1.3 shard_map.70.written
  125.3 1.3 shard_map.71
  (18 shorter events, 0.2 us)
Async XLA Ops:
  0.6 1.2 copy-start
  1.9 0.9 copy-start.4
  2.8 9.3 %copy-start.1 = (bf16[4,8,128,128]{3,2,1,0:T(8,128)(2,1)S(1)}, bf16[4,8,128,128]{3,2,1,0:T(8,128)(2,1)}, u32[]{:S(2)}) copy-start(bf16[4,8,128,128]{3,2,1,0:T(8,128)(2,1)} %clip.5) | copy-start | bytes 3145732
  2.8 9.3 %copy-start.3 = (bf16[3,3,3,128,256]{4,3,2,1,0:T(8,128)(2,1)S(1)}, bf16[3,3,3,128,256]{4,3,2,1,0:T(8,128)(2,1)}, u32[]{:S(2)}) copy-start(bf16[3,3,3,128,256]{4,3,2,1,0:T(8,128)(2,1)} %weight.3) | copy-start | bytes 5308420
  2.8 9.3 %copy-start.5 = (bf16[2,4,64,128]{3,2,1,0:T(8,128)(2,1)S(1)}, bf16[2,4,64,128]{3,2,1,0:T(8,128)(2,1)}, u32[]{:S(2)}) copy-start(bf16[2,4,64,128]{3,2,1,0:T(8,128)(2,1)} %cot.3) | copy-start | bytes 393220
  2.8 9.3 %collective-permute-start = (bf16[5,128,128]{2,1,0:T(8,128)(2,1)S(1)}, bf16[5,128,128]{2,1,0:T(8,128)(2,1)S(1)}, u32[]{:S(2)}, u32[]{:S(2)}) collective-permute-start(bf16[5,128,128]{2,1,0:T(8,128)(2,1)S(1)} %get-tuple-element.21), channel_id=1, source_target_pairs={{0,1},{1,2},{2,3},{3,4},{4,5},{5,6},{6,7},{8,9},{9,10},{10,11},{11... | collective-permute-start | bytes 491528 | tf_op jit(solution)/shard_map/ppermute | solution.py:278
  6.8 5.2 %collective-permute-start.1 = (bf16[2,64,128]{2,1,0:T(8,128)(2,1)S(1)}, bf16[2,64,128]{2,1,0:T(8,128)(2,1)S(1)}, u32[]{:S(2)}, u32[]{:S(2)}) collective-permute-start(bf16[2,64,128]{2,1,0:T(8,128)(2,1)S(1)} %get-tuple-element.22), channel_id=1, source_target_pairs={{1,0},{2,1},{3,2},{4,3},{5,4},{6,5},{7,6},{9,8},{10,9},{11,10},{12... | collective-permute-start | bytes 98312 | tf_op jit(solution)/shard_map/ppermute | solution.py:278
  9.3 34.9 %copy-start.2 = (bf16[3,3,3,256,128]{4,3,2,1,0:T(8,128)(2,1)S(1)}, bf16[3,3,3,256,128]{4,3,2,1,0:T(8,128)(2,1)}, u32[]{:S(2)}) copy-start(bf16[3,3,3,256,128]{4,3,2,1,0:T(8,128)(2,1)} %weight.5) | copy-start | bytes 5308420
  13.5 41.9 %collective-permute-start.8 = (bf16[2,9,128,128]{3,2,1,0:T(8,128)(2,1)S(1)}, bf16[2,9,128,128]{3,2,1,0:T(8,128)(2,1)S(1)}, u32[]{:S(2)}, u32[]{:S(2)}) collective-permute-start(bf16[2,9,128,128]{3,2,1,0:T(8,128)(2,1)S(1)} %get-tuple-element.33), channel_id=1, source_target_pairs={{128,8},{136,16},{144,24},{152,32},{160,40},{168,48},{176,56},{184... | collective-permute-start | bytes 1769480 | tf_op jit(solution)/shard_map/ppermute | solution.py:366
  17.1 17.1 %collective-permute-start.2 = (bf16[4,64,256]{2,1,0:T(8,128)(2,1)S(1)}, bf16[4,64,256]{2,1,0:T(8,128)(2,1)S(1)}, u32[]{:S(2)}, u32[]{:S(2)}) collective-permute-start(bf16[4,64,256]{2,1,0:T(8,128)(2,1)S(1)} %get-tuple-element.24), channel_id=1, source_target_pairs={{0,8},{8,16},{16,24},{24,32},{32,40},{40,48},{48,56},{56,64},{64,7... | collective-permute-start | bytes 393224 | tf_op jit(solution)/shard_map/ppermute | solution.py:273
  34.2 6.9 %collective-permute-start.3 = (bf16[2,2,64,256]{3,2,1,0:T(8,128)(2,1)S(1)}, bf16[2,2,64,256]{3,2,1,0:T(8,128)(2,1)S(1)}, u32[]{:S(2)}, u32[]{:S(2)}) collective-permute-start(bf16[2,2,64,256]{3,2,1,0:T(8,128)(2,1)S(1)} %get-tuple-element.27), channel_id=1, source_target_pairs={{0,1},{1,2},{2,3},{3,4},{4,5},{5,6},{6,7},{8,9},{9,10},{10,11},{11... | collective-permute-start | bytes 393224 | tf_op jit(solution)/shard_map/ppermute | solution.py:278
  37.9 6.3 %collective-permute-start.4 = (bf16[2,2,64,256]{3,2,1,0:T(8,128)(2,1)S(1)}, bf16[2,2,64,256]{3,2,1,0:T(8,128)(2,1)S(1)}, u32[]{:S(2)}, u32[]{:S(2)}) collective-permute-start(bf16[2,2,64,256]{3,2,1,0:T(8,128)(2,1)S(1)} %get-tuple-element.28), channel_id=1, source_target_pairs={{1,0},{2,1},{3,2},{4,3},{5,4},{6,5},{7,6},{9,8},{10,9},{11,10},{12... | collective-permute-start | bytes 393224 | tf_op jit(solution)/shard_map/ppermute | solution.py:278
  39.8 16.4 %collective-permute-start.7 = (bf16[2,6,64,128]{3,2,1,0:T(8,128)(2,1)S(1)}, bf16[2,6,64,128]{3,2,1,0:T(8,128)(2,1)S(1)}, u32[]{:S(2)}, u32[]{:S(2)}) collective-permute-start(bf16[2,6,64,128]{3,2,1,0:T(8,128)(2,1)S(1)} %get-tuple-element.32.cot), channel_id=1, source_target_pairs={{8,0},{16,8},{24,16},{32,24},{40,32},{48,40},{56,48},{64,56},{72,6... | collective-permute-start | bytes 589832 | tf_op jit(solution)/shard_map/ppermute | solution.py:273
  47.3 9.2 %collective-permute-start.6 = (bf16[2,6,64,128]{3,2,1,0:T(8,128)(2,1)S(1)}, bf16[2,6,64,128]{3,2,1,0:T(8,128)(2,1)S(1)}, u32[]{:S(2)}, u32[]{:S(2)}) collective-permute-start(bf16[2,6,64,128]{3,2,1,0:T(8,128)(2,1)S(1)} %get-tuple-element.31), channel_id=1, source_target_pairs={{8,0},{16,8},{24,16},{32,24},{40,32},{48,40},{56,48},{64,56},{72,6... | collective-permute-start | bytes 589832 | tf_op jit(solution)/shard_map/ppermute | solution.py:273
  48.6 9.3 %collective-permute-start.5 = (bf16[2,6,64,128]{3,2,1,0:T(8,128)(2,1)S(1)}, bf16[2,6,64,128]{3,2,1,0:T(8,128)(2,1)S(1)}, u32[]{:S(2)}, u32[]{:S(2)}) collective-permute-start(bf16[2,6,64,128]{3,2,1,0:T(8,128)(2,1)S(1)} %get-tuple-element.30.gone), channel_id=1, source_target_pairs={{0,8},{8,16},{16,24},{24,32},{32,40},{40,48},{48,56},{56,64},{64,7... | collective-permute-start | bytes 589832 | tf_op jit(solution)/shard_map/ppermute | solution.py:273
  60.5 2.5 %collective-permute-start.9 = (bf16[3456,128]{1,0:T(8,128)(2,1)S(1)}, bf16[3456,128]{1,0:T(8,128)(2,1)S(1)}, u32[]{:S(2)}, u32[]{:S(2)}) collective-permute-start(bf16[3456,128]{1,0:T(8,128)(2,1)S(1)} %get-tuple-element.39), channel_id=1, source_target_pairs={{0,1},{1,0},{2,3},{3,2},{4,5},{5,4},{6,7},{7,6},{8,9},{9,8},{10,11... | collective-permute-start | bytes 2654216 | tf_op jit(solution)/shard_map/ppermute | solution.py:268
  119.3 5.9 %collective-permute-start.10 = (bf16[3456,128]{1,0:T(8,128)(2,1)S(1)}, bf16[3456,128]{1,0:T(8,128)(2,1)S(1)}, u32[]{:S(2)}, u32[]{:S(2)}) collective-permute-start(bf16[3456,128]{1,0:T(8,128)(2,1)S(1)} %bitcast.5), channel_id=1, source_target_pairs={{0,1},{1,0},{2,3},{3,2},{4,5},{5,4},{6,7},{7,6},{8,9},{9,8},{10,11... | collective-permute-start | bytes 2654216 | tf_op jit(solution)/shard_map/ppermute | solution.py:268
